TPU v7x, 32 devices: a whole 2x2x4 slice. The times are simulated.
32 devices in a mesh: groups: 2 (over y), member: 4 (over x, core), fsdp: 4 (over z).
Axes of the slice: x: 2, y: 2, z: 4, core: 2. Of those that a mesh axis runs over, the one named last changes fastest.
Arguments:
- params: float32 [64, 1024, 1024], P(('groups', 'member'), 'fsdp'), parts along dimension 0, may hold values from -210 to 210
- gradients: bfloat16 [64, 1024, 1024], P(('groups', 'member'), 'fsdp'), parts along dimension 0, may hold values from -1.5258789e-05 to 1.5258789e-05
- first_moment: float32 [64, 1024, 1024], P(('groups', 'member'), 'fsdp'), parts along dimension 0, may hold values from -5.9604645e-07 to 5.9604645e-07
- second_moment: float32 [64, 1024, 1024], P(('groups', 'member'), 'fsdp'), parts along dimension 0, may hold values from 1.8189895e-15 to 3.6379787e-14
Outputs:
- new_params: float32 [64, 1024, 1024], P(('groups', 'member'), 'fsdp'), parts along dimension 0
- new_first: float32 [64, 1024, 1024], P(('groups', 'member'), 'fsdp'), parts along dimension 0
- new_second: float32 [64, 1024, 1024], P(('groups', 'member'), 'fsdp'), parts along dimension 0
- update: float32 [64, 1024, 1024], P(('groups', 'member'), 'fsdp'), parts along dimension 0
- stein_dir: float32 [64, 1024, 1024], P(('groups', 'member'), 'fsdp'), parts along dimension 0
- pair_distance: float32 [64, 32], P('groups'), parts along dimension 0
There are 2 independent parts, one for each index of `groups`. A program takes and returns all parts, laid end to end along the dimension named above; each array names one. Nothing has to cross between parts.
All inputs are finite; a program needn't handle non-finite values.
Results may differ from a plain program's by a relative error of at most 0.0025.
Values may be sent and summed in bfloat16 or wider, within the bound.
No kernel may reach another device: no remote copies, remote signals or barrier semaphores. Data moves between devices by JAX's collectives and lax.ppermute only.
A program may use at most 192 MiB of HBM per device.

v0:
```python
import math

import jax
import jax.numpy as jnp
from jax import lax
from jax.sharding import PartitionSpec as P

STEP_COUNT = 100


decay_first = 0.9
decay_second = 0.95
epsilon = 1e-08
learn_rate = 0.001
weight_decay = 0.05


def kernel_from(gram_total, members):
    self_dots = jnp.diagonal(gram_total)
    sqdist = self_dots[:, None] + self_dots[None, :] - 2.0 * gram_total
    kernel_scale = jnp.sum(sqdist) / (members * (members - 1)) / math.log(members)
    kernel = jnp.exp(-sqdist / kernel_scale)
    return (sqdist, kernel_scale, kernel.astype(jnp.bfloat16))


def adamw_step(params, stein_dir, first_moment, second_moment):
    descent = -stein_dir
    new_first = decay_first * first_moment + (1.0 - decay_first) * descent
    new_second = decay_second * second_moment + (1.0 - decay_second) * descent * descent
    first_hat = new_first / (1.0 - decay_first**STEP_COUNT)
    second_hat = new_second / (1.0 - decay_second**STEP_COUNT)
    update = first_hat / (jnp.sqrt(second_hat) + epsilon) + weight_decay * params
    new_params = params - learn_rate * update
    return (new_params, new_first, new_second, update)


def inner_products(left_flat, right_flat):
    return lax.dot_general(
        left_flat, right_flat, (((1,), (1,)), ((), ())), preferred_element_type=jnp.float32
    )


def shards(params, gradients, first_moment, second_moment):
    members_dev, rows_dev, feature_width = params.shape
    n_member = lax.axis_size("member")
    members = members_dev * n_member
    entries = rows_dev * lax.axis_size("fsdp") * feature_width
    working = params.astype(jnp.bfloat16)
    ascent = -gradients
    wide_work, wide_ascent = (
        lax.all_to_all(working, "member", split_axis=1, concat_axis=0, tiled=True),
        lax.all_to_all(ascent, "member", split_axis=1, concat_axis=0, tiled=True),
    )
    flat_work = wide_work.reshape(members, -1)
    gram_local = inner_products(flat_work, flat_work)
    flat_ascent = wide_ascent.reshape(members, -1)
    gram_total = lax.psum(gram_local, ("member", "fsdp"))
    sqdist, kernel_scale, kernel_half = kernel_from(gram_total, members)
    rowsum = jnp.sum(kernel_half.astype(jnp.float32), axis=1)
    repulse = 2.0 / kernel_scale
    mixed_ascent = jnp.dot(kernel_half, flat_ascent, preferred_element_type=jnp.float32)
    mixed_work = jnp.dot(kernel_half, flat_work, preferred_element_type=jnp.float32)
    stein_mix = (
        mixed_ascent + repulse * (rowsum[:, None] * flat_work.astype(jnp.float32) - mixed_work)
    ) / members
    stein_dir = lax.all_to_all(
        stein_mix.reshape(wide_work.shape), "member", split_axis=0, concat_axis=1, tiled=True
    )
    new_params, new_first, new_second, update = adamw_step(
        params, stein_dir, first_moment, second_moment
    )
    pair_distance = sqdist / entries
    return (new_params, new_first, new_second, update, stein_dir, pair_distance)


def solution(mesh):
    return jax.shard_map(
        shards,
        mesh=mesh,
        in_specs=(
            P(("groups", "member"), "fsdp", None),
            P(("groups", "member"), "fsdp", None),
            P(("groups", "member"), "fsdp", None),
            P(("groups", "member"), "fsdp", None),
        ),
        out_specs=(
            P(("groups", "member"), "fsdp", None),
            P(("groups", "member"), "fsdp", None),
            P(("groups", "member"), "fsdp", None),
            P(("groups", "member"), "fsdp", None),
            P(("groups", "member"), "fsdp", None),
            P("groups", None),
        ),
        check_vma=False,
    )
```

profile of v0, /device:TPU:0, one launch (start us, length us, event | category | flops | bytes accessed | tf_op | source)
XLA Modules:
  0.0 314.9 jit_solution(15781765817421736851)
XLA Ops:
  0.6 6.6 %copy_negate_fusion = bf16[8,256,1024]{2,0,1:T(8,128)(2,1)} fusion(bf16[8,256,1024]{2,1,0:T(8,128)(2,1)} %param.5), kind=kLoop, calls=%fused_computation.12 | loop fusion | flops 2097152 | bytes 8388608 | tf_op jit(solution)/shard_map/neg | solution.py:49
  7.3 4.8 %all-to-all-start.1 = ((bf16[8,256,1024]{2,0,1:T(8,128)(2,1)}), bf16[8,256,1024]{2,0,1:T(8,128)(2,1)}, u32[]{:S(2)}, u32[]{:S(2)}) async-start(bf16[8,256,1024]{2,0,1:T(8,128)(2,1)} %copy_negate_fusion), calls=%async_computation.1 | async-start | bytes 8388608 | tf_op jit(solution)/shard_map/all_to_all | solution.py:52
  12.1 9.8 %copy.24 = bf16[8,256,1024]{2,0,1:T(8,128)(2,1)} copy(f32[8,256,1024]{2,1,0:T(8,128)} %param.4) | data formatting | bytes 12582912 | tf_op args[0]
  22.0 39.0 %all-to-all-done.1 = bf16[8,256,1024]{2,0,1:T(8,128)(2,1)} async-done(((bf16[8,256,1024]{2,0,1:T(8,128)(2,1)}), bf16[8,256,1024]{2,0,1:T(8,128)(2,1)}, u32[]{:S(2)}, u32[]{:S(2)}) %all-to-all-start.1) | async-done | bytes 4194336 | tf_op jit(solution)/shard_map/all_to_all | solution.py:52
  61.0 5.0 %all-to-all-start = ((bf16[8,256,1024]{2,0,1:T(8,128)(2,1)}), bf16[8,256,1024]{2,0,1:T(8,128)(2,1)}, u32[]{:S(2)}, u32[]{:S(2)}) async-start(bf16[8,256,1024]{2,0,1:T(8,128)(2,1)} %copy.24), calls=%async_computation | async-start | bytes 8388608 | tf_op jit(solution)/shard_map/all_to_all | solution.py:51
  66.0 4.5 %copy.25 = bf16[8,4,64,1024]{3,2,0,1:T(8,128)(2,1)S(1)} copy(bf16[8,4,64,1024]{3,0,2,1:T(8,128)(2,1)} %bitcast.4) | data formatting | bytes 8388608 | tf_op jit(solution)/shard_map/all_to_all | solution.py:52
  70.5 4.3 %copy.19 = bf16[4,8,64,1024]{3,1,2,0:T(8,128)(2,1)} copy(bf16[4,8,64,1024]{3,2,1,0:T(8,128)(2,1)S(1)} %bitcast.34) | data formatting | bytes 8388608
  74.9 39.2 %all-to-all-done = bf16[8,256,1024]{2,0,1:T(8,128)(2,1)} async-done(((bf16[8,256,1024]{2,0,1:T(8,128)(2,1)}), bf16[8,256,1024]{2,0,1:T(8,128)(2,1)}, u32[]{:S(2)}, u32[]{:S(2)}) %all-to-all-start) | async-done | bytes 4194336 | tf_op jit(solution)/shard_map/all_to_all | solution.py:51
  114.1 4.7 %fusion.6 = f32[32,32]{1,0:T(8,128)S(1)} fusion(bf16[32,65536]{1,0:T(8,128)(2,1)} %bitcast.2), kind=kOutput, calls=%fused_computation.19 | convolution fusion | flops 134217728 | bytes 4198400 | tf_op jit(solution)/shard_map/dot_general | solution.py:38
  118.7 61.5 %psum.7 = f32[32,32]{1,0:T(8,128)S(1)} all-reduce(f32[32,32]{1,0:T(8,128)S(1)} %fusion.6), channel_id=1, replica_groups=mesh['groups'=2,'member'=4,'fsdp'=4] {'member','fsdp'}, use_global_device_ids=true, to_apply=%region_0.0 | all-reduce | flops 1024 | bytes 8192 | tf_op jit(solution)/shard_map/psum | solution.py:57
  180.2 0.7 gather_fusion
  180.9 1.3 fusion.3
  182.8 0.2 convert_reduce_fusion
  183.1 0.0 copy-start
  183.1 5.1 %fusion = f32[32,65536]{1,0:T(8,128)S(1)} fusion(bf16[32,32]{1,0:T(8,128)(2,1)S(1)} %get-tuple-element.11, bf16[32,65536]{1,0:T(8,128)(2,1)} %bitcast.2, f32[32]{0:T(128)S(1)} %get-tuple-element.10, f32[]{:T(128)S(6)} %div.43), kind=kOutput, calls=%fused_computation.2 | convolution fusion | flops 142606336 | bytes 12585092 | tf_op jit(solution)/shard_map/dot_general | solution.py:62
  188.2 0.0 copy-done
  188.2 1.2 fusion.1
  189.4 4.9 %copy.20 = f32[4,8,64,1024]{3,2,1,0:T(8,128)S(1)} copy(f32[4,8,64,1024]{3,1,2,0:T(8,128)S(1)} %bitcast.27) | data formatting | bytes 16777216
  194.3 0.0 slice-start
  194.3 96.1 %all_to_all.48 = f32[32,64,1024]{2,1,0:T(8,128)S(1)} all-to-all(f32[32,64,1024]{2,1,0:T(8,128)S(1)} %bitcast.28), channel_id=1, replica_groups=mesh['groups'=2,'member'=4,'fsdp'=4] {'member'}, dimensions={0} | all-to-all | bytes 16777216 | tf_op jit(solution)/shard_map/all_to_all | solution.py:66
  290.4 0.0 slice-start.1
  290.4 4.3 %copy.18 = f32[4,8,64,1024]{3,2,0,1:T(8,128)} copy(f32[4,8,64,1024]{3,2,1,0:T(8,128)S(1)} %bitcast.29) | data formatting | bytes 16777216 | tf_op jit(solution)/shard_map/all_to_all | solution.py:66
  294.7 0.0 slice-done
  294.7 0.0 slice-done.1
  294.7 20.2 %multiply_subtract_fusion = (f32[8,256,1024]{2,1,0:T(8,128)}, f32[8,256,1024]{2,1,0:T(8,128)}, f32[8,256,1024]{2,1,0:T(8,128)}, f32[8,256,1024]{2,1,0:T(8,128)}) fusion(f32[8,256,1024]{2,1,0:T(8,128)S(1)} %bitcast.31, f32[8,256,1024]{2,1,0:T(8,128)} %param.6, f32[8,256,1024]{2,1,0:T(8,128)} %param.7, f32[4,8,64,1024]{3,2,0,1:T(8,128)} %copy.18), kind=kLoop, calls=%fused_computation.8 | loop fusion | flops 33554432 | bytes 67108864 | tf_op jit(solution)/shard_map/sub | solution.py:33
  (2 shorter events, 0.0 us)
Async XLA Ops:
  7.3 53.7 %all-to-all-start.1 = ((bf16[8,256,1024]{2,0,1:T(8,128)(2,1)}), bf16[8,256,1024]{2,0,1:T(8,128)(2,1)}, u32[]{:S(2)}, u32[]{:S(2)}) async-start(bf16[8,256,1024]{2,0,1:T(8,128)(2,1)} %copy_negate_fusion), calls=%async_computation.1 | async-start | bytes 8388608 | tf_op jit(solution)/shard_map/all_to_all | solution.py:52
  61.0 53.1 %all-to-all-start = ((bf16[8,256,1024]{2,0,1:T(8,128)(2,1)}), bf16[8,256,1024]{2,0,1:T(8,128)(2,1)}, u32[]{:S(2)}, u32[]{:S(2)}) async-start(bf16[8,256,1024]{2,0,1:T(8,128)(2,1)} %copy.24), calls=%async_computation | async-start | bytes 8388608 | tf_op jit(solution)/shard_map/all_to_all | solution.py:51
  183.1 5.1 %copy-start = (bf16[4,8,64,1024]{3,1,2,0:T(8,128)(2,1)S(1)}, bf16[4,8,64,1024]{3,1,2,0:T(8,128)(2,1)}, u32[]{:S(2)}) copy-start(bf16[4,8,64,1024]{3,1,2,0:T(8,128)(2,1)} %copy.19) | copy-start | bytes 12582916
  194.3 100.4 %slice-start = ((s8[8388608]{0:T(1024)(128)(4,1)}), s8[4194304]{0:T(1024)(128)(4,1)S(1)}, s32[]{:S(2)}) async-start(s8[8388608]{0:T(1024)(128)(4,1)} %bitcast.30), calls=%async_computation.3 | async-start | bytes 8388608
  290.4 4.3 %slice-start.1 = ((s8[8388608]{0:T(1024)(128)(4,1)}), s8[4194304]{0:T(1024)(128)(4,1)S(1)}, s32[]{:S(2)}) async-start(s8[8388608]{0:T(1024)(128)(4,1)} %bitcast.30), calls=%async_computation.4 | async-start | bytes 8388608
where the time goes:
time: 315 us
  blocking collectives  158 us (50%)
  waiting for transfers between devices  78.2 us (25%)
  local copies, waits for them, and re-layouts  28.6 us (9%)
  other arithmetic  28.3 us (9%)
  matrix products  11 us (3%)
  starting transfers between devices  9.86 us (3%)
    all_to_all x1, blocking collectives, shards(): lax.all_to_all(stein_mix.reshape(wide_work.shape), 'member', split_axis=0...  96.1 us
    psum x1, blocking collectives, shards(): gram_total = lax.psum(gram_local, ('member', 'fsdp'))  61.5 us
    all_to_all x1, waiting for transfers between devices, shards(): lax.all_to_all(working, 'member', split_axis=1, concat_axis=0, tiled=True)  39.2 us
    all_to_all x1, waiting for transfers between devices, shards(): lax.all_to_all(ascent, 'member', split_axis=1, concat_axis=0, tiled=True)  39 us
    sub x1, other arithmetic, adamw_step(): new_params = params - learn_rate * update  20.2 us
    unnamed x9, local copies, waits for them, and re-layouts  19.1 us
    neg x1, other arithmetic, shards(): ascent = -gradients  6.63 us
  transfers between devices with their start and end apart: 2, of which 2 were waited for; matrix products, arithmetic and copies ran while one was open for 6% of the time, Pallas kernels for 0%

commit v1 on v0

v1 whole, which is shorter than its diff:
```python
import functools
import math

import jax
import jax.numpy as jnp
from jax import lax
from jax.experimental import pallas as pl
from jax.experimental.pallas import tpu as pltpu
from jax.sharding import PartitionSpec as P

STEP_COUNT = 100

decay_first = 0.9
decay_second = 0.95
epsilon = 1e-08
learn_rate = 0.001
weight_decay = 0.05

VMEM_BYTES = 48 << 20


def swap(x, axis, flip):
    return lax.ppermute(x, axis, [(i, i ^ flip) for i in range(lax.axis_size(axis))])


def tied(x, after):
    return lax.optimization_barrier((x, after))[0]


def sum_over(x, axis):
    stride, size = 1, lax.axis_size(axis)
    while stride < size:
        if size // stride >= 4:
            one, two, three = (swap(x, axis, flip * stride) for flip in (1, 2, 3))
            x = (x + one) + (two + three)
            stride *= 4
        else:
            x = x + swap(x, axis, stride)
            stride *= 2
    return x


def owner_matrix(me, n_member, members_dev, block_rows, dtype):
    members = n_member * members_dev
    stacked = lax.broadcasted_iota(jnp.int32, (members * block_rows, members), 0)
    column = lax.broadcasted_iota(jnp.int32, (members * block_rows, members), 1)
    slot = stacked // block_rows
    owner = ((slot // members_dev) ^ me) * members_dev + slot % members_dev
    return jnp.where(owner == column, 1.0, 0.0).astype(dtype)


def same_row(size, block_rows):
    left = lax.broadcasted_iota(jnp.int32, (size, size), 0) % block_rows
    right = lax.broadcasted_iota(jnp.int32, (size, size), 1) % block_rows
    return left == right


def stack_pieces(refs):
    parts = []
    for ref in refs:
        members_dev, block_rows, width = ref.shape
        parts.append(ref[...].astype(jnp.bfloat16).reshape(members_dev * block_rows, width))
    return jnp.concatenate(parts, axis=0)


def gram_kernel(me_ref, *refs):
    *piece_refs, gram_ref, acc_ref = refs
    step = pl.program_id(0)
    members_dev, block_rows, _ = piece_refs[0].shape
    n_member = len(piece_refs)

    @pl.when(step == 0)
    def _():
        acc_ref[...] = jnp.zeros_like(acc_ref)

    stacked = stack_pieces(piece_refs)
    acc_ref[...] += lax.dot_general(
        stacked, stacked, (((1,), (1,)), ((), ())), preferred_element_type=jnp.float32
    )

    @pl.when(step == pl.num_programs(0) - 1)
    def _():
        size = acc_ref.shape[0]
        owner = owner_matrix(me_ref[0], n_member, members_dev, block_rows, jnp.float32)
        kept = jnp.where(same_row(size, block_rows), acc_ref[...], 0.0)
        half = jnp.dot(kept, owner, precision=lax.Precision.HIGHEST)
        gram_ref[...] = lax.dot_general(
            owner, half, (((0,), (0,)), ((), ())), precision=lax.Precision.HIGHEST
        )


def local_gram(me, params, work_pieces):
    members_dev, rows_piece, width = work_pieces[0].shape
    n_member = len(work_pieces) + 1
    members = n_member * members_dev
    block_rows = min(16, rows_piece)
    steps = rows_piece // block_rows
    block = (members_dev, block_rows, width)
    size = members * block_rows
    return pl.pallas_call(
        gram_kernel,
        out_shape=jax.ShapeDtypeStruct((members, members), jnp.float32),
        grid_spec=pltpu.PrefetchScalarGridSpec(
            num_scalar_prefetch=1,
            grid=(steps,),
            in_specs=[pl.BlockSpec(block, lambda i, me_ref: (0, me_ref[0] * steps + i, 0))]
            + [pl.BlockSpec(block, lambda i, me_ref: (0, i, 0))] * (n_member - 1),
            out_specs=pl.BlockSpec((members, members), lambda i, me_ref: (0, 0)),
            scratch_shapes=[pltpu.VMEM((size, size), jnp.float32)],
        ),
        compiler_params=pltpu.CompilerParams(vmem_limit_bytes=VMEM_BYTES),
        cost_estimate=pl.CostEstimate(
            flops=2 * size * size * width * steps,
            bytes_accessed=(2 * n_member + 2) * members_dev * rows_piece * width,
            transcendentals=0,
        ),
        name="gram",
    )(me, params, *work_pieces)


def distances(gram):
    members = gram.shape[0]
    row = lax.broadcasted_iota(jnp.int32, gram.shape, 0)
    column = lax.broadcasted_iota(jnp.int32, gram.shape, 1)
    diagonal = jnp.where(row == column, gram, 0.0)
    down = jnp.sum(diagonal, axis=1, keepdims=True)
    across = jnp.sum(diagonal, axis=0, keepdims=True)
    return down + across - 2.0 * gram


def mix_kernel(n_member, me_ref, gram_ref, *refs):
    work_refs, grad_refs = refs[:n_member], refs[n_member : 2 * n_member]
    out_refs = refs[2 * n_member : 3 * n_member]
    big_ref, rowsum_ref, repulse_ref = refs[3 * n_member :]
    members_dev, block_rows, width = out_refs[0].shape
    members = n_member * members_dev
    size = members * block_rows

    @pl.when(pl.program_id(0) == 0)
    def _():
        sqdist = distances(gram_ref[...])
        total = jnp.sum(jnp.sum(sqdist, axis=1, keepdims=True), axis=0, keepdims=True)
        kernel_scale = total / (members * (members - 1)) / math.log(members)
        kernel_half = jnp.exp(-sqdist / kernel_scale).astype(jnp.bfloat16)
        owner = owner_matrix(me_ref[0], n_member, members_dev, block_rows, jnp.bfloat16)
        tall = jnp.dot(owner, kernel_half, preferred_element_type=jnp.float32)
        square = lax.dot_general(
            tall.astype(jnp.bfloat16), owner, (((1,), (1,)), ((), ())),
            preferred_element_type=jnp.float32,
        )
        big_ref[...] = jnp.where(same_row(size, block_rows), square, 0.0).astype(jnp.bfloat16)
        rowsum_ref[...] = jnp.sum(tall, axis=1, keepdims=True)
        repulse_ref[...] = 2.0 / kernel_scale

    big = big_ref[...]
    work = stack_pieces(work_refs)
    grads = stack_pieces(grad_refs)
    mixed_grads = jnp.dot(big, grads, preferred_element_type=jnp.float32)
    mixed_work = jnp.dot(big, work, preferred_element_type=jnp.float32)
    stein = (
        repulse_ref[...] * (rowsum_ref[...] * work.astype(jnp.float32) - mixed_work) - mixed_grads
    ) * (1.0 / members)
    stein = stein.astype(jnp.bfloat16)
    part = members_dev * block_rows
    for piece, out_ref in enumerate(out_refs):
        out_ref[...] = stein[piece * part : (piece + 1) * part].reshape(out_ref.shape)


def mix(me, gram, params, work_pieces, gradients, grad_pieces, first_row):
    members_dev, rows_piece, width = work_pieces[0].shape
    rows = grad_pieces[0].shape[1]
    n_member = len(work_pieces) + 1
    members = n_member * members_dev
    block_rows = min(16, rows)
    steps = rows // block_rows
    block = (members_dev, block_rows, width)
    size = members * block_rows
    skip = first_row // block_rows
    per_piece = rows_piece // block_rows
    whole = pl.BlockSpec(block, lambda i, me_ref: (0, me_ref[0] * per_piece + skip + i, 0))
    part = pl.BlockSpec(block, lambda i, me_ref: (0, i, 0))
    return pl.pallas_call(
        functools.partial(mix_kernel, n_member),
        out_shape=[jax.ShapeDtypeStruct((members_dev, rows, width), jnp.bfloat16)] * n_member,
        grid_spec=pltpu.PrefetchScalarGridSpec(
            num_scalar_prefetch=1,
            grid=(steps,),
            in_specs=[pl.BlockSpec((members, members), lambda i, me_ref: (0, 0)), whole]
            + [pl.BlockSpec(block, lambda i, me_ref: (0, skip + i, 0))] * (n_member - 1)
            + [whole]
            + [part] * (n_member - 1),
            out_specs=[part] * n_member,
            scratch_shapes=[
                pltpu.VMEM((size, size), jnp.bfloat16),
                pltpu.VMEM((size, 1), jnp.float32),
                pltpu.VMEM((1, 1), jnp.float32),
            ],
        ),
        compiler_params=pltpu.CompilerParams(vmem_limit_bytes=VMEM_BYTES),
        cost_estimate=pl.CostEstimate(
            flops=4 * size * size * width * steps,
            bytes_accessed=(6 * n_member + 2) * members_dev * rows * width,
            transcendentals=members * members,
        ),
        name="mix",
    )(me, gram, params, *work_pieces, gradients, *grad_pieces)


def adamw_kernel(row_ref, params_ref, first_ref, second_ref, stein_ref, *refs):
    del row_ref
    new_params_ref, new_first_ref, new_second_ref, update_ref, stein_dir_ref = refs[-5:]
    params = params_ref[...]
    stein_dir = stein_ref[...].astype(jnp.float32)
    new_first = decay_first * first_ref[...] - (1.0 - decay_first) * stein_dir
    new_second = decay_second * second_ref[...] + (1.0 - decay_second) * stein_dir * stein_dir
    first_hat = new_first * (1.0 / (1.0 - decay_first**STEP_COUNT))
    second_hat = new_second * (1.0 / (1.0 - decay_second**STEP_COUNT))
    update = first_hat / (jnp.sqrt(second_hat) + epsilon) + weight_decay * params
    new_params_ref[...] = params - learn_rate * update
    new_first_ref[...] = new_first
    new_second_ref[...] = new_second
    update_ref[...] = update
    stein_dir_ref[...] = stein_dir


def adamw(row_block, params, first_moment, second_moment, stein, earlier):
    members_dev, rows, width = stein.shape
    block_members = math.gcd(members_dev, 2)
    block = (block_members, rows, width)
    home = pl.BlockSpec(block, lambda i, row_ref: (i, row_ref[0], 0))
    shape = jax.ShapeDtypeStruct(params.shape, jnp.float32)
    entries = members_dev * rows * width
    return pl.pallas_call(
        adamw_kernel,
        out_shape=[shape] * 5,
        grid_spec=pltpu.PrefetchScalarGridSpec(
            num_scalar_prefetch=1,
            grid=(members_dev // block_members,),
            in_specs=[home] * 3
            + [pl.BlockSpec(block, lambda i, row_ref: (i, 0, 0))]
            + [pl.BlockSpec(memory_space=pl.ANY)] * len(earlier),
            out_specs=[home] * 5,
        ),
        input_output_aliases={5 + idx: idx for idx in range(len(earlier))},
        compiler_params=pltpu.CompilerParams(vmem_limit_bytes=VMEM_BYTES),
        cost_estimate=pl.CostEstimate(
            flops=20 * entries, bytes_accessed=34 * entries, transcendentals=entries
        ),
        name="adamw",
    )(row_block, params, first_moment, second_moment, stein, *earlier)


def shards(params, gradients, first_moment, second_moment):
    members_dev, rows_dev, feature_width = params.shape
    n_member = lax.axis_size("member")
    entries = rows_dev * lax.axis_size("fsdp") * feature_width
    rows_piece = rows_dev // n_member
    n_part = 2 if rows_piece % 32 == 0 else 1
    rows_part = rows_piece // n_part
    me = lax.axis_index("member")
    me_table = me[None]
    order = [2, 3, 1] if n_member == 4 else list(range(1, n_member))

    def rows_of(array, flip, part, rows):
        start = (me ^ flip) * rows_piece + part * rows_part
        return lax.dynamic_slice(array, (0, start, 0), (members_dev, rows, feature_width))

    work, source = {}, params
    for flip in order:
        packed = rows_of(source, flip, 0, rows_piece).astype(jnp.bfloat16)
        work[flip] = swap(packed, "member", flip)
        source = tied(params, packed)
    flips = range(1, n_member)

    def send_gradients(part, after):
        arrived, source = {}, tied(gradients, after)
        for flip in order:
            packed = rows_of(source, flip, part, rows_part)
            arrived[flip] = swap(packed, "member", flip)
            source = tied(gradients, packed)
        return [arrived[flip] for flip in flips]

    grads = [send_gradients(0, packed)]
    work = [work[flip] for flip in flips]
    gram = sum_over(local_gram(me_table, params, work), "fsdp")
    grads += [send_gradients(part, gram) for part in range(1, n_part)]
    gram = sum_over(gram, "member")

    stein, back = [], []
    for part in range(n_part):
        pieces = mix(
            me_table, gram, params, work, gradients, grads[part], part * rows_part
        )
        stein.append(pieces[0])
        back.append({flip: swap(pieces[flip], "member", flip) for flip in order})

    outs = ()

    def finish(flip, part, piece, outs):
        row_block = ((me ^ flip) * n_part + part)[None]
        return adamw(row_block, params, first_moment, second_moment, piece, outs)

    near = [flip for flip in flips if flip == 1]
    far = [flip for flip in order if flip != 1]
    for part in range(n_part):
        outs = finish(0, part, stein[part], outs)
        for flip in near:
            outs = finish(flip, part, back[part][flip], outs)
    for part in range(n_part):
        for flip in far:
            outs = finish(flip, part, back[part][flip], outs)
    new_params, new_first, new_second, update, stein_dir = outs
    self_dots = jnp.diagonal(gram)
    sqdist = self_dots[:, None] + self_dots[None, :] - 2.0 * gram
    pair_distance = sqdist / entries
    return (new_params, new_first, new_second, update, stein_dir, pair_distance)


def solution(mesh):
    return jax.shard_map(
        shards,
        mesh=mesh,
        in_specs=(
            P(("groups", "member"), "fsdp", None),
            P(("groups", "member"), "fsdp", None),
            P(("groups", "member"), "fsdp", None),
            P(("groups", "member"), "fsdp", None),
        ),
        out_specs=(
            P(("groups", "member"), "fsdp", None),
            P(("groups", "member"), "fsdp", None),
            P(("groups", "member"), "fsdp", None),
            P(("groups", "member"), "fsdp", None),
            P(("groups", "member"), "fsdp", None),
            P("groups", None),
        ),
        check_vma=False,
    )
```

time: 315 us -> 180 us (0.57)
  blocking collectives: 158 us -> 0 us
  Pallas kernels: 0 us -> 58.3 us
  other arithmetic: 28.3 us -> 0.7 us
  matrix products: 11 us -> 0 us
  local copies, waits for them, and re-layouts: 28.6 us -> 20.2 us
  starting transfers between devices: 9.86 us -> 17 us
  waiting for transfers between devices: 78.2 us -> 81.6 us
    all_to_all x1 -> x0, blocking collectives: 96.1 us -> none  [shards(): lax.all_to_all(stein_mix.reshape(wide_work.shape), 'member', split_axis=0...]
    ppermute x0 -> x21, waiting for transfers between devices: none -> 81.6 us  [swap(): lax.ppermute(x, axis, [(i, i ^ flip) for i in range(lax.axis_size(axis))])]
    all_to_all x2 -> x0, waiting for transfers between devices: 78.2 us -> none  [the longest x1 39.2 us: shards(): lax.all_to_all(working, 'member', split_axis=1, concat_axis=0, tiled=True)]
    psum x1 -> x0, blocking collectives: 61.5 us -> none  [shards(): gram_total = lax.psum(gram_local, ('member', 'fsdp'))]
    pallas_call x0 -> x11, Pallas kernels: none -> 58.3 us  [the longest x8 41.1 us: adamw(): pl.pallas_call(adamw_kernel, out_shape=[shape] * 5, grid_spec=pltpu.Prefe...]
    sub x1 -> x0, other arithmetic: 20.2 us -> none  [adamw_step(): new_params = params - learn_rate * update]
    ppermute x0 -> x21, starting transfers between devices: none -> 17 us  [swap(): lax.ppermute(x, axis, [(i, i ^ flip) for i in range(lax.axis_size(axis))])]
    unnamed x9 -> x14, local copies, waits for them, and re-layouts: 19.1 us -> 3.44 us
  transfers between devices with their start and end apart: 2 -> 21, of which waited for: 2 -> 9; matrix products, arithmetic and copies ran while one was open for 6% -> 6% of each run, Pallas kernels for 0% -> 30%
where the time goes in v1:
time: 180 us; the launch traced here: 178 us
  waiting for transfers between devices  81.6 us (45%)
  Pallas kernels  58.3 us (32%)
  local copies, waits for them, and re-layouts  20.2 us (11%)
  starting transfers between devices  17 us (9%)
    ppermute x21, waiting for transfers between devices, swap(): lax.ppermute(x, axis, [(i, i ^ flip) for i in range(lax.axis_size(axis))])  81.6 us
    pallas_call x8, Pallas kernels, adamw(): pl.pallas_call(adamw_kernel, out_shape=[shape] * 5, grid_spec=pltpu.Prefe...  41.1 us
    ppermute x21, starting transfers between devices, swap(): lax.ppermute(x, axis, [(i, i ^ flip) for i in range(lax.axis_size(axis))])  17 us
    pallas_call x2, Pallas kernels, mix(): pl.pallas_call(functools.partial(mix_kernel, n_member), out_shape=[jax.Sh...  11.2 us
    dynamic_slice x6, local copies, waits for them, and re-layouts, rows_of(): lax.dynamic_slice(array, (0, start, 0), (members_dev, rows, feature_width))  8.85 us
    convert_element_type x3, local copies, waits for them, and re-layouts, shards(): packed = rows_of(source, flip, 0, rows_piece).astype(jnp.bfloat16)  7.2 us
    pallas_call x1, Pallas kernels, local_gram(): pl.pallas_call(gram_kernel, out_shape=jax.ShapeDtypeStruct((members, memb...  5.97 us
  transfers between devices with their start and end apart: 21, of which 9 were waited for; matrix products, arithmetic and copies ran while one was open for 6% of the time, Pallas kernels for 30%

profile of v1, /device:TPU:0, one launch (start us, length us, event | category | flops | bytes accessed | tf_op | source)
XLA Modules:
  0.0 178.5 jit_solution(12846758867289758146)
XLA Ops:
  0.7 2.7 %dynamic-slice_convert_fusion.2 = bf16[8,64,1024]{2,1,0:T(8,128)(2,1)} fusion(f32[8,256,1024]{2,1,0:T(8,128)} %params_ref.15, s32[]{:T(128)S(6)} %select_n.25), kind=kLoop, calls=%fused_computation.3 | loop fusion | bytes 2097156 | tf_op jit(solution)/shard_map/convert_element_type | solution.py:270
  3.4 2.7 %dynamic-slice_convert_fusion.1 = bf16[8,64,1024]{2,1,0:T(8,128)(2,1)} fusion(f32[8,256,1024]{2,1,0:T(8,128)} %params_ref.15, s32[]{:T(128)S(6)} %select_n.26), kind=kLoop, calls=%fused_computation.2 | loop fusion | bytes 2097156 | tf_op jit(solution)/shard_map/convert_element_type | solution.py:270
  6.1 1.7 dynamic-slice_convert_fusion
  7.9 0.5 collective-permute-start
  8.4 2.6 %collective-permute-start.2 = (bf16[8,64,1024]{2,1,0:T(8,128)(2,1)}, bf16[8,64,1024]{2,1,0:T(8,128)(2,1)S(1)}, u32[]{:S(2)}, u32[]{:S(2)}) collective-permute-start(bf16[8,64,1024]{2,1,0:T(8,128)(2,1)} %dynamic-slice_convert_fusion.1), channel_id=1, source_target_pairs={{0,12},{4,8},{8,4},{12,0},{1,13},{5,9},{9,5},{13,1},{2,14},{6,10},... | collective-permute-start | bytes 3145736 | tf_op jit(solution)/shard_map/ppermute | solution.py:23
  11.0 1.9 %constant_dynamic-slice_fusion.2 = bf16[8,32,1024]{2,1,0:T(8,128)(2,1)} fusion(bf16[8,256,1024]{2,1,0:T(8,128)(2,1)} %refs_4_.3, s32[]{:T(128)S(6)} %select_n.25), kind=kLoop, calls=%fused_computation.9 | loop fusion | bytes 1048580 | tf_op jit(solution)/shard_map/dynamic_slice | solution.py:266
  12.9 1.9 %constant_dynamic-slice_fusion.1 = bf16[8,32,1024]{2,1,0:T(8,128)(2,1)} fusion(bf16[8,256,1024]{2,1,0:T(8,128)(2,1)} %refs_4_.3, s32[]{:T(128)S(6)} %select_n.26), kind=kLoop, calls=%fused_computation.8 | loop fusion | bytes 1048580 | tf_op jit(solution)/shard_map/dynamic_slice | solution.py:266
  14.8 1.9 %constant_dynamic-slice_fusion = bf16[8,32,1024]{2,1,0:T(8,128)(2,1)} fusion(bf16[8,256,1024]{2,1,0:T(8,128)(2,1)} %refs_4_.3, s32[]{:T(128)S(6)} %select_n.27), kind=kLoop, calls=%fused_computation.7 | loop fusion | bytes 1048580 | tf_op jit(solution)/shard_map/dynamic_slice | solution.py:266
  16.7 18.1 %collective-permute-done.2.refs_3_ = bf16[8,64,1024]{2,1,0:T(8,128)(2,1)S(1)} collective-permute-done((bf16[8,64,1024]{2,1,0:T(8,128)(2,1)}, bf16[8,64,1024]{2,1,0:T(8,128)(2,1)S(1)}, u32[]{:S(2)}, u32[]{:S(2)}) %collective-permute-start.2) | collective-permute-done | bytes 1048608 | tf_op jit(solution)/shard_map/ppermute | solution.py:23
  34.8 22.6 %collective-permute-done.1.refs_2_ = bf16[8,64,1024]{2,1,0:T(8,128)(2,1)S(1)} collective-permute-done((bf16[8,64,1024]{2,1,0:T(8,128)(2,1)}, bf16[8,64,1024]{2,1,0:T(8,128)(2,1)S(1)}, u32[]{:S(2)}, u32[]{:S(2)}) %collective-permute-start.1) | collective-permute-done | bytes 1048608 | tf_op jit(solution)/shard_map/ppermute | solution.py:23
  57.4 6.0 %gram.1 = f32[32,32]{1,0:T(8,128)S(1)} custom-call(s32[1]{0:T(128)} %bitcast.1.me_ref, f32[8,256,1024]{2,1,0:T(8,128)} %params_ref.15, bf16[8,64,1024]{2,1,0:T(8,128)(2,1)S(1)} %collective-permute-done.refs_1_, bf16[8,64,1024]{2,1,0:T(8,128)(2,1)S(1)} %collective-permute-done.1.refs_2_, bf16[8,64,1024]{2,1,0:T(8,128)(2,1)S(1)} %collective-permute-done.2.refs_3_), custom_call_target="tpu_custom_call" | custom-call | flops 2147483648 | bytes 5242880 | tf_op jit(solution)/shard_map/gram/pallas_call | solution.py:100
  63.4 3.9 %collective-permute-start.5 = (f32[32,32]{1,0:T(8,128)S(1)}, f32[32,32]{1,0:T(8,128)S(1)}, u32[]{:S(2)}, u32[]{:S(2)}) collective-permute-start(f32[32,32]{1,0:T(8,128)S(1)} %gram.1), channel_id=1, source_target_pairs={{0,3},{1,2},{2,1},{3,0},{4,7},{5,6},{6,5},{7,4},{8,11},{9,10},{10,... | collective-permute-start | bytes 12296 | tf_op jit(solution)/shard_map/ppermute | solution.py:23
  67.3 0.6 collective-permute-start.3
  68.0 1.0 collective-permute-done.5
  69.0 1.9 %collective-permute-start.15 = (bf16[8,32,1024]{2,1,0:T(8,128)(2,1)}, bf16[8,32,1024]{2,1,0:T(8,128)(2,1)S(1)}, u32[]{:S(2)}, u32[]{:S(2)}) collective-permute-start(bf16[8,32,1024]{2,1,0:T(8,128)(2,1)} %constant_dynamic-slice_fusion.2), channel_id=1, source_target_pairs={{0,8},{4,12},{8,0},{12,4},{1,9},{5,13},{9,1},{13,5},{2,10},{6,14},... | collective-permute-start | bytes 1572872 | tf_op jit(solution)/shard_map/ppermute | solution.py:23
  70.8 1.1 collective-permute-done.4
  72.0 1.5 collective-permute-start.7
  73.5 1.1 constant_dynamic-slice_fusion.5
  74.6 1.1 constant_dynamic-slice_fusion.4
  75.7 0.4 collective-permute-start.6
  76.1 1.1 constant_dynamic-slice_fusion.3
  77.2 16.6 %collective-permute-done.8 = f32[32,32]{1,0:T(8,128)S(1)} collective-permute-done((f32[32,32]{1,0:T(8,128)S(1)}, f32[32,32]{1,0:T(8,128)S(1)}, u32[]{:S(2)}, u32[]{:S(2)}) %collective-permute-start.8) | collective-permute-done | bytes 4128 | tf_op jit(solution)/shard_map/ppermute | solution.py:23
  93.7 0.5 collective-permute-done.7
  94.3 1.3 collective-permute-start.10
  95.6 5.7 %mix.3 = (bf16[8,32,1024]{2,1,0:T(8,128)(2,1)S(1)}, bf16[8,32,1024]{2,1,0:T(8,128)(2,1)S(1)}, bf16[8,32,1024]{2,1,0:T(8,128)(2,1)}, bf16[8,32,1024]{2,1,0:T(8,128)(2,1)}) custom-call(s32[1]{0:T(128)} %bitcast.1.me_ref, f32[32,32]{1,0:T(8,128)S(1)} %add_add_fusion.gram_ref, f32[8,256,1024]{2,1,0:T(8,128)} %params_ref.15, ...), custom_call_target="tpu_custom_call" | custom-call | flops 2147483648 | bytes 6815744 | tf_op jit(solution)/shard_map/mix/pallas_call | solution.py:182
  101.3 0.8 copy-done.5
  102.1 0.4 collective-permute-start.20
  102.5 5.1 %collective-permute-done.11.refs_7_ = bf16[8,32,1024]{2,1,0:T(8,128)(2,1)S(1)} collective-permute-done((bf16[8,32,1024]{2,1,0:T(8,128)(2,1)S(1)}, bf16[8,32,1024]{2,1,0:T(8,128)(2,1)S(1)}, u32[]{:S(2)}, u32[]{:S(2)}) %collective-permute-start.11) | collective-permute-done | bytes 524320 | tf_op jit(solution)/shard_map/ppermute | solution.py:23
  107.6 11.6 %collective-permute-done.10.refs_6_ = bf16[8,32,1024]{2,1,0:T(8,128)(2,1)S(1)} collective-permute-done((bf16[8,32,1024]{2,1,0:T(8,128)(2,1)S(1)}, bf16[8,32,1024]{2,1,0:T(8,128)(2,1)S(1)}, u32[]{:S(2)}, u32[]{:S(2)}) %collective-permute-start.10) | collective-permute-done | bytes 524320 | tf_op jit(solution)/shard_map/ppermute | solution.py:23
  119.2 5.5 %mix.2 = (bf16[8,32,1024]{2,1,0:T(8,128)(2,1)S(1)}, bf16[8,32,1024]{2,1,0:T(8,128)(2,1)}, bf16[8,32,1024]{2,1,0:T(8,128)(2,1)}, bf16[8,32,1024]{2,1,0:T(8,128)(2,1)}) custom-call(s32[1]{0:T(128)} %bitcast.1.me_ref, f32[32,32]{1,0:T(8,128)S(1)} %add_add_fusion.gram_ref, f32[8,256,1024]{2,1,0:T(8,128)} %params_ref.15, ...), custom_call_target="tpu_custom_call" | custom-call | flops 2147483648 | bytes 6815744 | tf_op jit(solution)/shard_map/mix/pallas_call | solution.py:182
  124.7 0.8 copy-done.1
  125.5 0.4 collective-permute-start.18
  126.0 1.4 collective-permute-start.17
  127.4 0.3 collective-permute-start.13
  127.7 0.8 copy-done.3
  128.5 1.3 collective-permute-start.12
  129.9 0.7 gather_fusion
  130.6 1.0 copy-done.6
  131.6 5.1 %adamw.8 = (f32[8,256,1024]{2,1,0:T(8,128)}, f32[8,256,1024]{2,1,0:T(8,128)}, f32[8,256,1024]{2,1,0:T(8,128)}, f32[8,256,1024]{2,1,0:T(8,128)}, f32[8,256,1024]{2,1,0:T(8,128)}) custom-call(s32[1]{0:T(128)} %bitcast.8.row_ref, f32[8,256,1024]{2,1,0:T(8,128)} %params_ref.15, f32[8,256,1024]{2,1,0:T(8,128)} %first_ref.15, f32[8,256,1024]{2,1,0:T(8,128)} %second_ref.15, ...), custom_call_target="tpu_custom_call" | custom-call | flops 5242880 | bytes 8912896 | tf_op jit(solution)/shard_map/adamw/pallas_call | solution.py:233
  136.8 0.7 subtract_multiply_fusion
  137.4 5.2 %adamw.9 = (f32[8,256,1024]{2,1,0:T(8,128)}, f32[8,256,1024]{2,1,0:T(8,128)}, f32[8,256,1024]{2,1,0:T(8,128)}, f32[8,256,1024]{2,1,0:T(8,128)}, f32[8,256,1024]{2,1,0:T(8,128)}) custom-call(s32[1]{0:T(128)} %bitcast.7.row_ref, f32[8,256,1024]{2,1,0:T(8,128)} %params_ref.15, ...), custom_call_target="tpu_custom_call", output_to_operand_aliasing={{0}: (5, {}), {1}: (6, {}), {2}: (7, {}), {3}: (8, {}), {4}... | custom-call | flops 5242880 | bytes 8912896 | tf_op jit(solution)/shard_map/adamw/pallas_call | solution.py:233
  142.6 5.1 %adamw.10 = (f32[8,256,1024]{2,1,0:T(8,128)}, f32[8,256,1024]{2,1,0:T(8,128)}, f32[8,256,1024]{2,1,0:T(8,128)}, f32[8,256,1024]{2,1,0:T(8,128)}, f32[8,256,1024]{2,1,0:T(8,128)}) custom-call(s32[1]{0:T(128)} %bitcast.6.row_ref, f32[8,256,1024]{2,1,0:T(8,128)} %params_ref.15, ...), custom_call_target="tpu_custom_call", output_to_operand_aliasing={{0}: (5, {}), {1}: (6, {}), {2}: (7, {}), {3}: (8, {}), {4}... | custom-call | flops 5242880 | bytes 8912896 | tf_op jit(solution)/shard_map/adamw/pallas_call | solution.py:233
  147.7 5.1 %adamw.11 = (f32[8,256,1024]{2,1,0:T(8,128)}, f32[8,256,1024]{2,1,0:T(8,128)}, f32[8,256,1024]{2,1,0:T(8,128)}, f32[8,256,1024]{2,1,0:T(8,128)}, f32[8,256,1024]{2,1,0:T(8,128)}) custom-call(s32[1]{0:T(128)} %bitcast.5.row_ref, f32[8,256,1024]{2,1,0:T(8,128)} %params_ref.15, ...), custom_call_target="tpu_custom_call", output_to_operand_aliasing={{0}: (5, {}), {1}: (6, {}), {2}: (7, {}), {3}: (8, {}), {4}... | custom-call | flops 5242880 | bytes 8912896 | tf_op jit(solution)/shard_map/adamw/pallas_call | solution.py:233
  152.9 5.1 %adamw.12 = (f32[8,256,1024]{2,1,0:T(8,128)}, f32[8,256,1024]{2,1,0:T(8,128)}, f32[8,256,1024]{2,1,0:T(8,128)}, f32[8,256,1024]{2,1,0:T(8,128)}, f32[8,256,1024]{2,1,0:T(8,128)}) custom-call(s32[1]{0:T(128)} %bitcast.4.row_ref, f32[8,256,1024]{2,1,0:T(8,128)} %params_ref.15, ...), custom_call_target="tpu_custom_call", output_to_operand_aliasing={{0}: (5, {}), {1}: (6, {}), {2}: (7, {}), {3}: (8, {}), {4}... | custom-call | flops 5242880 | bytes 8912896 | tf_op jit(solution)/shard_map/adamw/pallas_call | solution.py:233
  158.0 5.1 %adamw.13 = (f32[8,256,1024]{2,1,0:T(8,128)}, f32[8,256,1024]{2,1,0:T(8,128)}, f32[8,256,1024]{2,1,0:T(8,128)}, f32[8,256,1024]{2,1,0:T(8,128)}, f32[8,256,1024]{2,1,0:T(8,128)}) custom-call(s32[1]{0:T(128)} %bitcast.3.row_ref, f32[8,256,1024]{2,1,0:T(8,128)} %params_ref.15, ...), custom_call_target="tpu_custom_call", output_to_operand_aliasing={{0}: (5, {}), {1}: (6, {}), {2}: (7, {}), {3}: (8, {}), {4}... | custom-call | flops 5242880 | bytes 8912896 | tf_op jit(solution)/shard_map/adamw/pallas_call | solution.py:233
  163.2 5.1 %adamw.14 = (f32[8,256,1024]{2,1,0:T(8,128)}, f32[8,256,1024]{2,1,0:T(8,128)}, f32[8,256,1024]{2,1,0:T(8,128)}, f32[8,256,1024]{2,1,0:T(8,128)}, f32[8,256,1024]{2,1,0:T(8,128)}) custom-call(s32[1]{0:T(128)} %bitcast.2.row_ref, f32[8,256,1024]{2,1,0:T(8,128)} %params_ref.15, ...), custom_call_target="tpu_custom_call", output_to_operand_aliasing={{0}: (5, {}), {1}: (6, {}), {2}: (7, {}), {3}: (8, {}), {4}... | custom-call | flops 5242880 | bytes 8912896 | tf_op jit(solution)/shard_map/adamw/pallas_call | solution.py:233
  168.3 5.1 %collective-permute-done.12.stein_ref = bf16[8,32,1024]{2,1,0:T(8,128)(2,1)S(1)} collective-permute-done((bf16[8,32,1024]{2,1,0:T(8,128)(2,1)}, bf16[8,32,1024]{2,1,0:T(8,128)(2,1)S(1)}, u32[]{:S(2)}, u32[]{:S(2)}) %collective-permute-start.12) | collective-permute-done | bytes 524320 | tf_op jit(solution)/shard_map/ppermute | solution.py:23
  173.4 5.1 %adamw.15 = (f32[8,256,1024]{2,1,0:T(8,128)}, f32[8,256,1024]{2,1,0:T(8,128)}, f32[8,256,1024]{2,1,0:T(8,128)}, f32[8,256,1024]{2,1,0:T(8,128)}, f32[8,256,1024]{2,1,0:T(8,128)}) custom-call(s32[1]{0:T(128)} %bitcast.row_ref, f32[8,256,1024]{2,1,0:T(8,128)} %params_ref.15, ...), custom_call_target="tpu_custom_call", output_to_operand_aliasing={{0}: (5, {}), {1}: (6, {}), {2}: (7, {}), {3}: (8, {}), {4}... | custom-call | flops 5242880 | bytes 8912896 | tf_op jit(solution)/shard_map/adamw/pallas_call | solution.py:233
  (33 shorter events, 0.4 us)
Async XLA Ops:
  7.9 8.9 %collective-permute-start = (bf16[8,64,1024]{2,1,0:T(8,128)(2,1)S(1)}, bf16[8,64,1024]{2,1,0:T(8,128)(2,1)S(1)}, u32[]{:S(2)}, u32[]{:S(2)}) collective-permute-start(bf16[8,64,1024]{2,1,0:T(8,128)(2,1)S(1)} %dynamic-slice_convert_fusion), channel_id=1, source_target_pairs={{0,4},{4,0},{8,12},{12,8},{1,5},{5,1},{9,13},{13,9},{2,6},{6,2},{1... | collective-permute-start | bytes 3145736 | tf_op jit(solution)/shard_map/ppermute | solution.py:23
  8.4 26.4 %collective-permute-start.2 = (bf16[8,64,1024]{2,1,0:T(8,128)(2,1)}, bf16[8,64,1024]{2,1,0:T(8,128)(2,1)S(1)}, u32[]{:S(2)}, u32[]{:S(2)}) collective-permute-start(bf16[8,64,1024]{2,1,0:T(8,128)(2,1)} %dynamic-slice_convert_fusion.1), channel_id=1, source_target_pairs={{0,12},{4,8},{8,4},{12,0},{1,13},{5,9},{9,5},{13,1},{2,14},{6,10},... | collective-permute-start | bytes 3145736 | tf_op jit(solution)/shard_map/ppermute | solution.py:23
  11.0 46.4 %collective-permute-start.1 = (bf16[8,64,1024]{2,1,0:T(8,128)(2,1)}, bf16[8,64,1024]{2,1,0:T(8,128)(2,1)S(1)}, u32[]{:S(2)}, u32[]{:S(2)}) collective-permute-start(bf16[8,64,1024]{2,1,0:T(8,128)(2,1)} %dynamic-slice_convert_fusion.2), channel_id=1, source_target_pairs={{0,8},{4,12},{8,0},{12,4},{1,9},{5,13},{9,1},{13,5},{2,10},{6,14},... | collective-permute-start | bytes 3145736 | tf_op jit(solution)/shard_map/ppermute | solution.py:23
  16.6 59.1 %collective-permute-start.14 = (bf16[8,32,1024]{2,1,0:T(8,128)(2,1)}, bf16[8,32,1024]{2,1,0:T(8,128)(2,1)}, u32[]{:S(2)}, u32[]{:S(2)}) collective-permute-start(bf16[8,32,1024]{2,1,0:T(8,128)(2,1)} %constant_dynamic-slice_fusion), channel_id=1, source_target_pairs={{0,4},{4,0},{8,12},{12,8},{1,5},{5,1},{9,13},{13,9},{2,6},{6,2},{1... | collective-permute-start | bytes 1572872 | tf_op jit(solution)/shard_map/ppermute | solution.py:23
  34.8 60.8 %copy-start = (bf16[8,64,1024]{2,1,0:T(8,128)(2,1)}, bf16[8,64,1024]{2,1,0:T(8,128)(2,1)S(1)}, u32[]{:S(2)}) copy-start(bf16[8,64,1024]{2,1,0:T(8,128)(2,1)S(1)} %collective-permute-done.2.refs_3_) | copy-start | bytes 3145732
  63.4 5.6 %collective-permute-start.5 = (f32[32,32]{1,0:T(8,128)S(1)}, f32[32,32]{1,0:T(8,128)S(1)}, u32[]{:S(2)}, u32[]{:S(2)}) collective-permute-start(f32[32,32]{1,0:T(8,128)S(1)} %gram.1), channel_id=1, source_target_pairs={{0,3},{1,2},{2,1},{3,0},{4,7},{5,6},{6,5},{7,4},{8,11},{9,10},{10,... | collective-permute-start | bytes 12296 | tf_op jit(solution)/shard_map/ppermute | solution.py:23
  67.2 4.6 %collective-permute-start.4 = (f32[32,32]{1,0:T(8,128)S(1)}, f32[32,32]{1,0:T(8,128)S(1)}, u32[]{:S(2)}, u32[]{:S(2)}) collective-permute-start(f32[32,32]{1,0:T(8,128)S(1)} %gram.1), channel_id=1, source_target_pairs={{0,2},{1,3},{2,0},{3,1},{4,6},{5,7},{6,4},{7,5},{8,10},{9,11},{10,... | collective-permute-start | bytes 12296 | tf_op jit(solution)/shard_map/ppermute | solution.py:23
  67.3 4.6 %collective-permute-start.3 = (f32[32,32]{1,0:T(8,128)S(1)}, f32[32,32]{1,0:T(8,128)S(1)}, u32[]{:S(2)}, u32[]{:S(2)}) collective-permute-start(f32[32,32]{1,0:T(8,128)S(1)} %gram.1), channel_id=1, source_target_pairs={{0,1},{1,0},{2,3},{3,2},{4,5},{5,4},{6,7},{7,6},{8,9},{9,8},{10,11... | collective-permute-start | bytes 12296 | tf_op jit(solution)/shard_map/ppermute | solution.py:23
  67.9 27.7 %collective-permute-start.16 = (bf16[8,32,1024]{2,1,0:T(8,128)(2,1)}, bf16[8,32,1024]{2,1,0:T(8,128)(2,1)}, u32[]{:S(2)}, u32[]{:S(2)}) collective-permute-start(bf16[8,32,1024]{2,1,0:T(8,128)(2,1)} %constant_dynamic-slice_fusion.1), channel_id=1, source_target_pairs={{0,12},{4,8},{8,4},{12,0},{1,13},{5,9},{9,5},{13,1},{2,14},{6,10},... | collective-permute-start | bytes 1572872 | tf_op jit(solution)/shard_map/ppermute | solution.py:23
  69.0 26.7 %collective-permute-start.15 = (bf16[8,32,1024]{2,1,0:T(8,128)(2,1)}, bf16[8,32,1024]{2,1,0:T(8,128)(2,1)S(1)}, u32[]{:S(2)}, u32[]{:S(2)}) collective-permute-start(bf16[8,32,1024]{2,1,0:T(8,128)(2,1)} %constant_dynamic-slice_fusion.2), channel_id=1, source_target_pairs={{0,8},{4,12},{8,0},{12,4},{1,9},{5,13},{9,1},{13,5},{2,10},{6,14},... | collective-permute-start | bytes 1572872 | tf_op jit(solution)/shard_map/ppermute | solution.py:23
  71.9 21.8 %collective-permute-start.8 = (f32[32,32]{1,0:T(8,128)S(1)}, f32[32,32]{1,0:T(8,128)S(1)}, u32[]{:S(2)}, u32[]{:S(2)}) collective-permute-start(f32[32,32]{1,0:T(8,128)S(1)} %add_add_fusion.1), channel_id=1, source_target_pairs={{0,12},{4,8},{8,4},{12,0},{1,13},{5,9},{9,5},{13,1},{2,14},{6,10},... | collective-permute-start | bytes 12296 | tf_op jit(solution)/shard_map/ppermute | solution.py:23
  72.0 22.3 %collective-permute-start.7 = (f32[32,32]{1,0:T(8,128)S(1)}, f32[32,32]{1,0:T(8,128)S(1)}, u32[]{:S(2)}, u32[]{:S(2)}) collective-permute-start(f32[32,32]{1,0:T(8,128)S(1)} %add_add_fusion.1), channel_id=1, source_target_pairs={{0,8},{4,12},{8,0},{12,4},{1,9},{5,13},{9,1},{13,5},{2,10},{6,14},... | collective-permute-start | bytes 12296 | tf_op jit(solution)/shard_map/ppermute | solution.py:23
  75.7 19.8 %collective-permute-start.6 = (f32[32,32]{1,0:T(8,128)S(1)}, f32[32,32]{1,0:T(8,128)S(1)}, u32[]{:S(2)}, u32[]{:S(2)}) collective-permute-start(f32[32,32]{1,0:T(8,128)S(1)} %add_add_fusion.1), channel_id=1, source_target_pairs={{0,4},{4,0},{8,12},{12,8},{1,5},{5,1},{9,13},{13,9},{2,6},{6,2},{1... | collective-permute-start | bytes 12296 | tf_op jit(solution)/shard_map/ppermute | solution.py:23
  93.7 13.9 %collective-permute-start.11 = (bf16[8,32,1024]{2,1,0:T(8,128)(2,1)S(1)}, bf16[8,32,1024]{2,1,0:T(8,128)(2,1)S(1)}, u32[]{:S(2)}, u32[]{:S(2)}) collective-permute-start(bf16[8,32,1024]{2,1,0:T(8,128)(2,1)S(1)} %constant_dynamic-slice_fusion.4), channel_id=1, source_target_pairs={{0,12},{4,8},{8,4},{12,0},{1,13},{5,9},{9,5},{13,1},{2,14},{6,10},... | collective-permute-start | bytes 1572872 | tf_op jit(solution)/shard_map/ppermute | solution.py:23
  94.3 24.9 %collective-permute-start.10 = (bf16[8,32,1024]{2,1,0:T(8,128)(2,1)S(1)}, bf16[8,32,1024]{2,1,0:T(8,128)(2,1)S(1)}, u32[]{:S(2)}, u32[]{:S(2)}) collective-permute-start(bf16[8,32,1024]{2,1,0:T(8,128)(2,1)S(1)} %constant_dynamic-slice_fusion.5), channel_id=1, source_target_pairs={{0,8},{4,12},{8,0},{12,4},{1,9},{5,13},{9,1},{13,5},{2,10},{6,14},... | collective-permute-start | bytes 1572872 | tf_op jit(solution)/shard_map/ppermute | solution.py:23
  95.5 7.0 %collective-permute-start.9 = (bf16[8,32,1024]{2,1,0:T(8,128)(2,1)S(1)}, bf16[8,32,1024]{2,1,0:T(8,128)(2,1)S(1)}, u32[]{:S(2)}, u32[]{:S(2)}) collective-permute-start(bf16[8,32,1024]{2,1,0:T(8,128)(2,1)S(1)} %constant_dynamic-slice_fusion.3), channel_id=1, source_target_pairs={{0,4},{4,0},{8,12},{12,8},{1,5},{5,1},{9,13},{13,9},{2,6},{6,2},{1... | collective-permute-start | bytes 1572872 | tf_op jit(solution)/shard_map/ppermute | solution.py:23
  101.3 0.8 copy-start.5
  102.1 25.6 %collective-permute-start.20 = (bf16[8,32,1024]{2,1,0:T(8,128)(2,1)S(1)}, bf16[8,32,1024]{2,1,0:T(8,128)(2,1)S(1)}, u32[]{:S(2)}, u32[]{:S(2)}) collective-permute-start(bf16[8,32,1024]{2,1,0:T(8,128)(2,1)S(1)} %get-tuple-element.76), channel_id=1, source_target_pairs={{0,4},{4,0},{8,12},{12,8},{1,5},{5,1},{9,13},{13,9},{2,6},{6,2},{1... | collective-permute-start | bytes 1572872 | tf_op jit(solution)/shard_map/ppermute | solution.py:23
  124.7 0.8 copy-start.1
  125.5 22.2 %collective-permute-start.19 = (bf16[8,32,1024]{2,1,0:T(8,128)(2,1)}, bf16[8,32,1024]{2,1,0:T(8,128)(2,1)S(1)}, u32[]{:S(2)}, u32[]{:S(2)}) collective-permute-start(bf16[8,32,1024]{2,1,0:T(8,128)(2,1)} %get-tuple-element.74), channel_id=1, source_target_pairs={{0,4},{4,0},{8,12},{12,8},{1,5},{5,1},{9,13},{13,9},{2,6},{6,2},{1... | collective-permute-start | bytes 1572872 | tf_op jit(solution)/shard_map/ppermute | solution.py:23
  125.5 27.3 %collective-permute-start.18 = (bf16[8,32,1024]{2,1,0:T(8,128)(2,1)}, bf16[8,32,1024]{2,1,0:T(8,128)(2,1)S(1)}, u32[]{:S(2)}, u32[]{:S(2)}) collective-permute-start(bf16[8,32,1024]{2,1,0:T(8,128)(2,1)} %get-tuple-element.73), channel_id=1, source_target_pairs={{0,8},{4,12},{8,0},{12,4},{1,9},{5,13},{9,1},{13,5},{2,10},{6,14},... | collective-permute-start | bytes 1572872 | tf_op jit(solution)/shard_map/ppermute | solution.py:23
  126.0 32.1 %collective-permute-start.17 = (bf16[8,32,1024]{2,1,0:T(8,128)(2,1)}, bf16[8,32,1024]{2,1,0:T(8,128)(2,1)S(1)}, u32[]{:S(2)}, u32[]{:S(2)}) collective-permute-start(bf16[8,32,1024]{2,1,0:T(8,128)(2,1)} %get-tuple-element.72), channel_id=1, source_target_pairs={{0,12},{4,8},{8,4},{12,0},{1,13},{5,9},{9,5},{13,1},{2,14},{6,10},... | collective-permute-start | bytes 1572872 | tf_op jit(solution)/shard_map/ppermute | solution.py:23
  127.4 35.8 %collective-permute-start.13 = (bf16[8,32,1024]{2,1,0:T(8,128)(2,1)}, bf16[8,32,1024]{2,1,0:T(8,128)(2,1)S(1)}, u32[]{:S(2)}, u32[]{:S(2)}) collective-permute-start(bf16[8,32,1024]{2,1,0:T(8,128)(2,1)} %get-tuple-element.68), channel_id=1, source_target_pairs={{0,8},{4,12},{8,0},{12,4},{1,9},{5,13},{9,1},{13,5},{2,10},{6,14},... | collective-permute-start | bytes 1572872 | tf_op jit(solution)/shard_map/ppermute | solution.py:23
  127.7 0.8 copy-start.3
  128.5 44.9 %collective-permute-start.12 = (bf16[8,32,1024]{2,1,0:T(8,128)(2,1)}, bf16[8,32,1024]{2,1,0:T(8,128)(2,1)S(1)}, u32[]{:S(2)}, u32[]{:S(2)}) collective-permute-start(bf16[8,32,1024]{2,1,0:T(8,128)(2,1)} %get-tuple-element.67), channel_id=1, source_target_pairs={{0,12},{4,8},{8,4},{12,0},{1,13},{5,9},{9,5},{13,1},{2,14},{6,10},... | collective-permute-start | bytes 1572872 | tf_op jit(solution)/shard_map/ppermute | solution.py:23
  130.6 1.0 copy-start.6
  131.6 5.8 %copy-start.4 = (bf16[8,32,1024]{2,1,0:T(8,128)(2,1)S(1)}, bf16[8,32,1024]{2,1,0:T(8,128)(2,1)}, u32[]{:S(2)}) copy-start(bf16[8,32,1024]{2,1,0:T(8,128)(2,1)} %copy-done.3) | copy-start | bytes 1572868
  137.4 5.2 %copy-start.2 = (bf16[8,32,1024]{2,1,0:T(8,128)(2,1)S(1)}, bf16[8,32,1024]{2,1,0:T(8,128)(2,1)}, u32[]{:S(2)}) copy-start(bf16[8,32,1024]{2,1,0:T(8,128)(2,1)} %copy-done.1) | copy-start | bytes 1572868

commit v2 on v1

--- a/solution.py
+++ b/solution.py
@@ -17,6 +17,8 @@
 weight_decay = 0.05
 
 VMEM_BYTES = 48 << 20
+LIGHT = pl.CostEstimate(flops=1024, bytes_accessed=1024, transcendentals=0)
+STEP = pl.CostEstimate(flops=1024, bytes_accessed=1 << 20, transcendentals=0)
 
 
 def swap(x, axis, flip):
@@ -27,8 +29,8 @@
     return lax.optimization_barrier((x, after))[0]
 
 
-def sum_over(x, axis):
-    stride, size = 1, lax.axis_size(axis)
+def sum_over(x, axis, stride=1):
+    size = lax.axis_size(axis)
     while stride < size:
         if size // stride >= 4:
             one, two, three = (swap(x, axis, flip * stride) for flip in (1, 2, 3))
@@ -61,6 +63,34 @@
         members_dev, block_rows, width = ref.shape
         parts.append(ref[...].astype(jnp.bfloat16).reshape(members_dev * block_rows, width))
     return jnp.concatenate(parts, axis=0)
+
+
+def pack_kernel(me_ref, *refs):
+    del me_ref
+    for in_ref, out_ref in zip(refs[: len(refs) // 2], refs[len(refs) // 2 :]):
+        out_ref[...] = in_ref[...].astype(out_ref.dtype)
+
+
+def pack_rows(me, params, flips, rows):
+    members_dev, _, width = params.shape
+    block_members = max(1, members_dev // 2)
+    block = (block_members, rows, width)
+    return pl.pallas_call(
+        pack_kernel,
+        out_shape=[jax.ShapeDtypeStruct((members_dev, rows, width), jnp.bfloat16)] * len(flips),
+        grid_spec=pltpu.PrefetchScalarGridSpec(
+            num_scalar_prefetch=1,
+            grid=(members_dev // block_members,),
+            in_specs=[
+                pl.BlockSpec(block, lambda i, me_ref, flip=flip: (i, me_ref[0] ^ flip, 0))
+                for flip in flips
+            ],
+            out_specs=[pl.BlockSpec(block, lambda i, me_ref: (i, 0, 0))] * len(flips),
+        ),
+        compiler_params=pltpu.CompilerParams(vmem_limit_bytes=VMEM_BYTES),
+        cost_estimate=LIGHT,
+        name="pack",
+    )(me, *[params] * len(flips))
 
 
 def gram_kernel(me_ref, *refs):
@@ -109,11 +139,7 @@
             scratch_shapes=[pltpu.VMEM((size, size), jnp.float32)],
         ),
         compiler_params=pltpu.CompilerParams(vmem_limit_bytes=VMEM_BYTES),
-        cost_estimate=pl.CostEstimate(
-            flops=2 * size * size * width * steps,
-            bytes_accessed=(2 * n_member + 2) * members_dev * rows_piece * width,
-            transcendentals=0,
-        ),
+        cost_estimate=LIGHT,
         name="gram",
     )(me, params, *work_pieces)
 
@@ -168,7 +194,7 @@
 
 def mix(me, gram, params, work_pieces, gradients, grad_pieces, first_row):
     members_dev, rows_piece, width = work_pieces[0].shape
-    rows = grad_pieces[0].shape[1]
+    rows = min(piece.shape[1] for piece in grad_pieces)
     n_member = len(work_pieces) + 1
     members = n_member * members_dev
     block_rows = min(16, rows)
@@ -179,6 +205,7 @@
     per_piece = rows_piece // block_rows
     whole = pl.BlockSpec(block, lambda i, me_ref: (0, me_ref[0] * per_piece + skip + i, 0))
     part = pl.BlockSpec(block, lambda i, me_ref: (0, i, 0))
+    arrived = pl.BlockSpec(block, lambda i, me_ref: (0, skip + i, 0))
     return pl.pallas_call(
         functools.partial(mix_kernel, n_member),
         out_shape=[jax.ShapeDtypeStruct((members_dev, rows, width), jnp.bfloat16)] * n_member,
@@ -186,9 +213,9 @@
             num_scalar_prefetch=1,
             grid=(steps,),
             in_specs=[pl.BlockSpec((members, members), lambda i, me_ref: (0, 0)), whole]
-            + [pl.BlockSpec(block, lambda i, me_ref: (0, skip + i, 0))] * (n_member - 1)
+            + [arrived] * (n_member - 1)
             + [whole]
-            + [part] * (n_member - 1),
+            + [part if piece.shape[1] == rows else arrived for piece in grad_pieces],
             out_specs=[part] * n_member,
             scratch_shapes=[
                 pltpu.VMEM((size, size), jnp.bfloat16),
@@ -197,11 +224,7 @@
             ],
         ),
         compiler_params=pltpu.CompilerParams(vmem_limit_bytes=VMEM_BYTES),
-        cost_estimate=pl.CostEstimate(
-            flops=4 * size * size * width * steps,
-            bytes_accessed=(6 * n_member + 2) * members_dev * rows * width,
-            transcendentals=members * members,
-        ),
+        cost_estimate=LIGHT,
         name="mix",
     )(me, gram, params, *work_pieces, gradients, *grad_pieces)
 
@@ -225,11 +248,10 @@
 
 def adamw(row_block, params, first_moment, second_moment, stein, earlier):
     members_dev, rows, width = stein.shape
-    block_members = math.gcd(members_dev, 2)
+    block_members = math.gcd(members_dev, 4)
     block = (block_members, rows, width)
     home = pl.BlockSpec(block, lambda i, row_ref: (i, row_ref[0], 0))
     shape = jax.ShapeDtypeStruct(params.shape, jnp.float32)
-    entries = members_dev * rows * width
     return pl.pallas_call(
         adamw_kernel,
         out_shape=[shape] * 5,
@@ -243,9 +265,7 @@
         ),
         input_output_aliases={5 + idx: idx for idx in range(len(earlier))},
         compiler_params=pltpu.CompilerParams(vmem_limit_bytes=VMEM_BYTES),
-        cost_estimate=pl.CostEstimate(
-            flops=20 * entries, bytes_accessed=34 * entries, transcendentals=entries
-        ),
+        cost_estimate=STEP,
         name="adamw",
     )(row_block, params, first_moment, second_moment, stein, *earlier)
 
@@ -259,54 +279,70 @@
     rows_part = rows_piece // n_part
     me = lax.axis_index("member")
     me_table = me[None]
-    order = [2, 3, 1] if n_member == 4 else list(range(1, n_member))
+    flips = range(1, n_member)
+    near = [flip for flip in flips if flip == 1]
+    far = [2, 3] if n_member == 4 else list(flips)[1:]
 
     def rows_of(array, flip, part, rows):
         start = (me ^ flip) * rows_piece + part * rows_part
         return lax.dynamic_slice(array, (0, start, 0), (members_dev, rows, feature_width))
 
-    work, source = {}, params
-    for flip in order:
-        packed = rows_of(source, flip, 0, rows_piece).astype(jnp.bfloat16)
-        work[flip] = swap(packed, "member", flip)
-        source = tied(params, packed)
-    flips = range(1, n_member)
-
-    def send_gradients(part, after):
-        arrived, source = {}, tied(gradients, after)
-        for flip in order:
-            packed = rows_of(source, flip, part, rows_part)
-            arrived[flip] = swap(packed, "member", flip)
-            source = tied(gradients, packed)
-        return [arrived[flip] for flip in flips]
-
-    grads = [send_gradients(0, packed)]
-    work = [work[flip] for flip in flips]
-    gram = sum_over(local_gram(me_table, params, work), "fsdp")
-    grads += [send_gradients(part, gram) for part in range(1, n_part)]
-    gram = sum_over(gram, "member")
-
-    stein, back = [], []
-    for part in range(n_part):
-        pieces = mix(
-            me_table, gram, params, work, gradients, grads[part], part * rows_part
-        )
-        stein.append(pieces[0])
-        back.append({flip: swap(pieces[flip], "member", flip) for flip in order})
-
-    outs = ()
+    grads = [{} for _ in range(n_part)]
+    work = {}
+    last = None
 
     def finish(flip, part, piece, outs):
         row_block = ((me ^ flip) * n_part + part)[None]
         return adamw(row_block, params, first_moment, second_moment, piece, outs)
 
-    near = [flip for flip in flips if flip == 1]
-    far = [flip for flip in order if flip != 1]
+    def send(array, flip, part, rows, after):
+        source = array if after is None else tied(array, after)
+        packed = rows_of(source, flip, part, rows).astype(jnp.bfloat16)
+        return swap(packed, "member", flip), packed
+
+    packed = pack_rows(me_table, params, far, rows_piece)
+    for flip, piece in zip(far, packed):
+        work[flip] = swap(piece, "member", flip)
+    last = packed
+    for flip in far[:1]:
+        whole, last = send(gradients, flip, 0, rows_piece, last)
+        for part in range(n_part):
+            grads[part][flip] = whole
+    for flip in near:
+        last = (last, work[far[0]]) if far else last
+        work[flip], last = send(params, flip, 0, rows_piece, last)
+        whole, last = send(gradients, flip, 0, rows_piece, last)
+        for part in range(n_part):
+            grads[part][flip] = whole
+    gram = local_gram(me_table, params, [work[flip] for flip in flips])
+    gram = sum_over(tied(gram, last), "fsdp")
+    for flip in near:
+        gram = gram + swap(gram, "member", flip)
+    last = gram
     for part in range(n_part):
-        outs = finish(0, part, stein[part], outs)
-        for flip in near:
-            outs = finish(flip, part, back[part][flip], outs)
+        for flip in far[1:]:
+            grads[part][flip], last = send(gradients, flip, part, rows_part, last)
+    gram = sum_over(gram, "member", 2)
+    work = [work[flip] for flip in flips]
+    grads = [[piece[flip] for flip in flips] for piece in grads]
+
+    stein = [
+        mix(me_table, gram, params, work, gradients, grads[part], part * rows_part)
+        for part in range(n_part)
+    ]
+    back = [
+        {flip: swap(pieces[flip], "member", flip) for flip in far + near} for pieces in stein
+    ]
+    outs = ()
     for part in range(n_part):
+        outs = finish(0, part, stein[part][0], outs)
+        if part + 1 < n_part:
+            for flip in near:
+                outs = finish(flip, part, back[part][flip], outs)
+    for part in range(n_part):
+        if part + 1 == n_part:
+            for flip in near:
+                outs = finish(flip, part, back[part][flip], outs)
         for flip in far:
             outs = finish(flip, part, back[part][flip], outs)
     new_params, new_first, new_second, update, stein_dir = outs

time: 180 us -> 147 us (0.82)
  waiting for transfers between devices: 81.6 us -> 59.9 us
  local copies, waits for them, and re-layouts: 20.2 us -> 13.4 us
  Pallas kernels: 58.3 us -> 55.6 us
    ppermute x21 -> x18, waiting for transfers between devices: 81.6 us -> 59.9 us  [swap(): lax.ppermute(x, axis, [(i, i ^ flip) for i in range(lax.axis_size(axis))])]
    pallas_call x8, Pallas kernels: 41.1 us -> 35.1 us  [adamw(): pl.pallas_call(adamw_kernel, out_shape=[shape] * 5, grid_spec=pltpu.Prefe...]
    convert_element_type x3 -> x1, local copies, waits for them, and re-layouts: 7.2 us -> 1.74 us  [send(): packed = rows_of(source, flip, part, rows).astype(jnp.bfloat16)]
    pallas_call x0 -> x1, Pallas kernels: none -> 3.11 us  [pack_rows(): pl.pallas_call(pack_kernel, out_shape=[jax.ShapeDtypeStruct((members_dev,...]
    dynamic_slice x6 -> x4, local copies, waits for them, and re-layouts: 8.85 us -> 7.47 us  [rows_of(): lax.dynamic_slice(array, (0, start, 0), (members_dev, rows, feature_width))]
    ppermute x21 -> x18, starting transfers between devices: 17 us -> 16.4 us  [swap(): lax.ppermute(x, axis, [(i, i ^ flip) for i in range(lax.axis_size(axis))])]
  transfers between devices with their start and end apart: 21 -> 18, of which waited for: 9 -> 8; matrix products, arithmetic and copies ran while one was open for 6% -> 7% of each run, Pallas kernels for 30% -> 33%
where the time goes in v2:
time: 147 us
  waiting for transfers between devices  59.9 us (41%)
  Pallas kernels  55.6 us (38%)
  starting transfers between devices  16.4 us (11%)
  local copies, waits for them, and re-layouts  13.4 us (9%)
    ppermute x18, waiting for transfers between devices, swap(): lax.ppermute(x, axis, [(i, i ^ flip) for i in range(lax.axis_size(axis))])  59.9 us
    pallas_call x8, Pallas kernels, adamw(): pl.pallas_call(adamw_kernel, out_shape=[shape] * 5, grid_spec=pltpu.Prefe...  35.1 us
    ppermute x18, starting transfers between devices, swap(): lax.ppermute(x, axis, [(i, i ^ flip) for i in range(lax.axis_size(axis))])  16.4 us
    pallas_call x2, Pallas kernels, mix(): pl.pallas_call(functools.partial(mix_kernel, n_member), out_shape=[jax.Sh...  11.4 us
    dynamic_slice x4, local copies, waits for them, and re-layouts, rows_of(): lax.dynamic_slice(array, (0, start, 0), (members_dev, rows, feature_width))  7.47 us
    pallas_call x1, Pallas kernels, local_gram(): pl.pallas_call(gram_kernel, out_shape=jax.ShapeDtypeStruct((members, memb...  5.97 us
    unnamed x12, local copies, waits for them, and re-layouts  3.43 us
    pallas_call x1, Pallas kernels, pack_rows(): pl.pallas_call(pack_kernel, out_shape=[jax.ShapeDtypeStruct((members_dev,...  3.11 us
  transfers between devices with their start and end apart: 18, of which 8 were waited for; matrix products, arithmetic and copies ran while one was open for 7% of the time, Pallas kernels for 33%

profile of v2, /device:TPU:0, one launch (start us, length us, event | category | flops | bytes accessed | tf_op | source)
XLA Modules:
  0.0 146.7 jit_solution(12929943722072017681)
XLA Ops:
  0.6 3.1 %pack.1 = (bf16[8,64,1024]{2,1,0:T(8,128)(2,1)S(1)}, bf16[8,64,1024]{2,1,0:T(8,128)(2,1)}) custom-call(s32[1]{0:T(128)} %bitcast.1.me_ref, f32[8,256,1024]{2,1,0:T(8,128)} %params_ref.15, f32[8,256,1024]{2,1,0:T(8,128)} %params_ref.15), custom_call_target="tpu_custom_call" | custom-call | flops 1024 | bytes 1024 | tf_op jit(solution)/shard_map/pack/pallas_call | solution.py:78
  3.7 2.9 %collective-permute-start = (bf16[8,64,1024]{2,1,0:T(8,128)(2,1)S(1)}, bf16[8,64,1024]{2,1,0:T(8,128)(2,1)S(1)}, u32[]{:S(2)}, u32[]{:S(2)}) collective-permute-start(bf16[8,64,1024]{2,1,0:T(8,128)(2,1)S(1)} %get-tuple-element.62), channel_id=1, source_target_pairs={{0,8},{4,12},{8,0},{12,4},{1,9},{5,13},{9,1},{13,5},{2,10},{6,14},... | collective-permute-start | bytes 3145736 | tf_op jit(solution)/shard_map/ppermute | solution.py:25
  6.7 0.0 collective-permute-start.2
  6.7 2.3 %constant_dynamic-slice_fusion.3 = bf16[8,64,1024]{2,1,0:T(8,128)(2,1)} fusion(bf16[8,256,1024]{2,1,0:T(8,128)(2,1)} %refs_4_.3, s32[]{:T(128)S(6)} %select_n.17), kind=kLoop, calls=%fused_computation.7 | loop fusion | bytes 2097156 | tf_op jit(solution)/shard_map/dynamic_slice | solution.py:288
  9.0 21.7 %collective-permute-done.refs_2_ = bf16[8,64,1024]{2,1,0:T(8,128)(2,1)S(1)} collective-permute-done((bf16[8,64,1024]{2,1,0:T(8,128)(2,1)S(1)}, bf16[8,64,1024]{2,1,0:T(8,128)(2,1)S(1)}, u32[]{:S(2)}, u32[]{:S(2)}) %collective-permute-start) | collective-permute-done | bytes 1048608 | tf_op jit(solution)/shard_map/ppermute | solution.py:25
  30.7 1.7 %dynamic-slice_convert_fusion = bf16[8,64,1024]{2,1,0:T(8,128)(2,1)S(1)} fusion(f32[8,256,1024]{2,1,0:T(8,128)} %params_ref.15, s32[]{:T(128)S(6)} %select_n.18), kind=kLoop, calls=%fused_computation.1 | loop fusion | bytes 2097156 | tf_op jit(solution)/shard_map/convert_element_type | solution.py:300
  32.4 0.1 collective-permute-start.1
  32.5 2.1 %collective-permute-start.9 = (bf16[8,64,1024]{2,1,0:T(8,128)(2,1)}, bf16[8,64,1024]{2,1,0:T(8,128)(2,1)}, u32[]{:S(2)}, u32[]{:S(2)}) collective-permute-start(bf16[8,64,1024]{2,1,0:T(8,128)(2,1)} %constant_dynamic-slice_fusion.3), channel_id=1, source_target_pairs={{0,8},{4,12},{8,0},{12,4},{1,9},{5,13},{9,1},{13,5},{2,10},{6,14},... | collective-permute-start | bytes 3145736 | tf_op jit(solution)/shard_map/ppermute | solution.py:25
  34.6 2.3 %constant_dynamic-slice_fusion.2 = bf16[8,64,1024]{2,1,0:T(8,128)(2,1)} fusion(bf16[8,256,1024]{2,1,0:T(8,128)(2,1)} %refs_4_.3, s32[]{:T(128)S(6)} %select_n.18), kind=kLoop, calls=%fused_computation.6 | loop fusion | bytes 2097156 | tf_op jit(solution)/shard_map/dynamic_slice | solution.py:288
  36.9 0.2 collective-permute-start.8
  37.1 15.8 %collective-permute-done.2.refs_3_ = bf16[8,64,1024]{2,1,0:T(8,128)(2,1)S(1)} collective-permute-done((bf16[8,64,1024]{2,1,0:T(8,128)(2,1)}, bf16[8,64,1024]{2,1,0:T(8,128)(2,1)S(1)}, u32[]{:S(2)}, u32[]{:S(2)}) %collective-permute-start.2) | collective-permute-done | bytes 1048608 | tf_op jit(solution)/shard_map/ppermute | solution.py:25
  52.8 0.0 collective-permute-done.1.refs_1_
  52.8 6.0 %gram.1 = f32[32,32]{1,0:T(8,128)S(1)} custom-call(s32[1]{0:T(128)} %bitcast.1.me_ref, f32[8,256,1024]{2,1,0:T(8,128)} %params_ref.15, bf16[8,64,1024]{2,1,0:T(8,128)(2,1)S(1)} %collective-permute-done.1.refs_1_, bf16[8,64,1024]{2,1,0:T(8,128)(2,1)S(1)} %collective-permute-done.refs_2_, bf16[8,64,1024]{2,1,0:T(8,128)(2,1)S(1)} %collective-permute-done.2.refs_3_), custom_call_target="tpu_custom_call" | custom-call | flops 1024 | bytes 1024 | tf_op jit(solution)/shard_map/gram/pallas_call | solution.py:130
  58.8 3.7 %collective-permute-start.5 = (f32[32,32]{1,0:T(8,128)S(1)}, f32[32,32]{1,0:T(8,128)S(1)}, u32[]{:S(2)}, u32[]{:S(2)}) collective-permute-start(f32[32,32]{1,0:T(8,128)S(1)} %gram.1), channel_id=1, source_target_pairs={{0,3},{1,2},{2,1},{3,0},{4,7},{5,6},{6,5},{7,4},{8,11},{9,10},{10,... | collective-permute-start | bytes 12296 | tf_op jit(solution)/shard_map/ppermute | solution.py:25
  62.5 0.8 collective-permute-start.3
  63.3 1.1 collective-permute-done.5
  64.4 2.7 %collective-permute-done.4 = f32[32,32]{1,0:T(8,128)S(1)} collective-permute-done((f32[32,32]{1,0:T(8,128)S(1)}, f32[32,32]{1,0:T(8,128)S(1)}, u32[]{:S(2)}, u32[]{:S(2)}) %collective-permute-start.4) | collective-permute-done | bytes 4128 | tf_op jit(solution)/shard_map/ppermute | solution.py:25
  67.1 0.0 collective-permute-done.3
  67.1 0.1 collective-permute-start.6
  67.2 1.2 collective-permute-done.6
  68.4 1.9 %constant_dynamic-slice_fusion.1 = bf16[8,32,1024]{2,1,0:T(8,128)(2,1)} fusion(bf16[8,256,1024]{2,1,0:T(8,128)(2,1)} %refs_4_.3, s32[]{:T(128)S(6)} %select_n.19), kind=kLoop, calls=%fused_computation.5 | loop fusion | bytes 1048580 | tf_op jit(solution)/shard_map/dynamic_slice | solution.py:288
  70.2 0.4 collective-permute-start.14
  70.6 1.4 collective-permute-start.7
  72.0 1.1 constant_dynamic-slice_fusion
  73.1 0.3 collective-permute-start.10
  73.4 13.8 %collective-permute-done.7 = f32[32,32]{1,0:T(8,128)S(1)} collective-permute-done((f32[32,32]{1,0:T(8,128)S(1)}, f32[32,32]{1,0:T(8,128)S(1)}, u32[]{:S(2)}, u32[]{:S(2)}) %collective-permute-start.7) | collective-permute-done | bytes 4128 | tf_op jit(solution)/shard_map/ppermute | solution.py:25
  87.2 5.7 %mix.3 = (bf16[8,32,1024]{2,1,0:T(8,128)(2,1)S(1)}, bf16[8,32,1024]{2,1,0:T(8,128)(2,1)S(1)}, bf16[8,32,1024]{2,1,0:T(8,128)(2,1)}, bf16[8,32,1024]{2,1,0:T(8,128)(2,1)}) custom-call(s32[1]{0:T(128)} %bitcast.1.me_ref, f32[32,32]{1,0:T(8,128)S(1)} %add.69.gram_ref, f32[8,256,1024]{2,1,0:T(8,128)} %params_ref.15, ...), custom_call_target="tpu_custom_call" | custom-call | flops 1024 | bytes 1024 | tf_op jit(solution)/shard_map/mix/pallas_call | solution.py:209
  92.9 0.8 copy-done.4
  93.7 2.1 %collective-permute-start.16 = (bf16[8,32,1024]{2,1,0:T(8,128)(2,1)}, bf16[8,32,1024]{2,1,0:T(8,128)(2,1)}, u32[]{:S(2)}, u32[]{:S(2)}) collective-permute-start(bf16[8,32,1024]{2,1,0:T(8,128)(2,1)} %get-tuple-element.74), channel_id=1, source_target_pairs={{0,8},{4,12},{8,0},{12,4},{1,9},{5,13},{9,1},{13,5},{2,10},{6,14},... | collective-permute-start | bytes 1572872 | tf_op jit(solution)/shard_map/ppermute | solution.py:25
  95.8 0.1 collective-permute-start.15
  95.9 1.1 collective-permute-done.10.refs_7_
  97.0 5.7 %mix.2 = (bf16[8,32,1024]{2,1,0:T(8,128)(2,1)S(1)}, bf16[8,32,1024]{2,1,0:T(8,128)(2,1)}, bf16[8,32,1024]{2,1,0:T(8,128)(2,1)}, bf16[8,32,1024]{2,1,0:T(8,128)(2,1)}) custom-call(s32[1]{0:T(128)} %bitcast.1.me_ref, f32[32,32]{1,0:T(8,128)S(1)} %add.69.gram_ref, f32[8,256,1024]{2,1,0:T(8,128)} %params_ref.15, ...), custom_call_target="tpu_custom_call" | custom-call | flops 1024 | bytes 1024 | tf_op jit(solution)/shard_map/mix/pallas_call | solution.py:209
  102.7 0.8 copy-done
  103.5 0.6 collective-permute-start.13
  104.1 1.7 %collective-permute-start.12 = (bf16[8,32,1024]{2,1,0:T(8,128)(2,1)}, bf16[8,32,1024]{2,1,0:T(8,128)(2,1)S(1)}, u32[]{:S(2)}, u32[]{:S(2)}) collective-permute-start(bf16[8,32,1024]{2,1,0:T(8,128)(2,1)} %get-tuple-element.71), channel_id=1, source_target_pairs={{0,8},{4,12},{8,0},{12,4},{1,9},{5,13},{9,1},{13,5},{2,10},{6,14},... | collective-permute-start | bytes 1572872 | tf_op jit(solution)/shard_map/ppermute | solution.py:25
  105.8 0.8 copy-done.2
  106.6 0.7 gather_fusion
  107.3 0.7 subtract_multiply_fusion
  108.0 1.0 copy-done.5
  109.1 4.4 %adamw.8 = (f32[8,256,1024]{2,1,0:T(8,128)}, f32[8,256,1024]{2,1,0:T(8,128)}, f32[8,256,1024]{2,1,0:T(8,128)}, f32[8,256,1024]{2,1,0:T(8,128)}, f32[8,256,1024]{2,1,0:T(8,128)}) custom-call(s32[1]{0:T(128)} %bitcast.8.row_ref, f32[8,256,1024]{2,1,0:T(8,128)} %params_ref.15, f32[8,256,1024]{2,1,0:T(8,128)} %first_ref.15, f32[8,256,1024]{2,1,0:T(8,128)} %second_ref.15, ...), custom_call_target="tpu_custom_call" | custom-call | flops 1024 | bytes 1048576 | tf_op jit(solution)/shard_map/adamw/pallas_call | solution.py:255
  113.5 4.4 %adamw.9 = (f32[8,256,1024]{2,1,0:T(8,128)}, f32[8,256,1024]{2,1,0:T(8,128)}, f32[8,256,1024]{2,1,0:T(8,128)}, f32[8,256,1024]{2,1,0:T(8,128)}, f32[8,256,1024]{2,1,0:T(8,128)}) custom-call(s32[1]{0:T(128)} %bitcast.7.row_ref, f32[8,256,1024]{2,1,0:T(8,128)} %params_ref.15, ...), custom_call_target="tpu_custom_call", output_to_operand_aliasing={{0}: (5, {}), {1}: (6, {}), {2}: (7, {}), {3}: (8, {}), {4}... | custom-call | flops 1024 | bytes 1048576 | tf_op jit(solution)/shard_map/adamw/pallas_call | solution.py:255
  117.9 4.4 %adamw.10 = (f32[8,256,1024]{2,1,0:T(8,128)}, f32[8,256,1024]{2,1,0:T(8,128)}, f32[8,256,1024]{2,1,0:T(8,128)}, f32[8,256,1024]{2,1,0:T(8,128)}, f32[8,256,1024]{2,1,0:T(8,128)}) custom-call(s32[1]{0:T(128)} %bitcast.6.row_ref, f32[8,256,1024]{2,1,0:T(8,128)} %params_ref.15, ...), custom_call_target="tpu_custom_call", output_to_operand_aliasing={{0}: (5, {}), {1}: (6, {}), {2}: (7, {}), {3}: (8, {}), {4}... | custom-call | flops 1024 | bytes 1048576 | tf_op jit(solution)/shard_map/adamw/pallas_call | solution.py:255
  122.2 4.4 %adamw.11 = (f32[8,256,1024]{2,1,0:T(8,128)}, f32[8,256,1024]{2,1,0:T(8,128)}, f32[8,256,1024]{2,1,0:T(8,128)}, f32[8,256,1024]{2,1,0:T(8,128)}, f32[8,256,1024]{2,1,0:T(8,128)}) custom-call(s32[1]{0:T(128)} %bitcast.5.row_ref, f32[8,256,1024]{2,1,0:T(8,128)} %params_ref.15, ...), custom_call_target="tpu_custom_call", output_to_operand_aliasing={{0}: (5, {}), {1}: (6, {}), {2}: (7, {}), {3}: (8, {}), {4}... | custom-call | flops 1024 | bytes 1048576 | tf_op jit(solution)/shard_map/adamw/pallas_call | solution.py:255
  126.7 4.5 %adamw.12 = (f32[8,256,1024]{2,1,0:T(8,128)}, f32[8,256,1024]{2,1,0:T(8,128)}, f32[8,256,1024]{2,1,0:T(8,128)}, f32[8,256,1024]{2,1,0:T(8,128)}, f32[8,256,1024]{2,1,0:T(8,128)}) custom-call(s32[1]{0:T(128)} %bitcast.4.row_ref, f32[8,256,1024]{2,1,0:T(8,128)} %params_ref.15, ...), custom_call_target="tpu_custom_call", output_to_operand_aliasing={{0}: (5, {}), {1}: (6, {}), {2}: (7, {}), {3}: (8, {}), {4}... | custom-call | flops 1024 | bytes 1048576 | tf_op jit(solution)/shard_map/adamw/pallas_call | solution.py:255
  131.2 4.4 %adamw.13 = (f32[8,256,1024]{2,1,0:T(8,128)}, f32[8,256,1024]{2,1,0:T(8,128)}, f32[8,256,1024]{2,1,0:T(8,128)}, f32[8,256,1024]{2,1,0:T(8,128)}, f32[8,256,1024]{2,1,0:T(8,128)}) custom-call(s32[1]{0:T(128)} %bitcast.3.row_ref, f32[8,256,1024]{2,1,0:T(8,128)} %params_ref.15, ...), custom_call_target="tpu_custom_call", output_to_operand_aliasing={{0}: (5, {}), {1}: (6, {}), {2}: (7, {}), {3}: (8, {}), {4}... | custom-call | flops 1024 | bytes 1048576 | tf_op jit(solution)/shard_map/adamw/pallas_call | solution.py:255
  135.5 4.4 %adamw.14 = (f32[8,256,1024]{2,1,0:T(8,128)}, f32[8,256,1024]{2,1,0:T(8,128)}, f32[8,256,1024]{2,1,0:T(8,128)}, f32[8,256,1024]{2,1,0:T(8,128)}, f32[8,256,1024]{2,1,0:T(8,128)}) custom-call(s32[1]{0:T(128)} %bitcast.2.row_ref, f32[8,256,1024]{2,1,0:T(8,128)} %params_ref.15, ...), custom_call_target="tpu_custom_call", output_to_operand_aliasing={{0}: (5, {}), {1}: (6, {}), {2}: (7, {}), {3}: (8, {}), {4}... | custom-call | flops 1024 | bytes 1048576 | tf_op jit(solution)/shard_map/adamw/pallas_call | solution.py:255
  139.9 2.4 %collective-permute-done.11.stein_ref = bf16[8,32,1024]{2,1,0:T(8,128)(2,1)S(1)} collective-permute-done((bf16[8,32,1024]{2,1,0:T(8,128)(2,1)}, bf16[8,32,1024]{2,1,0:T(8,128)(2,1)S(1)}, u32[]{:S(2)}, u32[]{:S(2)}) %collective-permute-start.11) | collective-permute-done | bytes 524320 | tf_op jit(solution)/shard_map/ppermute | solution.py:25
  142.4 4.3 %adamw.15 = (f32[8,256,1024]{2,1,0:T(8,128)}, f32[8,256,1024]{2,1,0:T(8,128)}, f32[8,256,1024]{2,1,0:T(8,128)}, f32[8,256,1024]{2,1,0:T(8,128)}, f32[8,256,1024]{2,1,0:T(8,128)}) custom-call(s32[1]{0:T(128)} %bitcast.row_ref, f32[8,256,1024]{2,1,0:T(8,128)} %params_ref.15, ...), custom_call_target="tpu_custom_call", output_to_operand_aliasing={{0}: (5, {}), {1}: (6, {}), {2}: (7, {}), {3}: (8, {}), {4}... | custom-call | flops 1024 | bytes 1048576 | tf_op jit(solution)/shard_map/adamw/pallas_call | solution.py:255
  (23 shorter events, 0.1 us)
Async XLA Ops:
  3.7 26.9 %collective-permute-start = (bf16[8,64,1024]{2,1,0:T(8,128)(2,1)S(1)}, bf16[8,64,1024]{2,1,0:T(8,128)(2,1)S(1)}, u32[]{:S(2)}, u32[]{:S(2)}) collective-permute-start(bf16[8,64,1024]{2,1,0:T(8,128)(2,1)S(1)} %get-tuple-element.62), channel_id=1, source_target_pairs={{0,8},{4,12},{8,0},{12,4},{1,9},{5,13},{9,1},{13,5},{2,10},{6,14},... | collective-permute-start | bytes 3145736 | tf_op jit(solution)/shard_map/ppermute | solution.py:25
  6.7 46.1 %collective-permute-start.2 = (bf16[8,64,1024]{2,1,0:T(8,128)(2,1)}, bf16[8,64,1024]{2,1,0:T(8,128)(2,1)S(1)}, u32[]{:S(2)}, u32[]{:S(2)}) collective-permute-start(bf16[8,64,1024]{2,1,0:T(8,128)(2,1)} %get-tuple-element.63), channel_id=1, source_target_pairs={{0,12},{4,8},{8,4},{12,0},{1,13},{5,9},{9,5},{13,1},{2,14},{6,10},... | collective-permute-start | bytes 3145736 | tf_op jit(solution)/shard_map/ppermute | solution.py:25
  32.4 20.4 %collective-permute-start.1 = (bf16[8,64,1024]{2,1,0:T(8,128)(2,1)S(1)}, bf16[8,64,1024]{2,1,0:T(8,128)(2,1)S(1)}, u32[]{:S(2)}, u32[]{:S(2)}) collective-permute-start(bf16[8,64,1024]{2,1,0:T(8,128)(2,1)S(1)} %dynamic-slice_convert_fusion), channel_id=1, source_target_pairs={{0,4},{4,0},{8,12},{12,8},{1,5},{5,1},{9,13},{13,9},{2,6},{6,2},{1... | collective-permute-start | bytes 3145736 | tf_op jit(solution)/shard_map/ppermute | solution.py:25
  32.5 54.7 %collective-permute-start.9 = (bf16[8,64,1024]{2,1,0:T(8,128)(2,1)}, bf16[8,64,1024]{2,1,0:T(8,128)(2,1)}, u32[]{:S(2)}, u32[]{:S(2)}) collective-permute-start(bf16[8,64,1024]{2,1,0:T(8,128)(2,1)} %constant_dynamic-slice_fusion.3), channel_id=1, source_target_pairs={{0,8},{4,12},{8,0},{12,4},{1,9},{5,13},{9,1},{13,5},{2,10},{6,14},... | collective-permute-start | bytes 3145736 | tf_op jit(solution)/shard_map/ppermute | solution.py:25
  36.9 50.3 %collective-permute-start.8 = (bf16[8,64,1024]{2,1,0:T(8,128)(2,1)}, bf16[8,64,1024]{2,1,0:T(8,128)(2,1)}, u32[]{:S(2)}, u32[]{:S(2)}) collective-permute-start(bf16[8,64,1024]{2,1,0:T(8,128)(2,1)} %constant_dynamic-slice_fusion.2), channel_id=1, source_target_pairs={{0,4},{4,0},{8,12},{12,8},{1,5},{5,1},{9,13},{13,9},{2,6},{6,2},{1... | collective-permute-start | bytes 3145736 | tf_op jit(solution)/shard_map/ppermute | solution.py:25
  58.8 5.6 %collective-permute-start.5 = (f32[32,32]{1,0:T(8,128)S(1)}, f32[32,32]{1,0:T(8,128)S(1)}, u32[]{:S(2)}, u32[]{:S(2)}) collective-permute-start(f32[32,32]{1,0:T(8,128)S(1)} %gram.1), channel_id=1, source_target_pairs={{0,3},{1,2},{2,1},{3,0},{4,7},{5,6},{6,5},{7,4},{8,11},{9,10},{10,... | collective-permute-start | bytes 12296 | tf_op jit(solution)/shard_map/ppermute | solution.py:25
  62.5 4.6 %collective-permute-start.4 = (f32[32,32]{1,0:T(8,128)S(1)}, f32[32,32]{1,0:T(8,128)S(1)}, u32[]{:S(2)}, u32[]{:S(2)}) collective-permute-start(f32[32,32]{1,0:T(8,128)S(1)} %gram.1), channel_id=1, source_target_pairs={{0,2},{1,3},{2,0},{3,1},{4,6},{5,7},{6,4},{7,5},{8,10},{9,11},{10,... | collective-permute-start | bytes 12296 | tf_op jit(solution)/shard_map/ppermute | solution.py:25
  62.5 4.6 %collective-permute-start.3 = (f32[32,32]{1,0:T(8,128)S(1)}, f32[32,32]{1,0:T(8,128)S(1)}, u32[]{:S(2)}, u32[]{:S(2)}) collective-permute-start(f32[32,32]{1,0:T(8,128)S(1)} %gram.1), channel_id=1, source_target_pairs={{0,1},{1,0},{2,3},{3,2},{4,5},{5,4},{6,7},{7,6},{8,9},{9,8},{10,11... | collective-permute-start | bytes 12296 | tf_op jit(solution)/shard_map/ppermute | solution.py:25
  67.1 1.2 collective-permute-start.6
  70.2 17.0 %collective-permute-start.14 = (bf16[8,32,1024]{2,1,0:T(8,128)(2,1)}, bf16[8,32,1024]{2,1,0:T(8,128)(2,1)}, u32[]{:S(2)}, u32[]{:S(2)}) collective-permute-start(bf16[8,32,1024]{2,1,0:T(8,128)(2,1)} %constant_dynamic-slice_fusion.1), channel_id=1, source_target_pairs={{0,12},{4,8},{8,4},{12,0},{1,13},{5,9},{9,5},{13,1},{2,14},{6,10},... | collective-permute-start | bytes 1572872 | tf_op jit(solution)/shard_map/ppermute | solution.py:25
  70.6 16.6 %collective-permute-start.7 = (f32[32,32]{1,0:T(8,128)S(1)}, f32[32,32]{1,0:T(8,128)S(1)}, u32[]{:S(2)}, u32[]{:S(2)}) collective-permute-start(f32[32,32]{1,0:T(8,128)S(1)} %add.68), channel_id=1, source_target_pairs={{0,8},{4,12},{8,0},{12,4},{1,9},{5,13},{9,1},{13,5},{2,10},{6,14},... | collective-permute-start | bytes 12296 | tf_op jit(solution)/shard_map/ppermute | solution.py:25
  73.1 23.9 %collective-permute-start.10 = (bf16[8,32,1024]{2,1,0:T(8,128)(2,1)S(1)}, bf16[8,32,1024]{2,1,0:T(8,128)(2,1)S(1)}, u32[]{:S(2)}, u32[]{:S(2)}) collective-permute-start(bf16[8,32,1024]{2,1,0:T(8,128)(2,1)S(1)} %constant_dynamic-slice_fusion), channel_id=1, source_target_pairs={{0,12},{4,8},{8,4},{12,0},{1,13},{5,9},{9,5},{13,1},{2,14},{6,10},... | collective-permute-start | bytes 1572872 | tf_op jit(solution)/shard_map/ppermute | solution.py:25
  92.9 0.8 copy-start.4
  93.7 12.1 %collective-permute-start.17 = (bf16[8,32,1024]{2,1,0:T(8,128)(2,1)S(1)}, bf16[8,32,1024]{2,1,0:T(8,128)(2,1)S(1)}, u32[]{:S(2)}, u32[]{:S(2)}) collective-permute-start(bf16[8,32,1024]{2,1,0:T(8,128)(2,1)S(1)} %get-tuple-element.76), channel_id=1, source_target_pairs={{0,4},{4,0},{8,12},{12,8},{1,5},{5,1},{9,13},{13,9},{2,6},{6,2},{1... | collective-permute-start | bytes 1572872 | tf_op jit(solution)/shard_map/ppermute | solution.py:25
  93.7 28.5 %collective-permute-start.16 = (bf16[8,32,1024]{2,1,0:T(8,128)(2,1)}, bf16[8,32,1024]{2,1,0:T(8,128)(2,1)}, u32[]{:S(2)}, u32[]{:S(2)}) collective-permute-start(bf16[8,32,1024]{2,1,0:T(8,128)(2,1)} %get-tuple-element.74), channel_id=1, source_target_pairs={{0,8},{4,12},{8,0},{12,4},{1,9},{5,13},{9,1},{13,5},{2,10},{6,14},... | collective-permute-start | bytes 1572872 | tf_op jit(solution)/shard_map/ppermute | solution.py:25
  95.8 30.9 %collective-permute-start.15 = (bf16[8,32,1024]{2,1,0:T(8,128)(2,1)}, bf16[8,32,1024]{2,1,0:T(8,128)(2,1)}, u32[]{:S(2)}, u32[]{:S(2)}) collective-permute-start(bf16[8,32,1024]{2,1,0:T(8,128)(2,1)} %get-tuple-element.73), channel_id=1, source_target_pairs={{0,12},{4,8},{8,4},{12,0},{1,13},{5,9},{9,5},{13,1},{2,14},{6,10},... | collective-permute-start | bytes 1572872 | tf_op jit(solution)/shard_map/ppermute | solution.py:25
  102.7 0.8 copy-start
  103.5 27.7 %collective-permute-start.13 = (bf16[8,32,1024]{2,1,0:T(8,128)(2,1)}, bf16[8,32,1024]{2,1,0:T(8,128)(2,1)S(1)}, u32[]{:S(2)}, u32[]{:S(2)}) collective-permute-start(bf16[8,32,1024]{2,1,0:T(8,128)(2,1)} %get-tuple-element.72), channel_id=1, source_target_pairs={{0,4},{4,0},{8,12},{12,8},{1,5},{5,1},{9,13},{13,9},{2,6},{6,2},{1... | collective-permute-start | bytes 1572872 | tf_op jit(solution)/shard_map/ppermute | solution.py:25
  104.1 31.5 %collective-permute-start.12 = (bf16[8,32,1024]{2,1,0:T(8,128)(2,1)}, bf16[8,32,1024]{2,1,0:T(8,128)(2,1)S(1)}, u32[]{:S(2)}, u32[]{:S(2)}) collective-permute-start(bf16[8,32,1024]{2,1,0:T(8,128)(2,1)} %get-tuple-element.71), channel_id=1, source_target_pairs={{0,8},{4,12},{8,0},{12,4},{1,9},{5,13},{9,1},{13,5},{2,10},{6,14},... | collective-permute-start | bytes 1572872 | tf_op jit(solution)/shard_map/ppermute | solution.py:25
  105.8 0.8 copy-start.2
  106.6 35.8 %collective-permute-start.11 = (bf16[8,32,1024]{2,1,0:T(8,128)(2,1)}, bf16[8,32,1024]{2,1,0:T(8,128)(2,1)S(1)}, u32[]{:S(2)}, u32[]{:S(2)}) collective-permute-start(bf16[8,32,1024]{2,1,0:T(8,128)(2,1)} %get-tuple-element.70), channel_id=1, source_target_pairs={{0,12},{4,8},{8,4},{12,0},{1,13},{5,9},{9,5},{13,1},{2,14},{6,10},... | collective-permute-start | bytes 1572872 | tf_op jit(solution)/shard_map/ppermute | solution.py:25
  108.0 1.0 copy-start.5
  109.1 4.4 %copy-start.3 = (bf16[8,32,1024]{2,1,0:T(8,128)(2,1)S(1)}, bf16[8,32,1024]{2,1,0:T(8,128)(2,1)}, u32[]{:S(2)}) copy-start(bf16[8,32,1024]{2,1,0:T(8,128)(2,1)} %copy-done.2) | copy-start | bytes 1572868
  113.4 4.4 %copy-start.1 = (bf16[8,32,1024]{2,1,0:T(8,128)(2,1)S(1)}, bf16[8,32,1024]{2,1,0:T(8,128)(2,1)}, u32[]{:S(2)}) copy-start(bf16[8,32,1024]{2,1,0:T(8,128)(2,1)} %copy-done) | copy-start | bytes 1572868

commit v3 on v2

--- a/solution.py
+++ b/solution.py
@@ -19,6 +19,9 @@
 VMEM_BYTES = 48 << 20
 LIGHT = pl.CostEstimate(flops=1024, bytes_accessed=1024, transcendentals=0)
 STEP = pl.CostEstimate(flops=1024, bytes_accessed=1 << 20, transcendentals=0)
+
+
+LAST_CUTS = [(0, 16), (16, 16)]
 
 
 def swap(x, axis, flip):
@@ -57,35 +60,52 @@
     return left == right
 
 
-def stack_pieces(refs):
+def stack_pieces(blocks):
     parts = []
-    for ref in refs:
-        members_dev, block_rows, width = ref.shape
-        parts.append(ref[...].astype(jnp.bfloat16).reshape(members_dev * block_rows, width))
+    for block in blocks:
+        members_dev, block_rows, width = block.shape
+        parts.append(block.astype(jnp.bfloat16).reshape(members_dev * block_rows, width))
     return jnp.concatenate(parts, axis=0)
+
+
+def pieces_of(refs, head_refs, step):
+    blocks = [ref[...] for ref in refs]
+    for head_ref in head_refs:
+        blocks[-1] = jnp.where(step == 0, head_ref[...], blocks[-1])
+    return stack_pieces(blocks)
 
 
 def pack_kernel(me_ref, *refs):
     del me_ref
     for in_ref, out_ref in zip(refs[: len(refs) // 2], refs[len(refs) // 2 :]):
-        out_ref[...] = in_ref[...].astype(out_ref.dtype)
-
-
-def pack_rows(me, params, flips, rows):
-    members_dev, _, width = params.shape
+        skip = in_ref.shape[1] - out_ref.shape[1]
+        out_ref[...] = in_ref[:, skip:, :].astype(out_ref.dtype)
+
+
+def pack_rows(me, params, flips, skips):
+    members_dev, rows_dev, width = params.shape
+    rows = rows_dev // lax.axis_size("member")
     block_members = max(1, members_dev // 2)
-    block = (block_members, rows, width)
     return pl.pallas_call(
         pack_kernel,
-        out_shape=[jax.ShapeDtypeStruct((members_dev, rows, width), jnp.bfloat16)] * len(flips),
+        out_shape=[
+            jax.ShapeDtypeStruct((members_dev, rows - skip, width), jnp.bfloat16)
+            for skip in skips
+        ],
         grid_spec=pltpu.PrefetchScalarGridSpec(
             num_scalar_prefetch=1,
             grid=(members_dev // block_members,),
             in_specs=[
-                pl.BlockSpec(block, lambda i, me_ref, flip=flip: (i, me_ref[0] ^ flip, 0))
+                pl.BlockSpec(
+                    (block_members, rows, width),
+                    lambda i, me_ref, flip=flip: (i, me_ref[0] ^ flip, 0),
+                )
                 for flip in flips
             ],
-            out_specs=[pl.BlockSpec(block, lambda i, me_ref: (i, 0, 0))] * len(flips),
+            out_specs=[
+                pl.BlockSpec((block_members, rows - skip, width), lambda i, me_ref: (i, 0, 0))
+                for skip in skips
+            ],
         ),
         compiler_params=pltpu.CompilerParams(vmem_limit_bytes=VMEM_BYTES),
         cost_estimate=LIGHT,
@@ -93,17 +113,16 @@
     )(me, *[params] * len(flips))
 
 
-def gram_kernel(me_ref, *refs):
+def gram_kernel(n_member, me_ref, *refs):
     *piece_refs, gram_ref, acc_ref = refs
     step = pl.program_id(0)
     members_dev, block_rows, _ = piece_refs[0].shape
-    n_member = len(piece_refs)
 
     @pl.when(step == 0)
     def _():
         acc_ref[...] = jnp.zeros_like(acc_ref)
 
-    stacked = stack_pieces(piece_refs)
+    stacked = pieces_of(piece_refs[:n_member], piece_refs[n_member:], step)
     acc_ref[...] += lax.dot_general(
         stacked, stacked, (((1,), (1,)), ((), ())), preferred_element_type=jnp.float32
     )
@@ -119,7 +138,7 @@
         )
 
 
-def local_gram(me, params, work_pieces):
+def local_gram(me, params, work_pieces, head):
     members_dev, rows_piece, width = work_pieces[0].shape
     n_member = len(work_pieces) + 1
     members = n_member * members_dev
@@ -128,20 +147,22 @@
     block = (members_dev, block_rows, width)
     size = members * block_rows
     return pl.pallas_call(
-        gram_kernel,
+        functools.partial(gram_kernel, n_member),
         out_shape=jax.ShapeDtypeStruct((members, members), jnp.float32),
         grid_spec=pltpu.PrefetchScalarGridSpec(
             num_scalar_prefetch=1,
             grid=(steps,),
             in_specs=[pl.BlockSpec(block, lambda i, me_ref: (0, me_ref[0] * steps + i, 0))]
-            + [pl.BlockSpec(block, lambda i, me_ref: (0, i, 0))] * (n_member - 1),
+            + [pl.BlockSpec(block, lambda i, me_ref: (0, i, 0))] * (n_member - 2)
+            + [pl.BlockSpec(block, lambda i, me_ref: (0, jnp.maximum(i - len(head), 0), 0))]
+            + [pl.BlockSpec(block, lambda i, me_ref: (0, 0, 0))] * len(head),
             out_specs=pl.BlockSpec((members, members), lambda i, me_ref: (0, 0)),
             scratch_shapes=[pltpu.VMEM((size, size), jnp.float32)],
         ),
         compiler_params=pltpu.CompilerParams(vmem_limit_bytes=VMEM_BYTES),
         cost_estimate=LIGHT,
         name="gram",
-    )(me, params, *work_pieces)
+    )(me, params, *work_pieces, *head)
 
 
 def distances(gram):
@@ -154,10 +175,12 @@
     return down + across - 2.0 * gram
 
 
-def mix_kernel(n_member, me_ref, gram_ref, *refs):
-    work_refs, grad_refs = refs[:n_member], refs[n_member : 2 * n_member]
-    out_refs = refs[2 * n_member : 3 * n_member]
-    big_ref, rowsum_ref, repulse_ref = refs[3 * n_member :]
+def mix_kernel(n_member, n_head, cuts, entries, me_ref, gram_ref, *refs):
+    work_refs, refs = refs[:n_member], refs[n_member:]
+    head_refs, grad_refs = refs[:n_head], refs[n_head : n_head + n_member]
+    n_out = n_member - 1 + len(cuts)
+    distance_ref, big_ref, rowsum_ref, repulse_ref = refs[-4:]
+    out_refs = refs[-4 - n_out : -4]
     members_dev, block_rows, width = out_refs[0].shape
     members = n_member * members_dev
     size = members * block_rows
@@ -165,6 +188,7 @@
     @pl.when(pl.program_id(0) == 0)
     def _():
         sqdist = distances(gram_ref[...])
+        distance_ref[...] = sqdist / entries
         total = jnp.sum(jnp.sum(sqdist, axis=1, keepdims=True), axis=0, keepdims=True)
         kernel_scale = total / (members * (members - 1)) / math.log(members)
         kernel_half = jnp.exp(-sqdist / kernel_scale).astype(jnp.bfloat16)
@@ -179,22 +203,32 @@
         repulse_ref[...] = 2.0 / kernel_scale
 
     big = big_ref[...]
-    work = stack_pieces(work_refs)
-    grads = stack_pieces(grad_refs)
+    work = pieces_of(work_refs, head_refs, pl.program_id(0))
+    grads = stack_pieces([ref[...] for ref in grad_refs])
     mixed_grads = jnp.dot(big, grads, preferred_element_type=jnp.float32)
     mixed_work = jnp.dot(big, work, preferred_element_type=jnp.float32)
     stein = (
         repulse_ref[...] * (rowsum_ref[...] * work.astype(jnp.float32) - mixed_work) - mixed_grads
     ) * (1.0 / members)
-    stein = stein.astype(jnp.bfloat16)
-    part = members_dev * block_rows
-    for piece, out_ref in enumerate(out_refs):
-        out_ref[...] = stein[piece * part : (piece + 1) * part].reshape(out_ref.shape)
-
-
-def mix(me, gram, params, work_pieces, gradients, grad_pieces, first_row):
+    stein = stein.reshape(n_member, members_dev, block_rows, width)
+    for piece, out_ref in enumerate(out_refs[: n_member - 1]):
+        out_ref[...] = stein[piece].astype(jnp.bfloat16)
+    for (first, rows), out_ref in zip(cuts, out_refs[n_member - 1 :]):
+        if rows >= block_rows and len(cuts) == 1:
+            out_ref[...] = stein[-1].astype(jnp.bfloat16)
+            continue
+        inner = first % block_rows
+
+        @pl.when(pl.program_id(0) == first // block_rows)
+        def _():
+            out_ref[...] = stein[-1, :, inner : inner + rows].astype(jnp.bfloat16)
+
+
+def mix(
+    me, gram, params, work_pieces, head, gradients, grad_pieces, first_row, rows, cuts, earlier,
+    entries,
+):
     members_dev, rows_piece, width = work_pieces[0].shape
-    rows = min(piece.shape[1] for piece in grad_pieces)
     n_member = len(work_pieces) + 1
     members = n_member * members_dev
     block_rows = min(16, rows)
@@ -203,30 +237,51 @@
     size = members * block_rows
     skip = first_row // block_rows
     per_piece = rows_piece // block_rows
-    whole = pl.BlockSpec(block, lambda i, me_ref: (0, me_ref[0] * per_piece + skip + i, 0))
+    own = pl.BlockSpec(block, lambda i, me_ref: (0, me_ref[0] * per_piece + skip + i, 0))
+    whole = pl.BlockSpec(block, lambda i, me_ref: (0, skip + i, 0))
     part = pl.BlockSpec(block, lambda i, me_ref: (0, i, 0))
-    arrived = pl.BlockSpec(block, lambda i, me_ref: (0, skip + i, 0))
+
+    def fixed(count):
+        return pl.BlockSpec((members_dev, count, width), lambda i, me_ref: (0, 0, 0))
+
+    n_head = len(head)
+    late = pl.BlockSpec(block, lambda i, me_ref: (0, jnp.maximum(skip + i - n_head, 0), 0))
+    if first_row:
+        head = []
+    out_rows = [rows if piece else rows_piece for piece in range(n_member - 1)]
+    out_rows += [count for _, count in cuts]
     return pl.pallas_call(
-        functools.partial(mix_kernel, n_member),
-        out_shape=[jax.ShapeDtypeStruct((members_dev, rows, width), jnp.bfloat16)] * n_member,
+        functools.partial(mix_kernel, n_member, len(head), cuts, entries),
+        out_shape=[
+            jax.ShapeDtypeStruct((members_dev, count, width), jnp.bfloat16) for count in out_rows
+        ]
+        + [jax.ShapeDtypeStruct((members, members), jnp.float32)],
         grid_spec=pltpu.PrefetchScalarGridSpec(
             num_scalar_prefetch=1,
             grid=(steps,),
-            in_specs=[pl.BlockSpec((members, members), lambda i, me_ref: (0, 0)), whole]
-            + [arrived] * (n_member - 1)
-            + [whole]
-            + [part if piece.shape[1] == rows else arrived for piece in grad_pieces],
-            out_specs=[part] * n_member,
+            in_specs=[pl.BlockSpec((members, members), lambda i, me_ref: (0, 0)), own]
+            + [whole] * (n_member - 2)
+            + [late]
+            + [fixed(block_rows)] * len(head)
+            + [own]
+            + [part if piece.shape[1] == rows else whole for piece in grad_pieces]
+            + [pl.BlockSpec(memory_space=pl.ANY)] * len(earlier),
+            out_specs=[part if piece else whole for piece in range(n_member - 1)]
+            + [part if len(cuts) == 1 else fixed(count) for _, count in cuts]
+            + [pl.BlockSpec((members, members), lambda i, me_ref: (0, 0))],
             scratch_shapes=[
                 pltpu.VMEM((size, size), jnp.bfloat16),
                 pltpu.VMEM((size, 1), jnp.float32),
                 pltpu.VMEM((1, 1), jnp.float32),
             ],
         ),
+        input_output_aliases={
+            2 + 2 * n_member + len(head) + idx: idx for idx in range(len(earlier))
+        },
         compiler_params=pltpu.CompilerParams(vmem_limit_bytes=VMEM_BYTES),
         cost_estimate=LIGHT,
         name="mix",
-    )(me, gram, params, *work_pieces, gradients, *grad_pieces)
+    )(me, gram, params, *work_pieces, *head, gradients, *grad_pieces, *earlier)
 
 
 def adamw_kernel(row_ref, params_ref, first_ref, second_ref, stein_ref, *refs):
@@ -248,18 +303,20 @@
 
 def adamw(row_block, params, first_moment, second_moment, stein, earlier):
     members_dev, rows, width = stein.shape
-    block_members = math.gcd(members_dev, 4)
-    block = (block_members, rows, width)
-    home = pl.BlockSpec(block, lambda i, row_ref: (i, row_ref[0], 0))
+    block_members = math.gcd(members_dev, 4 if rows > 16 else 8)
+    block_rows = rows if rows != 16 else 8
+    block = (block_members, block_rows, width)
+    steps = rows // block_rows
+    home = pl.BlockSpec(block, lambda i, j, row_ref: (i, row_ref[0] * steps + j, 0))
     shape = jax.ShapeDtypeStruct(params.shape, jnp.float32)
     return pl.pallas_call(
         adamw_kernel,
         out_shape=[shape] * 5,
         grid_spec=pltpu.PrefetchScalarGridSpec(
             num_scalar_prefetch=1,
-            grid=(members_dev // block_members,),
+            grid=(members_dev // block_members, steps),
             in_specs=[home] * 3
-            + [pl.BlockSpec(block, lambda i, row_ref: (i, 0, 0))]
+            + [pl.BlockSpec(block, lambda i, j, row_ref: (i, j, 0))]
             + [pl.BlockSpec(memory_space=pl.ANY)] * len(earlier),
             out_specs=[home] * 5,
         ),
@@ -283,24 +340,31 @@
     near = [flip for flip in flips if flip == 1]
     far = [2, 3] if n_member == 4 else list(flips)[1:]
 
-    def rows_of(array, flip, part, rows):
-        start = (me ^ flip) * rows_piece + part * rows_part
+    def rows_of(array, flip, first, rows):
+        start = (me ^ flip) * rows_piece + first
         return lax.dynamic_slice(array, (0, start, 0), (members_dev, rows, feature_width))
 
     grads = [{} for _ in range(n_part)]
     work = {}
     last = None
 
-    def finish(flip, part, piece, outs):
-        row_block = ((me ^ flip) * n_part + part)[None]
+    def finish(arrived, outs):
+        flip, first, piece = arrived
+        row_block = (((me ^ flip) * rows_piece + first) // piece.shape[1])[None]
         return adamw(row_block, params, first_moment, second_moment, piece, outs)
 
-    def send(array, flip, part, rows, after):
+    def send(array, flip, first, rows, after):
         source = array if after is None else tied(array, after)
-        packed = rows_of(source, flip, part, rows).astype(jnp.bfloat16)
+        packed = rows_of(source, flip, first, rows).astype(jnp.bfloat16)
         return swap(packed, "member", flip), packed
 
-    packed = pack_rows(me_table, params, far, rows_piece)
+    rows_first = 16 if n_part > 1 else 0
+    head = []
+    if rows_first:
+        arrived, last = send(params, far[-1], 0, rows_first, None)
+        head.append(arrived)
+    skips = [rows_first if flip == far[-1] else 0 for flip in far]
+    packed = pack_rows(me_table if last is None else tied(me_table, last), params, far, skips)
     for flip, piece in zip(far, packed):
         work[flip] = swap(piece, "member", flip)
     last = packed
@@ -309,46 +373,43 @@
         for part in range(n_part):
             grads[part][flip] = whole
     for flip in near:
-        last = (last, work[far[0]]) if far else last
+        last = (last, head)
         work[flip], last = send(params, flip, 0, rows_piece, last)
         whole, last = send(gradients, flip, 0, rows_piece, last)
         for part in range(n_part):
             grads[part][flip] = whole
-    gram = local_gram(me_table, params, [work[flip] for flip in flips])
+    gram = local_gram(me_table, params, [work[flip] for flip in flips], head)
     gram = sum_over(tied(gram, last), "fsdp")
     for flip in near:
         gram = gram + swap(gram, "member", flip)
     last = gram
     for part in range(n_part):
         for flip in far[1:]:
-            grads[part][flip], last = send(gradients, flip, part, rows_part, last)
+            grads[part][flip], last = send(gradients, flip, part * rows_part, rows_part, last)
     gram = sum_over(gram, "member", 2)
     work = [work[flip] for flip in flips]
     grads = [[piece[flip] for flip in flips] for piece in grads]
 
-    stein = [
-        mix(me_table, gram, params, work, gradients, grads[part], part * rows_part)
-        for part in range(n_part)
-    ]
-    back = [
-        {flip: swap(pieces[flip], "member", flip) for flip in far + near} for pieces in stein
-    ]
-    outs = ()
+    kept, back = [], []
     for part in range(n_part):
-        outs = finish(0, part, stein[part][0], outs)
-        if part + 1 < n_part:
-            for flip in near:
-                outs = finish(flip, part, back[part][flip], outs)
-    for part in range(n_part):
-        if part + 1 == n_part:
-            for flip in near:
-                outs = finish(flip, part, back[part][flip], outs)
-        for flip in far:
-            outs = finish(flip, part, back[part][flip], outs)
+        cuts = [(0, rows_part)]
+        if part == n_part - 1 and rows_part == 32:
+            cuts = LAST_CUTS
+        *pieces, pair_distance = mix(
+            me_table, gram, params, work, head, gradients, grads[part],
+            part * rows_part, rows_part, cuts, kept, entries,
+        )
+        kept = pieces[:1]
+        sent = [(flip, 0, pieces[flip]) for flip in near + far[:-1]]
+        sent += [(far[-1], first, piece) for (first, _), piece in zip(cuts, pieces[n_member - 1 :])]
+        for order, (flip, first, piece) in enumerate(sent):
+            if part == 1 and order > 0:
+                piece = tied(piece, back[0][2])
+            back.append((flip, part * rows_part + first, swap(piece, "member", flip)))
+    outs = finish((0, 0, kept[0]), ())
+    for arrived in back:
+        outs = finish(arrived, outs)
     new_params, new_first, new_second, update, stein_dir = outs
-    self_dots = jnp.diagonal(gram)
-    sqdist = self_dots[:, None] + self_dots[None, :] - 2.0 * gram
-    pair_distance = sqdist / entries
     return (new_params, new_first, new_second, update, stein_dir, pair_distance)
 
 

time: 147 us -> 145 us (0.986)
  waiting for transfers between devices: 59.9 us -> 54.1 us
  starting transfers between devices: 16.4 us -> 18.9 us
  local copies, waits for them, and re-layouts: 13.4 us -> 15.4 us
    ppermute x18 -> x20, waiting for transfers between devices: 59.9 us -> 54.1 us  [swap(): lax.ppermute(x, axis, [(i, i ^ flip) for i in range(lax.axis_size(axis))])]
    ppermute x18 -> x20, starting transfers between devices: 16.4 us -> 18.9 us  [swap(): lax.ppermute(x, axis, [(i, i ^ flip) for i in range(lax.axis_size(axis))])]
    unnamed x12 -> x14, local copies, waits for them, and re-layouts: 3.43 us -> 5.09 us
  transfers between devices with their start and end apart: 18 -> 20, of which waited for: 8 -> 7; matrix products, arithmetic and copies ran while one was open for 7% -> 6% of each run, Pallas kernels for 33% -> 36%
where the time goes in v3:
time: 145 us
  Pallas kernels  55.6 us (38%)
  waiting for transfers between devices  54.1 us (37%)
  starting transfers between devices  18.9 us (13%)
  local copies, waits for them, and re-layouts  15.4 us (11%)
    ppermute x20, waiting for transfers between devices, swap(): lax.ppermute(x, axis, [(i, i ^ flip) for i in range(lax.axis_size(axis))])  54.1 us
    pallas_call x8, Pallas kernels, adamw(): pl.pallas_call(adamw_kernel, out_shape=[shape] * 5, grid_spec=pltpu.Prefe...  34.6 us
    ppermute x20, starting transfers between devices, swap(): lax.ppermute(x, axis, [(i, i ^ flip) for i in range(lax.axis_size(axis))])  18.9 us
    pallas_call x2, Pallas kernels, mix(): pl.pallas_call(functools.partial(mix_kernel, n_member, len(head), cuts, e...  11.5 us
    dynamic_slice x4, local copies, waits for them, and re-layouts, rows_of(): lax.dynamic_slice(array, (0, start, 0), (members_dev, rows, feature_width))  7.47 us
    pallas_call x1, Pallas kernels, local_gram(): pl.pallas_call(functools.partial(gram_kernel, n_member), out_shape=jax.Sh...  6.4 us
    unnamed x14, local copies, waits for them, and re-layouts  5.09 us
    pallas_call x1, Pallas kernels, pack_rows(): pl.pallas_call(pack_kernel, out_shape=[jax.ShapeDtypeStruct((members_dev,...  3.06 us
  transfers between devices with their start and end apart: 20, of which 7 were waited for; matrix products, arithmetic and copies ran while one was open for 6% of the time, Pallas kernels for 36%

profile of v3, /device:TPU:0, one launch (start us, length us, event | category | flops | bytes accessed | tf_op | source)
XLA Modules:
  0.0 144.8 jit_solution(8223919565370148858)
XLA Ops:
  0.6 1.1 dynamic-slice_convert_fusion.1
  1.7 2.4 %collective-permute-start = (bf16[8,16,1024]{2,1,0:T(8,128)(2,1)S(1)}, bf16[8,16,1024]{2,1,0:T(8,128)(2,1)S(1)}, u32[]{:S(2)}, u32[]{:S(2)}) collective-permute-start(bf16[8,16,1024]{2,1,0:T(8,128)(2,1)S(1)} %dynamic-slice_convert_fusion.1), channel_id=1, source_target_pairs={{0,12},{4,8},{8,4},{12,0},{1,13},{5,9},{9,5},{13,1},{2,14},{6,10},... | collective-permute-start | bytes 786440 | tf_op jit(solution)/shard_map/ppermute | solution.py:28
  4.2 3.1 %pack.1 = (bf16[8,64,1024]{2,1,0:T(8,128)(2,1)}, bf16[8,48,1024]{2,1,0:T(8,128)(2,1)S(1)}) custom-call(s32[1]{0:T(128)} %bitcast.1.me_ref, f32[8,256,1024]{2,1,0:T(8,128)} %params_ref.15, f32[8,256,1024]{2,1,0:T(8,128)} %params_ref.15), custom_call_target="tpu_custom_call" | custom-call | flops 1024 | bytes 1024 | tf_op jit(solution)/shard_map/pack/pallas_call | solution.py:89
  7.2 0.9 copy-done.6
  8.1 0.6 collective-permute-start.2
  8.7 2.3 %constant_dynamic-slice_fusion.3 = bf16[8,64,1024]{2,1,0:T(8,128)(2,1)} fusion(bf16[8,256,1024]{2,1,0:T(8,128)(2,1)} %refs_4_.1, s32[]{:T(128)S(6)} %select_n.42), kind=kLoop, calls=%fused_computation.6 | loop fusion | bytes 2097156 | tf_op jit(solution)/shard_map/dynamic_slice | solution.py:345
  11.0 1.7 %dynamic-slice_convert_fusion = bf16[8,64,1024]{2,1,0:T(8,128)(2,1)S(1)} fusion(f32[8,256,1024]{2,1,0:T(8,128)} %params_ref.15, s32[]{:T(128)S(6)} %select_n.43), kind=kLoop, calls=%fused_computation | loop fusion | bytes 2097156 | tf_op jit(solution)/shard_map/convert_element_type | solution.py:358
  12.8 0.1 collective-permute-start.1
  12.9 2.4 %collective-permute-start.3 = (bf16[8,48,1024]{2,1,0:T(8,128)(2,1)}, bf16[8,48,1024]{2,1,0:T(8,128)(2,1)S(1)}, u32[]{:S(2)}, u32[]{:S(2)}) collective-permute-start(bf16[8,48,1024]{2,1,0:T(8,128)(2,1)} %copy-done.6), channel_id=1, source_target_pairs={{0,12},{4,8},{8,4},{12,0},{1,13},{5,9},{9,5},{13,1},{2,14},{6,10},... | collective-permute-start | bytes 2359304 | tf_op jit(solution)/shard_map/ppermute | solution.py:28
  15.3 0.1 collective-permute-start.10
  15.3 2.3 %constant_dynamic-slice_fusion.2 = bf16[8,64,1024]{2,1,0:T(8,128)(2,1)} fusion(bf16[8,256,1024]{2,1,0:T(8,128)(2,1)} %refs_4_.1, s32[]{:T(128)S(6)} %select_n.43), kind=kLoop, calls=%fused_computation.5 | loop fusion | bytes 2097156 | tf_op jit(solution)/shard_map/dynamic_slice | solution.py:345
  17.6 0.1 collective-permute-start.9
  17.7 32.9 %collective-permute-done.3.refs_3_ = bf16[8,48,1024]{2,1,0:T(8,128)(2,1)S(1)} collective-permute-done((bf16[8,48,1024]{2,1,0:T(8,128)(2,1)}, bf16[8,48,1024]{2,1,0:T(8,128)(2,1)S(1)}, u32[]{:S(2)}, u32[]{:S(2)}) %collective-permute-start.3) | collective-permute-done | bytes 786464 | tf_op jit(solution)/shard_map/ppermute | solution.py:28
  50.6 6.4 %gram.1 = f32[32,32]{1,0:T(8,128)S(1)} custom-call(s32[1]{0:T(128)} %bitcast.1.me_ref, f32[8,256,1024]{2,1,0:T(8,128)} %params_ref.15, bf16[8,64,1024]{2,1,0:T(8,128)(2,1)S(1)} %collective-permute-done.1.refs_1_, bf16[8,64,1024]{2,1,0:T(8,128)(2,1)S(1)} %collective-permute-done.2.refs_2_, bf16[8,48,1024]{2,1,0:T(8,128)(2,1)S(1)} %collective-permute-done.3.refs_3_, ...), custom_call_target="tpu_custom_call" | custom-call | flops 1024 | bytes 1024 | tf_op jit(solution)/shard_map/gram/pallas_call | solution.py:149
  57.0 4.2 %collective-permute-start.6 = (f32[32,32]{1,0:T(8,128)S(1)}, f32[32,32]{1,0:T(8,128)S(1)}, u32[]{:S(2)}, u32[]{:S(2)}) collective-permute-start(f32[32,32]{1,0:T(8,128)S(1)} %gram.1), channel_id=1, source_target_pairs={{0,3},{1,2},{2,1},{3,0},{4,7},{5,6},{6,5},{7,4},{8,11},{9,10},{10,... | collective-permute-start | bytes 12296 | tf_op jit(solution)/shard_map/ppermute | solution.py:28
  61.2 0.6 collective-permute-start.4
  61.8 1.1 collective-permute-done.6
  62.9 2.9 %collective-permute-done.5 = f32[32,32]{1,0:T(8,128)S(1)} collective-permute-done((f32[32,32]{1,0:T(8,128)S(1)}, f32[32,32]{1,0:T(8,128)S(1)}, u32[]{:S(2)}, u32[]{:S(2)}) %collective-permute-start.5) | collective-permute-done | bytes 4128 | tf_op jit(solution)/shard_map/ppermute | solution.py:28
  65.9 0.1 collective-permute-start.7
  65.9 1.2 collective-permute-done.7
  67.1 1.9 %constant_dynamic-slice_fusion.1 = bf16[8,32,1024]{2,1,0:T(8,128)(2,1)} fusion(bf16[8,256,1024]{2,1,0:T(8,128)(2,1)} %refs_4_.1, s32[]{:T(128)S(6)} %select_n.41), kind=kLoop, calls=%fused_computation.4 | loop fusion | bytes 1048580 | tf_op jit(solution)/shard_map/dynamic_slice | solution.py:345
  69.0 1.3 collective-permute-start.12
  70.3 0.5 collective-permute-start.8
  70.8 1.1 constant_dynamic-slice_fusion
  71.9 1.3 collective-permute-start.11
  73.1 12.1 %collective-permute-done.8 = f32[32,32]{1,0:T(8,128)S(1)} collective-permute-done((f32[32,32]{1,0:T(8,128)S(1)}, f32[32,32]{1,0:T(8,128)S(1)}, u32[]{:S(2)}, u32[]{:S(2)}) %collective-permute-start.8) | collective-permute-done | bytes 4128 | tf_op jit(solution)/shard_map/ppermute | solution.py:28
  85.3 5.7 %mix.2 = (bf16[8,64,1024]{2,1,0:T(8,128)(2,1)S(1)}, bf16[8,32,1024]{2,1,0:T(8,128)(2,1)S(1)}, bf16[8,32,1024]{2,1,0:T(8,128)(2,1)S(1)}, bf16[8,32,1024]{2,1,0:T(8,128)(2,1)}, f32[32,32]{1,0:T(8,128)}) custom-call(s32[1]{0:T(128)} %bitcast.1.me_ref, f32[32,32]{1,0:T(8,128)S(1)} %add.60.gram_ref, f32[8,256,1024]{2,1,0:T(8,128)} %params_ref.15, ...), custom_call_target="tpu_custom_call" | custom-call | flops 1024 | bytes 1024 | tf_op jit(solution)/shard_map/mix/pallas_call | solution.py:253
  91.0 1.5 %collective-permute-start.19 = (bf16[8,32,1024]{2,1,0:T(8,128)(2,1)S(1)}, bf16[8,32,1024]{2,1,0:T(8,128)(2,1)S(1)}, u32[]{:S(2)}, u32[]{:S(2)}) collective-permute-start(bf16[8,32,1024]{2,1,0:T(8,128)(2,1)S(1)} %get-tuple-element.87), channel_id=1, source_target_pairs={{0,8},{4,12},{8,0},{12,4},{1,9},{5,13},{9,1},{13,5},{2,10},{6,14},... | collective-permute-start | bytes 1572872 | tf_op jit(solution)/shard_map/ppermute | solution.py:28
  92.6 0.3 collective-permute-start.18
  92.9 3.0 %collective-permute-done.11.refs_7_ = bf16[8,32,1024]{2,1,0:T(8,128)(2,1)S(1)} collective-permute-done((bf16[8,32,1024]{2,1,0:T(8,128)(2,1)S(1)}, bf16[8,32,1024]{2,1,0:T(8,128)(2,1)S(1)}, u32[]{:S(2)}, u32[]{:S(2)}) %collective-permute-start.11) | collective-permute-done | bytes 524320 | tf_op jit(solution)/shard_map/ppermute | solution.py:28
  95.9 1.2 copy-done.1
  97.1 5.8 %mix.3 = (bf16[8,64,1024]{2,1,0:T(8,128)(2,1)S(1)}, bf16[8,32,1024]{2,1,0:T(8,128)(2,1)}, bf16[8,32,1024]{2,1,0:T(8,128)(2,1)}, bf16[8,16,1024]{2,1,0:T(8,128)(2...) custom-call(s32[1]{0:T(128)} %bitcast.1.me_ref, ...), custom_call_target="tpu_custom_call", output_to_operand_aliasing={{0}: (10, {})} | custom-call | flops 1024 | bytes 1024 | tf_op jit(solution)/shard_map/mix/pallas_call | solution.py:253
  102.9 0.0 copy-start.2
  102.9 1.0 copy-done.2
  103.9 0.4 collective-permute-start.17
  104.3 0.8 copy-done.4
  105.1 1.8 %collective-permute-start.16 = (bf16[8,32,1024]{2,1,0:T(8,128)(2,1)}, bf16[8,32,1024]{2,1,0:T(8,128)(2,1)S(1)}, u32[]{:S(2)}, u32[]{:S(2)}) collective-permute-start(bf16[8,32,1024]{2,1,0:T(8,128)(2,1)} %get-tuple-element.84), channel_id=1, source_target_pairs={{0,8},{4,12},{8,0},{12,4},{1,9},{5,13},{9,1},{13,5},{2,10},{6,14},... | collective-permute-start | bytes 1572872 | tf_op jit(solution)/shard_map/ppermute | solution.py:28
  106.9 0.8 collective-permute-done.19.stein_ref
  107.7 1.2 collective-permute-start.14
  108.9 1.2 copy-done.3
  110.1 7.2 %adamw.8 = (f32[8,256,1024]{2,1,0:T(8,128)}, f32[8,256,1024]{2,1,0:T(8,128)}, f32[8,256,1024]{2,1,0:T(8,128)}, f32[8,256,1024]{2,1,0:T(8,128)}, f32[8,256,1024]{2,1,0:T(8,128)}) custom-call(s32[1]{0:T(128)} %bitcast.8.row_ref, f32[8,256,1024]{2,1,0:T(8,128)} %params_ref.15, f32[8,256,1024]{2,1,0:T(8,128)} %first_ref.15, f32[8,256,1024]{2,1,0:T(8,128)} %second_ref.15, ...), custom_call_target="tpu_custom_call" | custom-call | flops 1024 | bytes 1048576 | tf_op jit(solution)/shard_map/adamw/pallas_call | solution.py:312
  117.3 4.4 %adamw.9 = (f32[8,256,1024]{2,1,0:T(8,128)}, f32[8,256,1024]{2,1,0:T(8,128)}, f32[8,256,1024]{2,1,0:T(8,128)}, f32[8,256,1024]{2,1,0:T(8,128)}, f32[8,256,1024]{2,1,0:T(8,128)}) custom-call(s32[1]{0:T(128)} %bitcast.7.row_ref, f32[8,256,1024]{2,1,0:T(8,128)} %params_ref.15, ...), custom_call_target="tpu_custom_call", output_to_operand_aliasing={{0}: (5, {}), {1}: (6, {}), {2}: (7, {}), {3}: (8, {}), {4}... | custom-call | flops 1024 | bytes 1048576 | tf_op jit(solution)/shard_map/adamw/pallas_call | solution.py:312
  121.7 4.4 %adamw.10 = (f32[8,256,1024]{2,1,0:T(8,128)}, f32[8,256,1024]{2,1,0:T(8,128)}, f32[8,256,1024]{2,1,0:T(8,128)}, f32[8,256,1024]{2,1,0:T(8,128)}, f32[8,256,1024]{2,1,0:T(8,128)}) custom-call(s32[1]{0:T(128)} %bitcast.6.row_ref, f32[8,256,1024]{2,1,0:T(8,128)} %params_ref.15, ...), custom_call_target="tpu_custom_call", output_to_operand_aliasing={{0}: (5, {}), {1}: (6, {}), {2}: (7, {}), {3}: (8, {}), {4}... | custom-call | flops 1024 | bytes 1048576 | tf_op jit(solution)/shard_map/adamw/pallas_call | solution.py:312
  126.1 4.4 %adamw.11 = (f32[8,256,1024]{2,1,0:T(8,128)}, f32[8,256,1024]{2,1,0:T(8,128)}, f32[8,256,1024]{2,1,0:T(8,128)}, f32[8,256,1024]{2,1,0:T(8,128)}, f32[8,256,1024]{2,1,0:T(8,128)}) custom-call(s32[1]{0:T(128)} %bitcast.5.row_ref, f32[8,256,1024]{2,1,0:T(8,128)} %params_ref.15, ...), custom_call_target="tpu_custom_call", output_to_operand_aliasing={{0}: (5, {}), {1}: (6, {}), {2}: (7, {}), {3}: (8, {}), {4}... | custom-call | flops 1024 | bytes 1048576 | tf_op jit(solution)/shard_map/adamw/pallas_call | solution.py:312
  130.5 4.4 %adamw.12 = (f32[8,256,1024]{2,1,0:T(8,128)}, f32[8,256,1024]{2,1,0:T(8,128)}, f32[8,256,1024]{2,1,0:T(8,128)}, f32[8,256,1024]{2,1,0:T(8,128)}, f32[8,256,1024]{2,1,0:T(8,128)}) custom-call(s32[1]{0:T(128)} %bitcast.4.row_ref, f32[8,256,1024]{2,1,0:T(8,128)} %params_ref.15, ...), custom_call_target="tpu_custom_call", output_to_operand_aliasing={{0}: (5, {}), {1}: (6, {}), {2}: (7, {}), {3}: (8, {}), {4}... | custom-call | flops 1024 | bytes 1048576 | tf_op jit(solution)/shard_map/adamw/pallas_call | solution.py:312
  134.8 4.4 %adamw.13 = (f32[8,256,1024]{2,1,0:T(8,128)}, f32[8,256,1024]{2,1,0:T(8,128)}, f32[8,256,1024]{2,1,0:T(8,128)}, f32[8,256,1024]{2,1,0:T(8,128)}, f32[8,256,1024]{2,1,0:T(8,128)}) custom-call(s32[1]{0:T(128)} %bitcast.3.row_ref, f32[8,256,1024]{2,1,0:T(8,128)} %params_ref.15, ...), custom_call_target="tpu_custom_call", output_to_operand_aliasing={{0}: (5, {}), {1}: (6, {}), {2}: (7, {}), {3}: (8, {}), {4}... | custom-call | flops 1024 | bytes 1048576 | tf_op jit(solution)/shard_map/adamw/pallas_call | solution.py:312
  139.2 2.8 %adamw.14 = (f32[8,256,1024]{2,1,0:T(8,128)}, f32[8,256,1024]{2,1,0:T(8,128)}, f32[8,256,1024]{2,1,0:T(8,128)}, f32[8,256,1024]{2,1,0:T(8,128)}, f32[8,256,1024]{2,1,0:T(8,128)}) custom-call(s32[1]{0:T(128)} %bitcast.2.row_ref, f32[8,256,1024]{2,1,0:T(8,128)} %params_ref.15, ...), custom_call_target="tpu_custom_call", output_to_operand_aliasing={{0}: (5, {}), {1}: (6, {}), {2}: (7, {}), {3}: (8, {}), {4}... | custom-call | flops 1024 | bytes 1048576 | tf_op jit(solution)/shard_map/adamw/pallas_call | solution.py:312
  142.0 2.8 %adamw.15 = (f32[8,256,1024]{2,1,0:T(8,128)}, f32[8,256,1024]{2,1,0:T(8,128)}, f32[8,256,1024]{2,1,0:T(8,128)}, f32[8,256,1024]{2,1,0:T(8,128)}, f32[8,256,1024]{2,1,0:T(8,128)}) custom-call(s32[1]{0:T(128)} %bitcast.row_ref, f32[8,256,1024]{2,1,0:T(8,128)} %params_ref.15, ...), custom_call_target="tpu_custom_call", output_to_operand_aliasing={{0}: (5, {}), {1}: (6, {}), {2}: (7, {}), {3}: (8, {}), {4}... | custom-call | flops 1024 | bytes 1048576 | tf_op jit(solution)/shard_map/adamw/pallas_call | solution.py:312
  (27 shorter events, 0.1 us)
Async XLA Ops:
  1.7 9.3 %collective-permute-start = (bf16[8,16,1024]{2,1,0:T(8,128)(2,1)S(1)}, bf16[8,16,1024]{2,1,0:T(8,128)(2,1)S(1)}, u32[]{:S(2)}, u32[]{:S(2)}) collective-permute-start(bf16[8,16,1024]{2,1,0:T(8,128)(2,1)S(1)} %dynamic-slice_convert_fusion.1), channel_id=1, source_target_pairs={{0,12},{4,8},{8,4},{12,0},{1,13},{5,9},{9,5},{13,1},{2,14},{6,10},... | collective-permute-start | bytes 786440 | tf_op jit(solution)/shard_map/ppermute | solution.py:28
  7.2 0.9 copy-start.6
  8.1 42.5 %collective-permute-start.2 = (bf16[8,64,1024]{2,1,0:T(8,128)(2,1)}, bf16[8,64,1024]{2,1,0:T(8,128)(2,1)S(1)}, u32[]{:S(2)}, u32[]{:S(2)}) collective-permute-start(bf16[8,64,1024]{2,1,0:T(8,128)(2,1)} %get-tuple-element.69), channel_id=1, source_target_pairs={{0,8},{4,12},{8,0},{12,4},{1,9},{5,13},{9,1},{13,5},{2,10},{6,14},... | collective-permute-start | bytes 3145736 | tf_op jit(solution)/shard_map/ppermute | solution.py:28
  12.8 37.9 %collective-permute-start.1 = (bf16[8,64,1024]{2,1,0:T(8,128)(2,1)S(1)}, bf16[8,64,1024]{2,1,0:T(8,128)(2,1)S(1)}, u32[]{:S(2)}, u32[]{:S(2)}) collective-permute-start(bf16[8,64,1024]{2,1,0:T(8,128)(2,1)S(1)} %dynamic-slice_convert_fusion), channel_id=1, source_target_pairs={{0,4},{4,0},{8,12},{12,8},{1,5},{5,1},{9,13},{13,9},{2,6},{6,2},{1... | collective-permute-start | bytes 3145736 | tf_op jit(solution)/shard_map/ppermute | solution.py:28
  12.9 37.7 %collective-permute-start.3 = (bf16[8,48,1024]{2,1,0:T(8,128)(2,1)}, bf16[8,48,1024]{2,1,0:T(8,128)(2,1)S(1)}, u32[]{:S(2)}, u32[]{:S(2)}) collective-permute-start(bf16[8,48,1024]{2,1,0:T(8,128)(2,1)} %copy-done.6), channel_id=1, source_target_pairs={{0,12},{4,8},{8,4},{12,0},{1,13},{5,9},{9,5},{13,1},{2,14},{6,10},... | collective-permute-start | bytes 2359304 | tf_op jit(solution)/shard_map/ppermute | solution.py:28
  15.3 70.0 %collective-permute-start.10 = (bf16[8,64,1024]{2,1,0:T(8,128)(2,1)}, bf16[8,64,1024]{2,1,0:T(8,128)(2,1)}, u32[]{:S(2)}, u32[]{:S(2)}) collective-permute-start(bf16[8,64,1024]{2,1,0:T(8,128)(2,1)} %constant_dynamic-slice_fusion.3), channel_id=1, source_target_pairs={{0,8},{4,12},{8,0},{12,4},{1,9},{5,13},{9,1},{13,5},{2,10},{6,14},... | collective-permute-start | bytes 3145736 | tf_op jit(solution)/shard_map/ppermute | solution.py:28
  17.6 67.7 %collective-permute-start.9 = (bf16[8,64,1024]{2,1,0:T(8,128)(2,1)}, bf16[8,64,1024]{2,1,0:T(8,128)(2,1)}, u32[]{:S(2)}, u32[]{:S(2)}) collective-permute-start(bf16[8,64,1024]{2,1,0:T(8,128)(2,1)} %constant_dynamic-slice_fusion.2), channel_id=1, source_target_pairs={{0,4},{4,0},{8,12},{12,8},{1,5},{5,1},{9,13},{13,9},{2,6},{6,2},{1... | collective-permute-start | bytes 3145736 | tf_op jit(solution)/shard_map/ppermute | solution.py:28
  50.6 34.7 %copy-start = (bf16[8,64,1024]{2,1,0:T(8,128)(2,1)}, bf16[8,64,1024]{2,1,0:T(8,128)(2,1)S(1)}, u32[]{:S(2)}) copy-start(bf16[8,64,1024]{2,1,0:T(8,128)(2,1)S(1)} %collective-permute-done.2.refs_2_) | copy-start | bytes 3145732
  57.0 5.9 %collective-permute-start.6 = (f32[32,32]{1,0:T(8,128)S(1)}, f32[32,32]{1,0:T(8,128)S(1)}, u32[]{:S(2)}, u32[]{:S(2)}) collective-permute-start(f32[32,32]{1,0:T(8,128)S(1)} %gram.1), channel_id=1, source_target_pairs={{0,3},{1,2},{2,1},{3,0},{4,7},{5,6},{6,5},{7,4},{8,11},{9,10},{10,... | collective-permute-start | bytes 12296 | tf_op jit(solution)/shard_map/ppermute | solution.py:28
  61.2 4.6 %collective-permute-start.5 = (f32[32,32]{1,0:T(8,128)S(1)}, f32[32,32]{1,0:T(8,128)S(1)}, u32[]{:S(2)}, u32[]{:S(2)}) collective-permute-start(f32[32,32]{1,0:T(8,128)S(1)} %gram.1), channel_id=1, source_target_pairs={{0,2},{1,3},{2,0},{3,1},{4,6},{5,7},{6,4},{7,5},{8,10},{9,11},{10,... | collective-permute-start | bytes 12296 | tf_op jit(solution)/shard_map/ppermute | solution.py:28
  61.2 4.6 %collective-permute-start.4 = (f32[32,32]{1,0:T(8,128)S(1)}, f32[32,32]{1,0:T(8,128)S(1)}, u32[]{:S(2)}, u32[]{:S(2)}) collective-permute-start(f32[32,32]{1,0:T(8,128)S(1)} %gram.1), channel_id=1, source_target_pairs={{0,1},{1,0},{2,3},{3,2},{4,5},{5,4},{6,7},{7,6},{8,9},{9,8},{10,11... | collective-permute-start | bytes 12296 | tf_op jit(solution)/shard_map/ppermute | solution.py:28
  65.9 1.2 collective-permute-start.7
  69.0 16.3 %collective-permute-start.12 = (bf16[8,32,1024]{2,1,0:T(8,128)(2,1)}, bf16[8,32,1024]{2,1,0:T(8,128)(2,1)}, u32[]{:S(2)}, u32[]{:S(2)}) collective-permute-start(bf16[8,32,1024]{2,1,0:T(8,128)(2,1)} %constant_dynamic-slice_fusion.1), channel_id=1, source_target_pairs={{0,12},{4,8},{8,4},{12,0},{1,13},{5,9},{9,5},{13,1},{2,14},{6,10},... | collective-permute-start | bytes 1572872 | tf_op jit(solution)/shard_map/ppermute | solution.py:28
  70.3 15.0 %collective-permute-start.8 = (f32[32,32]{1,0:T(8,128)S(1)}, f32[32,32]{1,0:T(8,128)S(1)}, u32[]{:S(2)}, u32[]{:S(2)}) collective-permute-start(f32[32,32]{1,0:T(8,128)S(1)} %add.59), channel_id=1, source_target_pairs={{0,8},{4,12},{8,0},{12,4},{1,9},{5,13},{9,1},{13,5},{2,10},{6,14},... | collective-permute-start | bytes 12296 | tf_op jit(solution)/shard_map/ppermute | solution.py:28
  71.9 24.1 %collective-permute-start.11 = (bf16[8,32,1024]{2,1,0:T(8,128)(2,1)S(1)}, bf16[8,32,1024]{2,1,0:T(8,128)(2,1)S(1)}, u32[]{:S(2)}, u32[]{:S(2)}) collective-permute-start(bf16[8,32,1024]{2,1,0:T(8,128)(2,1)S(1)} %constant_dynamic-slice_fusion), channel_id=1, source_target_pairs={{0,12},{4,8},{8,4},{12,0},{1,13},{5,9},{9,5},{13,1},{2,14},{6,10},... | collective-permute-start | bytes 1572872 | tf_op jit(solution)/shard_map/ppermute | solution.py:28
  91.0 13.3 %collective-permute-start.13 = (bf16[8,32,1024]{2,1,0:T(8,128)(2,1)S(1)}, bf16[8,32,1024]{2,1,0:T(8,128)(2,1)S(1)}, u32[]{:S(2)}, u32[]{:S(2)}) collective-permute-start(bf16[8,32,1024]{2,1,0:T(8,128)(2,1)S(1)} %get-tuple-element.79), channel_id=1, source_target_pairs={{0,4},{4,0},{8,12},{12,8},{1,5},{5,1},{9,13},{13,9},{2,6},{6,2},{1... | collective-permute-start | bytes 1572872 | tf_op jit(solution)/shard_map/ppermute | solution.py:28
  91.0 16.7 %collective-permute-start.19 = (bf16[8,32,1024]{2,1,0:T(8,128)(2,1)S(1)}, bf16[8,32,1024]{2,1,0:T(8,128)(2,1)S(1)}, u32[]{:S(2)}, u32[]{:S(2)}) collective-permute-start(bf16[8,32,1024]{2,1,0:T(8,128)(2,1)S(1)} %get-tuple-element.87), channel_id=1, source_target_pairs={{0,8},{4,12},{8,0},{12,4},{1,9},{5,13},{9,1},{13,5},{2,10},{6,14},... | collective-permute-start | bytes 1572872 | tf_op jit(solution)/shard_map/ppermute | solution.py:28
  92.6 33.5 %collective-permute-start.18 = (bf16[8,32,1024]{2,1,0:T(8,128)(2,1)}, bf16[8,32,1024]{2,1,0:T(8,128)(2,1)S(1)}, u32[]{:S(2)}, u32[]{:S(2)}) collective-permute-start(bf16[8,32,1024]{2,1,0:T(8,128)(2,1)} %get-tuple-element.86), channel_id=1, source_target_pairs={{0,12},{4,8},{8,4},{12,0},{1,13},{5,9},{9,5},{13,1},{2,14},{6,10},... | collective-permute-start | bytes 1572872 | tf_op jit(solution)/shard_map/ppermute | solution.py:28
  95.9 1.2 copy-start.1
  102.9 1.0 copy-start.2
  103.9 26.6 %collective-permute-start.17 = (bf16[8,32,1024]{2,1,0:T(8,128)(2,1)}, bf16[8,32,1024]{2,1,0:T(8,128)(2,1)S(1)}, u32[]{:S(2)}, u32[]{:S(2)}) collective-permute-start(bf16[8,32,1024]{2,1,0:T(8,128)(2,1)} %get-tuple-element.85), channel_id=1, source_target_pairs={{0,4},{4,0},{8,12},{12,8},{1,5},{5,1},{9,13},{13,9},{2,6},{6,2},{1... | collective-permute-start | bytes 1572872 | tf_op jit(solution)/shard_map/ppermute | solution.py:28
  104.3 0.8 copy-start.4
  105.1 29.7 %collective-permute-start.16 = (bf16[8,32,1024]{2,1,0:T(8,128)(2,1)}, bf16[8,32,1024]{2,1,0:T(8,128)(2,1)S(1)}, u32[]{:S(2)}, u32[]{:S(2)}) collective-permute-start(bf16[8,32,1024]{2,1,0:T(8,128)(2,1)} %get-tuple-element.84), channel_id=1, source_target_pairs={{0,8},{4,12},{8,0},{12,4},{1,9},{5,13},{9,1},{13,5},{2,10},{6,14},... | collective-permute-start | bytes 1572872 | tf_op jit(solution)/shard_map/ppermute | solution.py:28
  106.9 32.3 %collective-permute-start.15 = (bf16[8,16,1024]{2,1,0:T(8,128)(2,1)}, bf16[8,16,1024]{2,1,0:T(8,128)(2,1)S(1)}, u32[]{:S(2)}, u32[]{:S(2)}) collective-permute-start(bf16[8,16,1024]{2,1,0:T(8,128)(2,1)} %get-tuple-element.82), channel_id=1, source_target_pairs={{0,12},{4,8},{8,4},{12,0},{1,13},{5,9},{9,5},{13,1},{2,14},{6,10},... | collective-permute-start | bytes 786440 | tf_op jit(solution)/shard_map/ppermute | solution.py:28
  107.7 34.3 %collective-permute-start.14 = (bf16[8,16,1024]{2,1,0:T(8,128)(2,1)}, bf16[8,16,1024]{2,1,0:T(8,128)(2,1)S(1)}, u32[]{:S(2)}, u32[]{:S(2)}) collective-permute-start(bf16[8,16,1024]{2,1,0:T(8,128)(2,1)} %get-tuple-element.80), channel_id=1, source_target_pairs={{0,12},{4,8},{8,4},{12,0},{1,13},{5,9},{9,5},{13,1},{2,14},{6,10},... | collective-permute-start | bytes 786440 | tf_op jit(solution)/shard_map/ppermute | solution.py:28
  108.9 1.2 copy-start.3
  110.1 7.2 %copy-start.5 = (bf16[8,32,1024]{2,1,0:T(8,128)(2,1)S(1)}, bf16[8,32,1024]{2,1,0:T(8,128)(2,1)}, u32[]{:S(2)}) copy-start(bf16[8,32,1024]{2,1,0:T(8,128)(2,1)} %copy-done.4) | copy-start | bytes 1572868

commit v4 on v3

--- a/solution.py
+++ b/solution.py
@@ -284,11 +284,14 @@
     )(me, gram, params, *work_pieces, *head, gradients, *grad_pieces, *earlier)
 
 
-def adamw_kernel(row_ref, params_ref, first_ref, second_ref, stein_ref, *refs):
+def adamw_kernel(n_pieces, row_ref, params_ref, first_ref, second_ref, *refs):
     del row_ref
     new_params_ref, new_first_ref, new_second_ref, update_ref, stein_dir_ref = refs[-5:]
+    stein = refs[0][...]
+    for piece in range(1, n_pieces):
+        stein = jnp.where(pl.program_id(0) >= piece, refs[piece][...], stein)
     params = params_ref[...]
-    stein_dir = stein_ref[...].astype(jnp.float32)
+    stein_dir = stein.astype(jnp.float32)
     new_first = decay_first * first_ref[...] - (1.0 - decay_first) * stein_dir
     new_second = decay_second * second_ref[...] + (1.0 - decay_second) * stein_dir * stein_dir
     first_hat = new_first * (1.0 / (1.0 - decay_first**STEP_COUNT))
@@ -301,30 +304,41 @@
     stein_dir_ref[...] = stein_dir
 
 
-def adamw(row_block, params, first_moment, second_moment, stein, earlier):
-    members_dev, rows, width = stein.shape
-    block_members = math.gcd(members_dev, 4 if rows > 16 else 8)
+def adamw(row_blocks, params, first_moment, second_moment, pieces, earlier):
+    members_dev, rows, width = pieces[0].shape
+    block_members = math.gcd(members_dev, 4 if rows > 16 and len(pieces) == 1 else 8)
     block_rows = rows if rows != 16 else 8
     block = (block_members, block_rows, width)
-    steps = rows // block_rows
-    home = pl.BlockSpec(block, lambda i, j, row_ref: (i, row_ref[0] * steps + j, 0))
+    outer, inner = members_dev // block_members, rows // block_rows
+
+    def home_index(q, i, j, row_ref):
+        return (i, row_ref[q] * inner + j, 0)
+
+    def piece_spec(piece):
+        def index(q, i, j, row_ref):
+            away = jnp.where(q < piece, 0, outer - 1), jnp.where(q < piece, 0, inner - 1)
+            return (jnp.where(q == piece, i, away[0]), jnp.where(q == piece, j, away[1]), 0)
+
+        return pl.BlockSpec(block, index)
+
+    home = pl.BlockSpec(block, home_index)
     shape = jax.ShapeDtypeStruct(params.shape, jnp.float32)
     return pl.pallas_call(
-        adamw_kernel,
+        functools.partial(adamw_kernel, len(pieces)),
         out_shape=[shape] * 5,
         grid_spec=pltpu.PrefetchScalarGridSpec(
             num_scalar_prefetch=1,
-            grid=(members_dev // block_members, steps),
+            grid=(len(pieces), outer, inner),
             in_specs=[home] * 3
-            + [pl.BlockSpec(block, lambda i, j, row_ref: (i, j, 0))]
+            + [piece_spec(piece) for piece in range(len(pieces))]
             + [pl.BlockSpec(memory_space=pl.ANY)] * len(earlier),
             out_specs=[home] * 5,
         ),
-        input_output_aliases={5 + idx: idx for idx in range(len(earlier))},
+        input_output_aliases={4 + len(pieces) + idx: idx for idx in range(len(earlier))},
         compiler_params=pltpu.CompilerParams(vmem_limit_bytes=VMEM_BYTES),
         cost_estimate=STEP,
         name="adamw",
-    )(row_block, params, first_moment, second_moment, stein, *earlier)
+    )(row_blocks, params, first_moment, second_moment, *pieces, *earlier)
 
 
 def shards(params, gradients, first_moment, second_moment):
@@ -348,10 +362,12 @@
     work = {}
     last = None
 
-    def finish(arrived, outs):
-        flip, first, piece = arrived
-        row_block = (((me ^ flip) * rows_piece + first) // piece.shape[1])[None]
-        return adamw(row_block, params, first_moment, second_moment, piece, outs)
+    def finish(group, outs):
+        blocks = [((me ^ flip) * rows_piece + first) // piece.shape[1] for flip, first, piece in group]
+        pieces = [piece for _, _, piece in group]
+        return adamw(
+            jnp.stack(blocks), params, first_moment, second_moment, pieces, outs
+        )
 
     def send(array, flip, first, rows, after):
         source = array if after is None else tied(array, after)
@@ -406,9 +422,15 @@
             if part == 1 and order > 0:
                 piece = tied(piece, back[0][2])
             back.append((flip, part * rows_part + first, swap(piece, "member", flip)))
-    outs = finish((0, 0, kept[0]), ())
-    for arrived in back:
-        outs = finish(arrived, outs)
+    groups = [[(0, 0, kept[0])]]
+    for idx, arrived in enumerate(back):
+        if n_part > 1 and idx in (2, 4) and arrived[2].shape == back[idx - 1][2].shape:
+            groups[-1].append(arrived)
+        else:
+            groups.append([arrived])
+    outs = ()
+    for group in groups:
+        outs = finish(group, outs)
     new_params, new_first, new_second, update, stein_dir = outs
     return (new_params, new_first, new_second, update, stein_dir, pair_distance)
 

time: 145 us -> 144 us (level)
  Pallas kernels: 55.6 us -> 53.4 us
  waiting for transfers between devices: 54.1 us -> 55.8 us
    pallas_call x8 -> x6, Pallas kernels: 34.6 us -> 32.4 us  [adamw(): pl.pallas_call(functools.partial(adamw_kernel, len(pieces)), out_shape=[s...]
    ppermute x20, waiting for transfers between devices: 54.1 us -> 55.8 us  [swap(): lax.ppermute(x, axis, [(i, i ^ flip) for i in range(lax.axis_size(axis))])]
    unnamed x14 -> x10, local copies, waits for them, and re-layouts: 5.09 us -> 4.3 us
  transfers between devices with their start and end apart: 20 -> 20, of which waited for: 7 -> 9; matrix products, arithmetic and copies ran while one was open for 6% -> 7% of each run, Pallas kernels for 36% -> 35%
where the time goes in v4:
time: 144 us
  waiting for transfers between devices  55.8 us (39%)
  Pallas kernels  53.4 us (37%)
  starting transfers between devices  18.9 us (13%)
  local copies, waits for them, and re-layouts  14.6 us (10%)
    ppermute x20, waiting for transfers between devices, swap(): lax.ppermute(x, axis, [(i, i ^ flip) for i in range(lax.axis_size(axis))])  55.8 us
    pallas_call x6, Pallas kernels, adamw(): pl.pallas_call(functools.partial(adamw_kernel, len(pieces)), out_shape=[s...  32.4 us
    ppermute x20, starting transfers between devices, swap(): lax.ppermute(x, axis, [(i, i ^ flip) for i in range(lax.axis_size(axis))])  18.9 us
    pallas_call x2, Pallas kernels, mix(): pl.pallas_call(functools.partial(mix_kernel, n_member, len(head), cuts, e...  11.5 us
    dynamic_slice x4, local copies, waits for them, and re-layouts, rows_of(): lax.dynamic_slice(array, (0, start, 0), (members_dev, rows, feature_width))  7.47 us
    pallas_call x1, Pallas kernels, local_gram(): pl.pallas_call(functools.partial(gram_kernel, n_member), out_shape=jax.Sh...  6.4 us
    unnamed x10, local copies, waits for them, and re-layouts  4.3 us
    pallas_call x1, Pallas kernels, pack_rows(): pl.pallas_call(pack_kernel, out_shape=[jax.ShapeDtypeStruct((members_dev,...  3.06 us
  transfers between devices with their start and end apart: 20, of which 9 were waited for; matrix products, arithmetic and copies ran while one was open for 7% of the time, Pallas kernels for 35%

profile of v4, /device:TPU:0, one launch (start us, length us, event | category | flops | bytes accessed | tf_op | source)
XLA Modules:
  0.0 143.5 jit_solution(16542544159056752724)
XLA Ops:
  0.6 1.1 dynamic-slice_convert_fusion.1
  1.7 2.4 %collective-permute-start = (bf16[8,16,1024]{2,1,0:T(8,128)(2,1)S(1)}, bf16[8,16,1024]{2,1,0:T(8,128)(2,1)S(1)}, u32[]{:S(2)}, u32[]{:S(2)}) collective-permute-start(bf16[8,16,1024]{2,1,0:T(8,128)(2,1)S(1)} %dynamic-slice_convert_fusion.1), channel_id=1, source_target_pairs={{0,12},{4,8},{8,4},{12,0},{1,13},{5,9},{9,5},{13,1},{2,14},{6,10},... | collective-permute-start | bytes 786440 | tf_op jit(solution)/shard_map/ppermute | solution.py:28
  4.2 3.1 %pack.1 = (bf16[8,64,1024]{2,1,0:T(8,128)(2,1)}, bf16[8,48,1024]{2,1,0:T(8,128)(2,1)S(1)}) custom-call(s32[1]{0:T(128)} %bitcast.1.me_ref, f32[8,256,1024]{2,1,0:T(8,128)} %params_ref.11, f32[8,256,1024]{2,1,0:T(8,128)} %params_ref.11), custom_call_target="tpu_custom_call" | custom-call | flops 1024 | bytes 1024 | tf_op jit(solution)/shard_map/pack/pallas_call | solution.py:89
  7.2 0.9 copy-done.4
  8.1 0.6 collective-permute-start.2
  8.7 2.3 %constant_dynamic-slice_fusion.3 = bf16[8,64,1024]{2,1,0:T(8,128)(2,1)} fusion(bf16[8,256,1024]{2,1,0:T(8,128)(2,1)} %refs_4_.1, s32[]{:T(128)S(6)} %select_n.42), kind=kLoop, calls=%fused_computation.6 | loop fusion | bytes 2097156 | tf_op jit(solution)/shard_map/dynamic_slice | solution.py:359
  11.0 1.7 %dynamic-slice_convert_fusion = bf16[8,64,1024]{2,1,0:T(8,128)(2,1)S(1)} fusion(f32[8,256,1024]{2,1,0:T(8,128)} %params_ref.11, s32[]{:T(128)S(6)} %select_n.43), kind=kLoop, calls=%fused_computation | loop fusion | bytes 2097156 | tf_op jit(solution)/shard_map/convert_element_type | solution.py:374
  12.8 0.1 collective-permute-start.1
  12.9 2.4 %collective-permute-start.3 = (bf16[8,48,1024]{2,1,0:T(8,128)(2,1)}, bf16[8,48,1024]{2,1,0:T(8,128)(2,1)S(1)}, u32[]{:S(2)}, u32[]{:S(2)}) collective-permute-start(bf16[8,48,1024]{2,1,0:T(8,128)(2,1)} %copy-done.4), channel_id=1, source_target_pairs={{0,12},{4,8},{8,4},{12,0},{1,13},{5,9},{9,5},{13,1},{2,14},{6,10},... | collective-permute-start | bytes 2359304 | tf_op jit(solution)/shard_map/ppermute | solution.py:28
  15.3 0.1 collective-permute-start.10
  15.3 2.3 %constant_dynamic-slice_fusion.2 = bf16[8,64,1024]{2,1,0:T(8,128)(2,1)} fusion(bf16[8,256,1024]{2,1,0:T(8,128)(2,1)} %refs_4_.1, s32[]{:T(128)S(6)} %select_n.43), kind=kLoop, calls=%fused_computation.5 | loop fusion | bytes 2097156 | tf_op jit(solution)/shard_map/dynamic_slice | solution.py:359
  17.6 0.1 collective-permute-start.9
  17.7 32.9 %collective-permute-done.3.refs_3_ = bf16[8,48,1024]{2,1,0:T(8,128)(2,1)S(1)} collective-permute-done((bf16[8,48,1024]{2,1,0:T(8,128)(2,1)}, bf16[8,48,1024]{2,1,0:T(8,128)(2,1)S(1)}, u32[]{:S(2)}, u32[]{:S(2)}) %collective-permute-start.3) | collective-permute-done | bytes 786464 | tf_op jit(solution)/shard_map/ppermute | solution.py:28
  50.6 6.4 %gram.1 = f32[32,32]{1,0:T(8,128)S(1)} custom-call(s32[1]{0:T(128)} %bitcast.1.me_ref, f32[8,256,1024]{2,1,0:T(8,128)} %params_ref.11, bf16[8,64,1024]{2,1,0:T(8,128)(2,1)S(1)} %collective-permute-done.1.refs_1_, bf16[8,64,1024]{2,1,0:T(8,128)(2,1)S(1)} %collective-permute-done.2.refs_2_, bf16[8,48,1024]{2,1,0:T(8,128)(2,1)S(1)} %collective-permute-done.3.refs_3_, ...), custom_call_target="tpu_custom_call" | custom-call | flops 1024 | bytes 1024 | tf_op jit(solution)/shard_map/gram/pallas_call | solution.py:149
  57.0 4.2 %collective-permute-start.6 = (f32[32,32]{1,0:T(8,128)S(1)}, f32[32,32]{1,0:T(8,128)S(1)}, u32[]{:S(2)}, u32[]{:S(2)}) collective-permute-start(f32[32,32]{1,0:T(8,128)S(1)} %gram.1), channel_id=1, source_target_pairs={{0,3},{1,2},{2,1},{3,0},{4,7},{5,6},{6,5},{7,4},{8,11},{9,10},{10,... | collective-permute-start | bytes 12296 | tf_op jit(solution)/shard_map/ppermute | solution.py:28
  61.2 0.6 collective-permute-start.4
  61.8 1.1 collective-permute-done.6
  62.9 2.9 %collective-permute-done.5 = f32[32,32]{1,0:T(8,128)S(1)} collective-permute-done((f32[32,32]{1,0:T(8,128)S(1)}, f32[32,32]{1,0:T(8,128)S(1)}, u32[]{:S(2)}, u32[]{:S(2)}) %collective-permute-start.5) | collective-permute-done | bytes 4128 | tf_op jit(solution)/shard_map/ppermute | solution.py:28
  65.9 0.1 collective-permute-start.7
  65.9 1.2 collective-permute-done.7
  67.1 1.9 %constant_dynamic-slice_fusion.1 = bf16[8,32,1024]{2,1,0:T(8,128)(2,1)} fusion(bf16[8,256,1024]{2,1,0:T(8,128)(2,1)} %refs_4_.1, s32[]{:T(128)S(6)} %select_n.41), kind=kLoop, calls=%fused_computation.4 | loop fusion | bytes 1048580 | tf_op jit(solution)/shard_map/dynamic_slice | solution.py:359
  69.0 1.3 collective-permute-start.12
  70.3 0.5 collective-permute-start.8
  70.8 1.1 constant_dynamic-slice_fusion
  71.9 1.3 collective-permute-start.11
  73.1 12.1 %collective-permute-done.8 = f32[32,32]{1,0:T(8,128)S(1)} collective-permute-done((f32[32,32]{1,0:T(8,128)S(1)}, f32[32,32]{1,0:T(8,128)S(1)}, u32[]{:S(2)}, u32[]{:S(2)}) %collective-permute-start.8) | collective-permute-done | bytes 4128 | tf_op jit(solution)/shard_map/ppermute | solution.py:28
  85.3 5.8 %mix.2 = (bf16[8,64,1024]{2,1,0:T(8,128)(2,1)S(1)}, bf16[8,32,1024]{2,1,0:T(8,128)(2,1)S(1)}, bf16[8,32,1024]{2,1,0:T(8,128)(2,1)S(1)}, bf16[8,32,1024]{2,1,0:T(8,128)(2,1)}, f32[32,32]{1,0:T(8,128)}) custom-call(s32[1]{0:T(128)} %bitcast.1.me_ref, f32[32,32]{1,0:T(8,128)S(1)} %add.60.gram_ref, f32[8,256,1024]{2,1,0:T(8,128)} %params_ref.11, ...), custom_call_target="tpu_custom_call" | custom-call | flops 1024 | bytes 1024 | tf_op jit(solution)/shard_map/mix/pallas_call | solution.py:253
  91.1 1.5 %collective-permute-start.18 = (bf16[8,32,1024]{2,1,0:T(8,128)(2,1)S(1)}, bf16[8,32,1024]{2,1,0:T(8,128)(2,1)S(1)}, u32[]{:S(2)}, u32[]{:S(2)}) collective-permute-start(bf16[8,32,1024]{2,1,0:T(8,128)(2,1)S(1)} %get-tuple-element.76), channel_id=1, source_target_pairs={{0,8},{4,12},{8,0},{12,4},{1,9},{5,13},{9,1},{13,5},{2,10},{6,14},... | collective-permute-start | bytes 1572872 | tf_op jit(solution)/shard_map/ppermute | solution.py:28
  92.6 0.3 collective-permute-start.19
  92.9 3.0 %collective-permute-done.11.refs_7_ = bf16[8,32,1024]{2,1,0:T(8,128)(2,1)S(1)} collective-permute-done((bf16[8,32,1024]{2,1,0:T(8,128)(2,1)S(1)}, bf16[8,32,1024]{2,1,0:T(8,128)(2,1)S(1)}, u32[]{:S(2)}, u32[]{:S(2)}) %collective-permute-start.11) | collective-permute-done | bytes 524320 | tf_op jit(solution)/shard_map/ppermute | solution.py:28
  95.9 1.2 copy-done.1
  97.1 5.8 %mix.3 = (bf16[8,64,1024]{2,1,0:T(8,128)(2,1)S(1)}, bf16[8,32,1024]{2,1,0:T(8,128)(2,1)}, bf16[8,32,1024]{2,1,0:T(8,128)(2,1)}, bf16[8,16,1024]{2,1,0:T(8,128)(2...) custom-call(s32[1]{0:T(128)} %bitcast.1.me_ref, ...), custom_call_target="tpu_custom_call", output_to_operand_aliasing={{0}: (10, {})} | custom-call | flops 1024 | bytes 1024 | tf_op jit(solution)/shard_map/mix/pallas_call | solution.py:253
  102.9 1.0 copy-done.2
  103.9 0.4 collective-permute-start.16
  104.3 1.8 %collective-permute-start.17 = (bf16[8,32,1024]{2,1,0:T(8,128)(2,1)}, bf16[8,32,1024]{2,1,0:T(8,128)(2,1)S(1)}, u32[]{:S(2)}, u32[]{:S(2)}) collective-permute-start(bf16[8,32,1024]{2,1,0:T(8,128)(2,1)} %get-tuple-element.75), channel_id=1, source_target_pairs={{0,8},{4,12},{8,0},{12,4},{1,9},{5,13},{9,1},{13,5},{2,10},{6,14},... | collective-permute-start | bytes 1572872 | tf_op jit(solution)/shard_map/ppermute | solution.py:28
  106.1 1.6 %collective-permute-done.18.refs_0_ = bf16[8,32,1024]{2,1,0:T(8,128)(2,1)S(1)} collective-permute-done((bf16[8,32,1024]{2,1,0:T(8,128)(2,1)S(1)}, bf16[8,32,1024]{2,1,0:T(8,128)(2,1)S(1)}, u32[]{:S(2)}, u32[]{:S(2)}) %collective-permute-start.18) | collective-permute-done | bytes 524320 | tf_op jit(solution)/shard_map/ppermute | solution.py:28
  107.7 1.2 collective-permute-start.14
  108.9 0.1 pad_add_fusion.1.row_ref
  109.0 0.1 pad_add_fusion.row_ref
  109.1 1.2 copy-done.3
  110.3 7.1 %adamw.6 = (f32[8,256,1024]{2,1,0:T(8,128)}, f32[8,256,1024]{2,1,0:T(8,128)}, f32[8,256,1024]{2,1,0:T(8,128)}, f32[8,256,1024]{2,1,0:T(8,128)}, f32[8,256,1024]{2,1,0:T(8,128)}) custom-call(s32[1]{0:T(128)} %bitcast.8.row_ref, f32[8,256,1024]{2,1,0:T(8,128)} %params_ref.11, f32[8,256,1024]{2,1,0:T(8,128)} %first_ref.11, f32[8,256,1024]{2,1,0:T(8,128)} %second_ref.11, ...), custom_call_target="tpu_custom_call" | custom-call | flops 1024 | bytes 1048576 | tf_op jit(solution)/shard_map/adamw/pallas_call | solution.py:326
  117.4 4.4 %adamw.7 = (f32[8,256,1024]{2,1,0:T(8,128)}, f32[8,256,1024]{2,1,0:T(8,128)}, f32[8,256,1024]{2,1,0:T(8,128)}, f32[8,256,1024]{2,1,0:T(8,128)}, f32[8,256,1024]{2,1,0:T(8,128)}) custom-call(s32[1]{0:T(128)} %bitcast.7.row_ref, f32[8,256,1024]{2,1,0:T(8,128)} %params_ref.11, ...), custom_call_target="tpu_custom_call", output_to_operand_aliasing={{0}: (5, {}), {1}: (6, {}), {2}: (7, {}), {3}: (8, {}), {4}... | custom-call | flops 1024 | bytes 1048576 | tf_op jit(solution)/shard_map/adamw/pallas_call | solution.py:326
  121.8 7.7 %adamw.8 = (f32[8,256,1024]{2,1,0:T(8,128)}, f32[8,256,1024]{2,1,0:T(8,128)}, f32[8,256,1024]{2,1,0:T(8,128)}, f32[8,256,1024]{2,1,0:T(8,128)}, f32[8,256,1024]{2,1,0:T(8,128)}) custom-call(s32[2]{0:T(128)S(1)} %pad_add_fusion.1.row_ref, f32[8,256,1024]{2,1,0:T(8,128)} %params_ref.11, ...), custom_call_target="tpu_custom_call", output_to_operand_aliasing={{0}: (6, {}), {1}: (7, {}), {2}: (8, {}), {3}: (9, {}), {4}... | custom-call | flops 1024 | bytes 1048576 | tf_op jit(solution)/shard_map/adamw/pallas_call | solution.py:326
  129.5 0.7 collective-permute-done.17.refs_1_
  130.2 7.7 %adamw.9 = (f32[8,256,1024]{2,1,0:T(8,128)}, f32[8,256,1024]{2,1,0:T(8,128)}, f32[8,256,1024]{2,1,0:T(8,128)}, f32[8,256,1024]{2,1,0:T(8,128)}, f32[8,256,1024]{2,1,0:T(8,128)}) custom-call(s32[2]{0:T(128)S(1)} %pad_add_fusion.row_ref, f32[8,256,1024]{2,1,0:T(8,128)} %params_ref.11, ...), custom_call_target="tpu_custom_call", output_to_operand_aliasing={{0}: (6, {}), {1}: (7, {}), {2}: (8, {}), {3}: (9, {}), {4}... | custom-call | flops 1024 | bytes 1048576 | tf_op jit(solution)/shard_map/adamw/pallas_call | solution.py:326
  137.9 2.8 %adamw.10 = (f32[8,256,1024]{2,1,0:T(8,128)}, f32[8,256,1024]{2,1,0:T(8,128)}, f32[8,256,1024]{2,1,0:T(8,128)}, f32[8,256,1024]{2,1,0:T(8,128)}, f32[8,256,1024]{2,1,0:T(8,128)}) custom-call(s32[1]{0:T(128)} %bitcast.2.row_ref, f32[8,256,1024]{2,1,0:T(8,128)} %params_ref.11, ...), custom_call_target="tpu_custom_call", output_to_operand_aliasing={{0}: (5, {}), {1}: (6, {}), {2}: (7, {}), {3}: (8, {}), {4}... | custom-call | flops 1024 | bytes 1048576 | tf_op jit(solution)/shard_map/adamw/pallas_call | solution.py:326
  140.7 0.2 collective-permute-done.14.refs_0_
  140.9 2.7 %adamw.11 = (f32[8,256,1024]{2,1,0:T(8,128)}, f32[8,256,1024]{2,1,0:T(8,128)}, f32[8,256,1024]{2,1,0:T(8,128)}, f32[8,256,1024]{2,1,0:T(8,128)}, f32[8,256,1024]{2,1,0:T(8,128)}) custom-call(s32[1]{0:T(128)} %bitcast.row_ref, f32[8,256,1024]{2,1,0:T(8,128)} %params_ref.11, ...), custom_call_target="tpu_custom_call", output_to_operand_aliasing={{0}: (5, {}), {1}: (6, {}), {2}: (7, {}), {3}: (8, {}), {4}... | custom-call | flops 1024 | bytes 1048576 | tf_op jit(solution)/shard_map/adamw/pallas_call | solution.py:326
  (23 shorter events, 0.1 us)
Async XLA Ops:
  1.7 9.3 %collective-permute-start = (bf16[8,16,1024]{2,1,0:T(8,128)(2,1)S(1)}, bf16[8,16,1024]{2,1,0:T(8,128)(2,1)S(1)}, u32[]{:S(2)}, u32[]{:S(2)}) collective-permute-start(bf16[8,16,1024]{2,1,0:T(8,128)(2,1)S(1)} %dynamic-slice_convert_fusion.1), channel_id=1, source_target_pairs={{0,12},{4,8},{8,4},{12,0},{1,13},{5,9},{9,5},{13,1},{2,14},{6,10},... | collective-permute-start | bytes 786440 | tf_op jit(solution)/shard_map/ppermute | solution.py:28
  7.2 0.9 copy-start.4
  8.1 42.5 %collective-permute-start.2 = (bf16[8,64,1024]{2,1,0:T(8,128)(2,1)}, bf16[8,64,1024]{2,1,0:T(8,128)(2,1)S(1)}, u32[]{:S(2)}, u32[]{:S(2)}) collective-permute-start(bf16[8,64,1024]{2,1,0:T(8,128)(2,1)} %get-tuple-element.59), channel_id=1, source_target_pairs={{0,8},{4,12},{8,0},{12,4},{1,9},{5,13},{9,1},{13,5},{2,10},{6,14},... | collective-permute-start | bytes 3145736 | tf_op jit(solution)/shard_map/ppermute | solution.py:28
  12.8 37.9 %collective-permute-start.1 = (bf16[8,64,1024]{2,1,0:T(8,128)(2,1)S(1)}, bf16[8,64,1024]{2,1,0:T(8,128)(2,1)S(1)}, u32[]{:S(2)}, u32[]{:S(2)}) collective-permute-start(bf16[8,64,1024]{2,1,0:T(8,128)(2,1)S(1)} %dynamic-slice_convert_fusion), channel_id=1, source_target_pairs={{0,4},{4,0},{8,12},{12,8},{1,5},{5,1},{9,13},{13,9},{2,6},{6,2},{1... | collective-permute-start | bytes 3145736 | tf_op jit(solution)/shard_map/ppermute | solution.py:28
  12.9 37.7 %collective-permute-start.3 = (bf16[8,48,1024]{2,1,0:T(8,128)(2,1)}, bf16[8,48,1024]{2,1,0:T(8,128)(2,1)S(1)}, u32[]{:S(2)}, u32[]{:S(2)}) collective-permute-start(bf16[8,48,1024]{2,1,0:T(8,128)(2,1)} %copy-done.4), channel_id=1, source_target_pairs={{0,12},{4,8},{8,4},{12,0},{1,13},{5,9},{9,5},{13,1},{2,14},{6,10},... | collective-permute-start | bytes 2359304 | tf_op jit(solution)/shard_map/ppermute | solution.py:28
  15.3 70.0 %collective-permute-start.10 = (bf16[8,64,1024]{2,1,0:T(8,128)(2,1)}, bf16[8,64,1024]{2,1,0:T(8,128)(2,1)}, u32[]{:S(2)}, u32[]{:S(2)}) collective-permute-start(bf16[8,64,1024]{2,1,0:T(8,128)(2,1)} %constant_dynamic-slice_fusion.3), channel_id=1, source_target_pairs={{0,8},{4,12},{8,0},{12,4},{1,9},{5,13},{9,1},{13,5},{2,10},{6,14},... | collective-permute-start | bytes 3145736 | tf_op jit(solution)/shard_map/ppermute | solution.py:28
  17.6 67.7 %collective-permute-start.9 = (bf16[8,64,1024]{2,1,0:T(8,128)(2,1)}, bf16[8,64,1024]{2,1,0:T(8,128)(2,1)}, u32[]{:S(2)}, u32[]{:S(2)}) collective-permute-start(bf16[8,64,1024]{2,1,0:T(8,128)(2,1)} %constant_dynamic-slice_fusion.2), channel_id=1, source_target_pairs={{0,4},{4,0},{8,12},{12,8},{1,5},{5,1},{9,13},{13,9},{2,6},{6,2},{1... | collective-permute-start | bytes 3145736 | tf_op jit(solution)/shard_map/ppermute | solution.py:28
  50.6 34.7 %copy-start = (bf16[8,64,1024]{2,1,0:T(8,128)(2,1)}, bf16[8,64,1024]{2,1,0:T(8,128)(2,1)S(1)}, u32[]{:S(2)}) copy-start(bf16[8,64,1024]{2,1,0:T(8,128)(2,1)S(1)} %collective-permute-done.2.refs_2_) | copy-start | bytes 3145732
  57.0 5.9 %collective-permute-start.6 = (f32[32,32]{1,0:T(8,128)S(1)}, f32[32,32]{1,0:T(8,128)S(1)}, u32[]{:S(2)}, u32[]{:S(2)}) collective-permute-start(f32[32,32]{1,0:T(8,128)S(1)} %gram.1), channel_id=1, source_target_pairs={{0,3},{1,2},{2,1},{3,0},{4,7},{5,6},{6,5},{7,4},{8,11},{9,10},{10,... | collective-permute-start | bytes 12296 | tf_op jit(solution)/shard_map/ppermute | solution.py:28
  61.2 4.6 %collective-permute-start.5 = (f32[32,32]{1,0:T(8,128)S(1)}, f32[32,32]{1,0:T(8,128)S(1)}, u32[]{:S(2)}, u32[]{:S(2)}) collective-permute-start(f32[32,32]{1,0:T(8,128)S(1)} %gram.1), channel_id=1, source_target_pairs={{0,2},{1,3},{2,0},{3,1},{4,6},{5,7},{6,4},{7,5},{8,10},{9,11},{10,... | collective-permute-start | bytes 12296 | tf_op jit(solution)/shard_map/ppermute | solution.py:28
  61.2 4.6 %collective-permute-start.4 = (f32[32,32]{1,0:T(8,128)S(1)}, f32[32,32]{1,0:T(8,128)S(1)}, u32[]{:S(2)}, u32[]{:S(2)}) collective-permute-start(f32[32,32]{1,0:T(8,128)S(1)} %gram.1), channel_id=1, source_target_pairs={{0,1},{1,0},{2,3},{3,2},{4,5},{5,4},{6,7},{7,6},{8,9},{9,8},{10,11... | collective-permute-start | bytes 12296 | tf_op jit(solution)/shard_map/ppermute | solution.py:28
  65.9 1.2 collective-permute-start.7
  69.0 16.3 %collective-permute-start.12 = (bf16[8,32,1024]{2,1,0:T(8,128)(2,1)}, bf16[8,32,1024]{2,1,0:T(8,128)(2,1)}, u32[]{:S(2)}, u32[]{:S(2)}) collective-permute-start(bf16[8,32,1024]{2,1,0:T(8,128)(2,1)} %constant_dynamic-slice_fusion.1), channel_id=1, source_target_pairs={{0,12},{4,8},{8,4},{12,0},{1,13},{5,9},{9,5},{13,1},{2,14},{6,10},... | collective-permute-start | bytes 1572872 | tf_op jit(solution)/shard_map/ppermute | solution.py:28
  70.3 15.0 %collective-permute-start.8 = (f32[32,32]{1,0:T(8,128)S(1)}, f32[32,32]{1,0:T(8,128)S(1)}, u32[]{:S(2)}, u32[]{:S(2)}) collective-permute-start(f32[32,32]{1,0:T(8,128)S(1)} %add.59), channel_id=1, source_target_pairs={{0,8},{4,12},{8,0},{12,4},{1,9},{5,13},{9,1},{13,5},{2,10},{6,14},... | collective-permute-start | bytes 12296 | tf_op jit(solution)/shard_map/ppermute | solution.py:28
  71.9 24.1 %collective-permute-start.11 = (bf16[8,32,1024]{2,1,0:T(8,128)(2,1)S(1)}, bf16[8,32,1024]{2,1,0:T(8,128)(2,1)S(1)}, u32[]{:S(2)}, u32[]{:S(2)}) collective-permute-start(bf16[8,32,1024]{2,1,0:T(8,128)(2,1)S(1)} %constant_dynamic-slice_fusion), channel_id=1, source_target_pairs={{0,12},{4,8},{8,4},{12,0},{1,13},{5,9},{9,5},{13,1},{2,14},{6,10},... | collective-permute-start | bytes 1572872 | tf_op jit(solution)/shard_map/ppermute | solution.py:28
  91.1 13.2 %collective-permute-start.13 = (bf16[8,32,1024]{2,1,0:T(8,128)(2,1)S(1)}, bf16[8,32,1024]{2,1,0:T(8,128)(2,1)S(1)}, u32[]{:S(2)}, u32[]{:S(2)}) collective-permute-start(bf16[8,32,1024]{2,1,0:T(8,128)(2,1)S(1)} %get-tuple-element.69), channel_id=1, source_target_pairs={{0,4},{4,0},{8,12},{12,8},{1,5},{5,1},{9,13},{13,9},{2,6},{6,2},{1... | collective-permute-start | bytes 1572872 | tf_op jit(solution)/shard_map/ppermute | solution.py:28
  91.1 16.7 %collective-permute-start.18 = (bf16[8,32,1024]{2,1,0:T(8,128)(2,1)S(1)}, bf16[8,32,1024]{2,1,0:T(8,128)(2,1)S(1)}, u32[]{:S(2)}, u32[]{:S(2)}) collective-permute-start(bf16[8,32,1024]{2,1,0:T(8,128)(2,1)S(1)} %get-tuple-element.76), channel_id=1, source_target_pairs={{0,8},{4,12},{8,0},{12,4},{1,9},{5,13},{9,1},{13,5},{2,10},{6,14},... | collective-permute-start | bytes 1572872 | tf_op jit(solution)/shard_map/ppermute | solution.py:28
  92.6 29.2 %collective-permute-start.19 = (bf16[8,32,1024]{2,1,0:T(8,128)(2,1)}, bf16[8,32,1024]{2,1,0:T(8,128)(2,1)S(1)}, u32[]{:S(2)}, u32[]{:S(2)}) collective-permute-start(bf16[8,32,1024]{2,1,0:T(8,128)(2,1)} %get-tuple-element.77), channel_id=1, source_target_pairs={{0,12},{4,8},{8,4},{12,0},{1,13},{5,9},{9,5},{13,1},{2,14},{6,10},... | collective-permute-start | bytes 1572872 | tf_op jit(solution)/shard_map/ppermute | solution.py:28
  95.9 1.2 copy-start.1
  102.9 1.0 copy-start.2
  103.9 25.6 %collective-permute-start.16 = (bf16[8,32,1024]{2,1,0:T(8,128)(2,1)}, bf16[8,32,1024]{2,1,0:T(8,128)(2,1)S(1)}, u32[]{:S(2)}, u32[]{:S(2)}) collective-permute-start(bf16[8,32,1024]{2,1,0:T(8,128)(2,1)} %get-tuple-element.73), channel_id=1, source_target_pairs={{0,4},{4,0},{8,12},{12,8},{1,5},{5,1},{9,13},{13,9},{2,6},{6,2},{1... | collective-permute-start | bytes 1572872 | tf_op jit(solution)/shard_map/ppermute | solution.py:28
  104.3 25.9 %collective-permute-start.17 = (bf16[8,32,1024]{2,1,0:T(8,128)(2,1)}, bf16[8,32,1024]{2,1,0:T(8,128)(2,1)S(1)}, u32[]{:S(2)}, u32[]{:S(2)}) collective-permute-start(bf16[8,32,1024]{2,1,0:T(8,128)(2,1)} %get-tuple-element.75), channel_id=1, source_target_pairs={{0,8},{4,12},{8,0},{12,4},{1,9},{5,13},{9,1},{13,5},{2,10},{6,14},... | collective-permute-start | bytes 1572872 | tf_op jit(solution)/shard_map/ppermute | solution.py:28
  106.1 31.8 %collective-permute-start.15 = (bf16[8,16,1024]{2,1,0:T(8,128)(2,1)}, bf16[8,16,1024]{2,1,0:T(8,128)(2,1)S(1)}, u32[]{:S(2)}, u32[]{:S(2)}) collective-permute-start(bf16[8,16,1024]{2,1,0:T(8,128)(2,1)} %get-tuple-element.72), channel_id=1, source_target_pairs={{0,12},{4,8},{8,4},{12,0},{1,13},{5,9},{9,5},{13,1},{2,14},{6,10},... | collective-permute-start | bytes 786440 | tf_op jit(solution)/shard_map/ppermute | solution.py:28
  107.7 33.1 %collective-permute-start.14 = (bf16[8,16,1024]{2,1,0:T(8,128)(2,1)}, bf16[8,16,1024]{2,1,0:T(8,128)(2,1)S(1)}, u32[]{:S(2)}, u32[]{:S(2)}) collective-permute-start(bf16[8,16,1024]{2,1,0:T(8,128)(2,1)} %get-tuple-element.70), channel_id=1, source_target_pairs={{0,12},{4,8},{8,4},{12,0},{1,13},{5,9},{9,5},{13,1},{2,14},{6,10},... | collective-permute-start | bytes 786440 | tf_op jit(solution)/shard_map/ppermute | solution.py:28
  109.0 1.2 copy-start.3

commit v5 on v4

--- a/solution.py
+++ b/solution.py
@@ -424,7 +424,7 @@
             back.append((flip, part * rows_part + first, swap(piece, "member", flip)))
     groups = [[(0, 0, kept[0])]]
     for idx, arrived in enumerate(back):
-        if n_part > 1 and idx in (2, 4) and arrived[2].shape == back[idx - 1][2].shape:
+        if n_part > 1 and idx in (1, 3) and arrived[2].shape == back[idx - 1][2].shape:
             groups[-1].append(arrived)
         else:
             groups.append([arrived])

time: 144 us -> 144 us (level)
  transfers between devices with their start and end apart: 20 -> 20, of which waited for: 9 -> 7; matrix products, arithmetic and copies ran while one was open for 7% -> 7% of each run, Pallas kernels for 35% -> 35%
where the time goes in v5:
time: 144 us
  waiting for transfers between devices  54.5 us (38%)
  Pallas kernels  53.4 us (37%)
  starting transfers between devices  20.2 us (14%)
  local copies, waits for them, and re-layouts  14.6 us (10%)
    ppermute x20, waiting for transfers between devices, swap(): lax.ppermute(x, axis, [(i, i ^ flip) for i in range(lax.axis_size(axis))])  54.5 us
    pallas_call x6, Pallas kernels, adamw(): pl.pallas_call(functools.partial(adamw_kernel, len(pieces)), out_shape=[s...  32.4 us
    ppermute x20, starting transfers between devices, swap(): lax.ppermute(x, axis, [(i, i ^ flip) for i in range(lax.axis_size(axis))])  20.2 us
    pallas_call x2, Pallas kernels, mix(): pl.pallas_call(functools.partial(mix_kernel, n_member, len(head), cuts, e...  11.5 us
    dynamic_slice x4, local copies, waits for them, and re-layouts, rows_of(): lax.dynamic_slice(array, (0, start, 0), (members_dev, rows, feature_width))  7.47 us
    pallas_call x1, Pallas kernels, local_gram(): pl.pallas_call(functools.partial(gram_kernel, n_member), out_shape=jax.Sh...  6.4 us
    unnamed x10, local copies, waits for them, and re-layouts  4.3 us
    pallas_call x1, Pallas kernels, pack_rows(): pl.pallas_call(pack_kernel, out_shape=[jax.ShapeDtypeStruct((members_dev,...  3.06 us
  transfers between devices with their start and end apart: 20, of which 7 were waited for; matrix products, arithmetic and copies ran while one was open for 7% of the time, Pallas kernels for 35%

profile of v5, /device:TPU:0, one launch (start us, length us, event | category | flops | bytes accessed | tf_op | source)
XLA Modules:
  0.0 143.6 jit_solution(15331494699666391529)
XLA Ops:
  0.6 1.1 dynamic-slice_convert_fusion.1
  1.7 2.4 %collective-permute-start = (bf16[8,16,1024]{2,1,0:T(8,128)(2,1)S(1)}, bf16[8,16,1024]{2,1,0:T(8,128)(2,1)S(1)}, u32[]{:S(2)}, u32[]{:S(2)}) collective-permute-start(bf16[8,16,1024]{2,1,0:T(8,128)(2,1)S(1)} %dynamic-slice_convert_fusion.1), channel_id=1, source_target_pairs={{0,12},{4,8},{8,4},{12,0},{1,13},{5,9},{9,5},{13,1},{2,14},{6,10},... | collective-permute-start | bytes 786440 | tf_op jit(solution)/shard_map/ppermute | solution.py:28
  4.2 3.1 %pack.1 = (bf16[8,64,1024]{2,1,0:T(8,128)(2,1)}, bf16[8,48,1024]{2,1,0:T(8,128)(2,1)S(1)}) custom-call(s32[1]{0:T(128)} %bitcast.1.me_ref, f32[8,256,1024]{2,1,0:T(8,128)} %params_ref.11, f32[8,256,1024]{2,1,0:T(8,128)} %params_ref.11), custom_call_target="tpu_custom_call" | custom-call | flops 1024 | bytes 1024 | tf_op jit(solution)/shard_map/pack/pallas_call | solution.py:89
  7.2 0.9 copy-done.4
  8.1 0.6 collective-permute-start.2
  8.7 2.3 %constant_dynamic-slice_fusion.3 = bf16[8,64,1024]{2,1,0:T(8,128)(2,1)} fusion(bf16[8,256,1024]{2,1,0:T(8,128)(2,1)} %refs_4_.1, s32[]{:T(128)S(6)} %select_n.42), kind=kLoop, calls=%fused_computation.6 | loop fusion | bytes 2097156 | tf_op jit(solution)/shard_map/dynamic_slice | solution.py:359
  11.0 1.7 %dynamic-slice_convert_fusion = bf16[8,64,1024]{2,1,0:T(8,128)(2,1)S(1)} fusion(f32[8,256,1024]{2,1,0:T(8,128)} %params_ref.11, s32[]{:T(128)S(6)} %select_n.43), kind=kLoop, calls=%fused_computation | loop fusion | bytes 2097156 | tf_op jit(solution)/shard_map/convert_element_type | solution.py:374
  12.8 0.1 collective-permute-start.1
  12.9 2.4 %collective-permute-start.3 = (bf16[8,48,1024]{2,1,0:T(8,128)(2,1)}, bf16[8,48,1024]{2,1,0:T(8,128)(2,1)S(1)}, u32[]{:S(2)}, u32[]{:S(2)}) collective-permute-start(bf16[8,48,1024]{2,1,0:T(8,128)(2,1)} %copy-done.4), channel_id=1, source_target_pairs={{0,12},{4,8},{8,4},{12,0},{1,13},{5,9},{9,5},{13,1},{2,14},{6,10},... | collective-permute-start | bytes 2359304 | tf_op jit(solution)/shard_map/ppermute | solution.py:28
  15.3 0.1 collective-permute-start.10
  15.3 2.3 %constant_dynamic-slice_fusion.2 = bf16[8,64,1024]{2,1,0:T(8,128)(2,1)} fusion(bf16[8,256,1024]{2,1,0:T(8,128)(2,1)} %refs_4_.1, s32[]{:T(128)S(6)} %select_n.43), kind=kLoop, calls=%fused_computation.5 | loop fusion | bytes 2097156 | tf_op jit(solution)/shard_map/dynamic_slice | solution.py:359
  17.6 0.1 collective-permute-start.9
  17.7 32.9 %collective-permute-done.3.refs_3_ = bf16[8,48,1024]{2,1,0:T(8,128)(2,1)S(1)} collective-permute-done((bf16[8,48,1024]{2,1,0:T(8,128)(2,1)}, bf16[8,48,1024]{2,1,0:T(8,128)(2,1)S(1)}, u32[]{:S(2)}, u32[]{:S(2)}) %collective-permute-start.3) | collective-permute-done | bytes 786464 | tf_op jit(solution)/shard_map/ppermute | solution.py:28
  50.6 6.4 %gram.1 = f32[32,32]{1,0:T(8,128)S(1)} custom-call(s32[1]{0:T(128)} %bitcast.1.me_ref, f32[8,256,1024]{2,1,0:T(8,128)} %params_ref.11, bf16[8,64,1024]{2,1,0:T(8,128)(2,1)S(1)} %collective-permute-done.1.refs_1_, bf16[8,64,1024]{2,1,0:T(8,128)(2,1)S(1)} %collective-permute-done.2.refs_2_, bf16[8,48,1024]{2,1,0:T(8,128)(2,1)S(1)} %collective-permute-done.3.refs_3_, ...), custom_call_target="tpu_custom_call" | custom-call | flops 1024 | bytes 1024 | tf_op jit(solution)/shard_map/gram/pallas_call | solution.py:149
  57.0 4.2 %collective-permute-start.6 = (f32[32,32]{1,0:T(8,128)S(1)}, f32[32,32]{1,0:T(8,128)S(1)}, u32[]{:S(2)}, u32[]{:S(2)}) collective-permute-start(f32[32,32]{1,0:T(8,128)S(1)} %gram.1), channel_id=1, source_target_pairs={{0,3},{1,2},{2,1},{3,0},{4,7},{5,6},{6,5},{7,4},{8,11},{9,10},{10,... | collective-permute-start | bytes 12296 | tf_op jit(solution)/shard_map/ppermute | solution.py:28
  61.2 0.6 collective-permute-start.4
  61.8 1.1 collective-permute-done.6
  62.9 2.9 %collective-permute-done.5 = f32[32,32]{1,0:T(8,128)S(1)} collective-permute-done((f32[32,32]{1,0:T(8,128)S(1)}, f32[32,32]{1,0:T(8,128)S(1)}, u32[]{:S(2)}, u32[]{:S(2)}) %collective-permute-start.5) | collective-permute-done | bytes 4128 | tf_op jit(solution)/shard_map/ppermute | solution.py:28
  65.9 0.1 collective-permute-start.7
  65.9 1.2 collective-permute-done.7
  67.1 1.9 %constant_dynamic-slice_fusion.1 = bf16[8,32,1024]{2,1,0:T(8,128)(2,1)} fusion(bf16[8,256,1024]{2,1,0:T(8,128)(2,1)} %refs_4_.1, s32[]{:T(128)S(6)} %select_n.41), kind=kLoop, calls=%fused_computation.4 | loop fusion | bytes 1048580 | tf_op jit(solution)/shard_map/dynamic_slice | solution.py:359
  69.0 1.3 collective-permute-start.12
  70.3 0.5 collective-permute-start.8
  70.8 1.1 constant_dynamic-slice_fusion
  71.9 1.3 collective-permute-start.11
  73.1 12.1 %collective-permute-done.8 = f32[32,32]{1,0:T(8,128)S(1)} collective-permute-done((f32[32,32]{1,0:T(8,128)S(1)}, f32[32,32]{1,0:T(8,128)S(1)}, u32[]{:S(2)}, u32[]{:S(2)}) %collective-permute-start.8) | collective-permute-done | bytes 4128 | tf_op jit(solution)/shard_map/ppermute | solution.py:28
  85.3 5.8 %mix.2 = (bf16[8,64,1024]{2,1,0:T(8,128)(2,1)S(1)}, bf16[8,32,1024]{2,1,0:T(8,128)(2,1)S(1)}, bf16[8,32,1024]{2,1,0:T(8,128)(2,1)S(1)}, bf16[8,32,1024]{2,1,0:T(8,128)(2,1)}, f32[32,32]{1,0:T(8,128)}) custom-call(s32[1]{0:T(128)} %bitcast.1.me_ref, f32[32,32]{1,0:T(8,128)S(1)} %add.60.gram_ref, f32[8,256,1024]{2,1,0:T(8,128)} %params_ref.11, ...), custom_call_target="tpu_custom_call" | custom-call | flops 1024 | bytes 1024 | tf_op jit(solution)/shard_map/mix/pallas_call | solution.py:253
  91.1 1.5 %collective-permute-start.19 = (bf16[8,32,1024]{2,1,0:T(8,128)(2,1)S(1)}, bf16[8,32,1024]{2,1,0:T(8,128)(2,1)S(1)}, u32[]{:S(2)}, u32[]{:S(2)}) collective-permute-start(bf16[8,32,1024]{2,1,0:T(8,128)(2,1)S(1)} %get-tuple-element.77), channel_id=1, source_target_pairs={{0,8},{4,12},{8,0},{12,4},{1,9},{5,13},{9,1},{13,5},{2,10},{6,14},... | collective-permute-start | bytes 1572872 | tf_op jit(solution)/shard_map/ppermute | solution.py:28
  92.6 3.3 %collective-permute-done.11.refs_7_ = bf16[8,32,1024]{2,1,0:T(8,128)(2,1)S(1)} collective-permute-done((bf16[8,32,1024]{2,1,0:T(8,128)(2,1)S(1)}, bf16[8,32,1024]{2,1,0:T(8,128)(2,1)S(1)}, u32[]{:S(2)}, u32[]{:S(2)}) %collective-permute-start.11) | collective-permute-done | bytes 524320 | tf_op jit(solution)/shard_map/ppermute | solution.py:28
  95.9 1.2 copy-done.1
  97.1 5.8 %mix.3 = (bf16[8,64,1024]{2,1,0:T(8,128)(2,1)S(1)}, bf16[8,32,1024]{2,1,0:T(8,128)(2,1)}, bf16[8,32,1024]{2,1,0:T(8,128)(2,1)}, bf16[8,16,1024]{2,1,0:T(8,128)(2...) custom-call(s32[1]{0:T(128)} %bitcast.1.me_ref, ...), custom_call_target="tpu_custom_call", output_to_operand_aliasing={{0}: (10, {})} | custom-call | flops 1024 | bytes 1024 | tf_op jit(solution)/shard_map/mix/pallas_call | solution.py:253
  102.9 0.0 copy-start.2
  102.9 1.0 copy-done.2
  103.9 0.4 collective-permute-start.18
  104.3 1.7 %collective-permute-start.17 = (bf16[8,32,1024]{2,1,0:T(8,128)(2,1)}, bf16[8,32,1024]{2,1,0:T(8,128)(2,1)S(1)}, u32[]{:S(2)}, u32[]{:S(2)}) collective-permute-start(bf16[8,32,1024]{2,1,0:T(8,128)(2,1)} %get-tuple-element.75), channel_id=1, source_target_pairs={{0,12},{4,8},{8,4},{12,0},{1,13},{5,9},{9,5},{13,1},{2,14},{6,10},... | collective-permute-start | bytes 1572872 | tf_op jit(solution)/shard_map/ppermute | solution.py:28
  106.0 0.0 collective-permute-start.16
  106.1 1.5 %collective-permute-start.15 = (bf16[8,16,1024]{2,1,0:T(8,128)(2,1)}, bf16[8,16,1024]{2,1,0:T(8,128)(2,1)S(1)}, u32[]{:S(2)}, u32[]{:S(2)}) collective-permute-start(bf16[8,16,1024]{2,1,0:T(8,128)(2,1)} %get-tuple-element.72), channel_id=1, source_target_pairs={{0,12},{4,8},{8,4},{12,0},{1,13},{5,9},{9,5},{13,1},{2,14},{6,10},... | collective-permute-start | bytes 786440 | tf_op jit(solution)/shard_map/ppermute | solution.py:28
  107.6 1.3 collective-permute-start.14
  108.9 0.1 pad_add_fusion.row_ref
  109.0 0.1 pad_add_fusion.1.row_ref
  109.1 1.2 copy-done.3
  110.3 7.1 %adamw.6 = (f32[8,256,1024]{2,1,0:T(8,128)}, f32[8,256,1024]{2,1,0:T(8,128)}, f32[8,256,1024]{2,1,0:T(8,128)}, f32[8,256,1024]{2,1,0:T(8,128)}, f32[8,256,1024]{2,1,0:T(8,128)}) custom-call(s32[1]{0:T(128)} %bitcast.8.row_ref, f32[8,256,1024]{2,1,0:T(8,128)} %params_ref.11, f32[8,256,1024]{2,1,0:T(8,128)} %first_ref.11, f32[8,256,1024]{2,1,0:T(8,128)} %second_ref.11, ...), custom_call_target="tpu_custom_call" | custom-call | flops 1024 | bytes 1048576 | tf_op jit(solution)/shard_map/adamw/pallas_call | solution.py:326
  117.4 7.7 %adamw.7 = (f32[8,256,1024]{2,1,0:T(8,128)}, f32[8,256,1024]{2,1,0:T(8,128)}, f32[8,256,1024]{2,1,0:T(8,128)}, f32[8,256,1024]{2,1,0:T(8,128)}, f32[8,256,1024]{2,1,0:T(8,128)}) custom-call(s32[2]{0:T(128)S(1)} %pad_add_fusion.1.row_ref, f32[8,256,1024]{2,1,0:T(8,128)} %params_ref.11, ...), custom_call_target="tpu_custom_call", output_to_operand_aliasing={{0}: (6, {}), {1}: (7, {}), {2}: (8, {}), {3}: (9, {}), {4}... | custom-call | flops 1024 | bytes 1048576 | tf_op jit(solution)/shard_map/adamw/pallas_call | solution.py:326
  125.1 7.7 %adamw.8 = (f32[8,256,1024]{2,1,0:T(8,128)}, f32[8,256,1024]{2,1,0:T(8,128)}, f32[8,256,1024]{2,1,0:T(8,128)}, f32[8,256,1024]{2,1,0:T(8,128)}, f32[8,256,1024]{2,1,0:T(8,128)}) custom-call(s32[2]{0:T(128)S(1)} %pad_add_fusion.row_ref, f32[8,256,1024]{2,1,0:T(8,128)} %params_ref.11, ...), custom_call_target="tpu_custom_call", output_to_operand_aliasing={{0}: (6, {}), {1}: (7, {}), {2}: (8, {}), {3}: (9, {}), {4}... | custom-call | flops 1024 | bytes 1048576 | tf_op jit(solution)/shard_map/adamw/pallas_call | solution.py:326
  132.9 4.4 %adamw.9 = (f32[8,256,1024]{2,1,0:T(8,128)}, f32[8,256,1024]{2,1,0:T(8,128)}, f32[8,256,1024]{2,1,0:T(8,128)}, f32[8,256,1024]{2,1,0:T(8,128)}, f32[8,256,1024]{2,1,0:T(8,128)}) custom-call(s32[1]{0:T(128)} %bitcast.3.row_ref, f32[8,256,1024]{2,1,0:T(8,128)} %params_ref.11, ...), custom_call_target="tpu_custom_call", output_to_operand_aliasing={{0}: (5, {}), {1}: (6, {}), {2}: (7, {}), {3}: (8, {}), {4}... | custom-call | flops 1024 | bytes 1048576 | tf_op jit(solution)/shard_map/adamw/pallas_call | solution.py:326
  137.2 2.8 %adamw.10 = (f32[8,256,1024]{2,1,0:T(8,128)}, f32[8,256,1024]{2,1,0:T(8,128)}, f32[8,256,1024]{2,1,0:T(8,128)}, f32[8,256,1024]{2,1,0:T(8,128)}, f32[8,256,1024]{2,1,0:T(8,128)}) custom-call(s32[1]{0:T(128)} %bitcast.2.row_ref, f32[8,256,1024]{2,1,0:T(8,128)} %params_ref.11, ...), custom_call_target="tpu_custom_call", output_to_operand_aliasing={{0}: (5, {}), {1}: (6, {}), {2}: (7, {}), {3}: (8, {}), {4}... | custom-call | flops 1024 | bytes 1048576 | tf_op jit(solution)/shard_map/adamw/pallas_call | solution.py:326
  140.0 0.9 collective-permute-done.14.refs_0_
  140.9 2.7 %adamw.11 = (f32[8,256,1024]{2,1,0:T(8,128)}, f32[8,256,1024]{2,1,0:T(8,128)}, f32[8,256,1024]{2,1,0:T(8,128)}, f32[8,256,1024]{2,1,0:T(8,128)}, f32[8,256,1024]{2,1,0:T(8,128)}) custom-call(s32[1]{0:T(128)} %bitcast.row_ref, f32[8,256,1024]{2,1,0:T(8,128)} %params_ref.11, ...), custom_call_target="tpu_custom_call", output_to_operand_aliasing={{0}: (5, {}), {1}: (6, {}), {2}: (7, {}), {3}: (8, {}), {4}... | custom-call | flops 1024 | bytes 1048576 | tf_op jit(solution)/shard_map/adamw/pallas_call | solution.py:326
  (23 shorter events, 0.1 us)
Async XLA Ops:
  1.7 9.3 %collective-permute-start = (bf16[8,16,1024]{2,1,0:T(8,128)(2,1)S(1)}, bf16[8,16,1024]{2,1,0:T(8,128)(2,1)S(1)}, u32[]{:S(2)}, u32[]{:S(2)}) collective-permute-start(bf16[8,16,1024]{2,1,0:T(8,128)(2,1)S(1)} %dynamic-slice_convert_fusion.1), channel_id=1, source_target_pairs={{0,12},{4,8},{8,4},{12,0},{1,13},{5,9},{9,5},{13,1},{2,14},{6,10},... | collective-permute-start | bytes 786440 | tf_op jit(solution)/shard_map/ppermute | solution.py:28
  7.2 0.9 copy-start.4
  8.1 42.5 %collective-permute-start.2 = (bf16[8,64,1024]{2,1,0:T(8,128)(2,1)}, bf16[8,64,1024]{2,1,0:T(8,128)(2,1)S(1)}, u32[]{:S(2)}, u32[]{:S(2)}) collective-permute-start(bf16[8,64,1024]{2,1,0:T(8,128)(2,1)} %get-tuple-element.59), channel_id=1, source_target_pairs={{0,8},{4,12},{8,0},{12,4},{1,9},{5,13},{9,1},{13,5},{2,10},{6,14},... | collective-permute-start | bytes 3145736 | tf_op jit(solution)/shard_map/ppermute | solution.py:28
  12.8 37.9 %collective-permute-start.1 = (bf16[8,64,1024]{2,1,0:T(8,128)(2,1)S(1)}, bf16[8,64,1024]{2,1,0:T(8,128)(2,1)S(1)}, u32[]{:S(2)}, u32[]{:S(2)}) collective-permute-start(bf16[8,64,1024]{2,1,0:T(8,128)(2,1)S(1)} %dynamic-slice_convert_fusion), channel_id=1, source_target_pairs={{0,4},{4,0},{8,12},{12,8},{1,5},{5,1},{9,13},{13,9},{2,6},{6,2},{1... | collective-permute-start | bytes 3145736 | tf_op jit(solution)/shard_map/ppermute | solution.py:28
  12.9 37.7 %collective-permute-start.3 = (bf16[8,48,1024]{2,1,0:T(8,128)(2,1)}, bf16[8,48,1024]{2,1,0:T(8,128)(2,1)S(1)}, u32[]{:S(2)}, u32[]{:S(2)}) collective-permute-start(bf16[8,48,1024]{2,1,0:T(8,128)(2,1)} %copy-done.4), channel_id=1, source_target_pairs={{0,12},{4,8},{8,4},{12,0},{1,13},{5,9},{9,5},{13,1},{2,14},{6,10},... | collective-permute-start | bytes 2359304 | tf_op jit(solution)/shard_map/ppermute | solution.py:28
  15.3 70.0 %collective-permute-start.10 = (bf16[8,64,1024]{2,1,0:T(8,128)(2,1)}, bf16[8,64,1024]{2,1,0:T(8,128)(2,1)}, u32[]{:S(2)}, u32[]{:S(2)}) collective-permute-start(bf16[8,64,1024]{2,1,0:T(8,128)(2,1)} %constant_dynamic-slice_fusion.3), channel_id=1, source_target_pairs={{0,8},{4,12},{8,0},{12,4},{1,9},{5,13},{9,1},{13,5},{2,10},{6,14},... | collective-permute-start | bytes 3145736 | tf_op jit(solution)/shard_map/ppermute | solution.py:28
  17.6 67.7 %collective-permute-start.9 = (bf16[8,64,1024]{2,1,0:T(8,128)(2,1)}, bf16[8,64,1024]{2,1,0:T(8,128)(2,1)}, u32[]{:S(2)}, u32[]{:S(2)}) collective-permute-start(bf16[8,64,1024]{2,1,0:T(8,128)(2,1)} %constant_dynamic-slice_fusion.2), channel_id=1, source_target_pairs={{0,4},{4,0},{8,12},{12,8},{1,5},{5,1},{9,13},{13,9},{2,6},{6,2},{1... | collective-permute-start | bytes 3145736 | tf_op jit(solution)/shard_map/ppermute | solution.py:28
  50.6 34.7 %copy-start = (bf16[8,64,1024]{2,1,0:T(8,128)(2,1)}, bf16[8,64,1024]{2,1,0:T(8,128)(2,1)S(1)}, u32[]{:S(2)}) copy-start(bf16[8,64,1024]{2,1,0:T(8,128)(2,1)S(1)} %collective-permute-done.2.refs_2_) | copy-start | bytes 3145732
  57.0 5.9 %collective-permute-start.6 = (f32[32,32]{1,0:T(8,128)S(1)}, f32[32,32]{1,0:T(8,128)S(1)}, u32[]{:S(2)}, u32[]{:S(2)}) collective-permute-start(f32[32,32]{1,0:T(8,128)S(1)} %gram.1), channel_id=1, source_target_pairs={{0,3},{1,2},{2,1},{3,0},{4,7},{5,6},{6,5},{7,4},{8,11},{9,10},{10,... | collective-permute-start | bytes 12296 | tf_op jit(solution)/shard_map/ppermute | solution.py:28
  61.2 4.6 %collective-permute-start.5 = (f32[32,32]{1,0:T(8,128)S(1)}, f32[32,32]{1,0:T(8,128)S(1)}, u32[]{:S(2)}, u32[]{:S(2)}) collective-permute-start(f32[32,32]{1,0:T(8,128)S(1)} %gram.1), channel_id=1, source_target_pairs={{0,2},{1,3},{2,0},{3,1},{4,6},{5,7},{6,4},{7,5},{8,10},{9,11},{10,... | collective-permute-start | bytes 12296 | tf_op jit(solution)/shard_map/ppermute | solution.py:28
  61.2 4.6 %collective-permute-start.4 = (f32[32,32]{1,0:T(8,128)S(1)}, f32[32,32]{1,0:T(8,128)S(1)}, u32[]{:S(2)}, u32[]{:S(2)}) collective-permute-start(f32[32,32]{1,0:T(8,128)S(1)} %gram.1), channel_id=1, source_target_pairs={{0,1},{1,0},{2,3},{3,2},{4,5},{5,4},{6,7},{7,6},{8,9},{9,8},{10,11... | collective-permute-start | bytes 12296 | tf_op jit(solution)/shard_map/ppermute | solution.py:28
  65.9 1.2 collective-permute-start.7
  69.0 16.3 %collective-permute-start.12 = (bf16[8,32,1024]{2,1,0:T(8,128)(2,1)}, bf16[8,32,1024]{2,1,0:T(8,128)(2,1)}, u32[]{:S(2)}, u32[]{:S(2)}) collective-permute-start(bf16[8,32,1024]{2,1,0:T(8,128)(2,1)} %constant_dynamic-slice_fusion.1), channel_id=1, source_target_pairs={{0,12},{4,8},{8,4},{12,0},{1,13},{5,9},{9,5},{13,1},{2,14},{6,10},... | collective-permute-start | bytes 1572872 | tf_op jit(solution)/shard_map/ppermute | solution.py:28
  70.3 15.0 %collective-permute-start.8 = (f32[32,32]{1,0:T(8,128)S(1)}, f32[32,32]{1,0:T(8,128)S(1)}, u32[]{:S(2)}, u32[]{:S(2)}) collective-permute-start(f32[32,32]{1,0:T(8,128)S(1)} %add.59), channel_id=1, source_target_pairs={{0,8},{4,12},{8,0},{12,4},{1,9},{5,13},{9,1},{13,5},{2,10},{6,14},... | collective-permute-start | bytes 12296 | tf_op jit(solution)/shard_map/ppermute | solution.py:28
  71.9 24.1 %collective-permute-start.11 = (bf16[8,32,1024]{2,1,0:T(8,128)(2,1)S(1)}, bf16[8,32,1024]{2,1,0:T(8,128)(2,1)S(1)}, u32[]{:S(2)}, u32[]{:S(2)}) collective-permute-start(bf16[8,32,1024]{2,1,0:T(8,128)(2,1)S(1)} %constant_dynamic-slice_fusion), channel_id=1, source_target_pairs={{0,12},{4,8},{8,4},{12,0},{1,13},{5,9},{9,5},{13,1},{2,14},{6,10},... | collective-permute-start | bytes 1572872 | tf_op jit(solution)/shard_map/ppermute | solution.py:28
  91.1 15.0 %collective-permute-start.13 = (bf16[8,32,1024]{2,1,0:T(8,128)(2,1)S(1)}, bf16[8,32,1024]{2,1,0:T(8,128)(2,1)S(1)}, u32[]{:S(2)}, u32[]{:S(2)}) collective-permute-start(bf16[8,32,1024]{2,1,0:T(8,128)(2,1)S(1)} %get-tuple-element.69), channel_id=1, source_target_pairs={{0,4},{4,0},{8,12},{12,8},{1,5},{5,1},{9,13},{13,9},{2,6},{6,2},{1... | collective-permute-start | bytes 1572872 | tf_op jit(solution)/shard_map/ppermute | solution.py:28
  91.1 16.5 %collective-permute-start.19 = (bf16[8,32,1024]{2,1,0:T(8,128)(2,1)S(1)}, bf16[8,32,1024]{2,1,0:T(8,128)(2,1)S(1)}, u32[]{:S(2)}, u32[]{:S(2)}) collective-permute-start(bf16[8,32,1024]{2,1,0:T(8,128)(2,1)S(1)} %get-tuple-element.77), channel_id=1, source_target_pairs={{0,8},{4,12},{8,0},{12,4},{1,9},{5,13},{9,1},{13,5},{2,10},{6,14},... | collective-permute-start | bytes 1572872 | tf_op jit(solution)/shard_map/ppermute | solution.py:28
  95.9 1.2 copy-start.1
  102.9 1.0 copy-start.2
  103.9 21.2 %collective-permute-start.18 = (bf16[8,32,1024]{2,1,0:T(8,128)(2,1)}, bf16[8,32,1024]{2,1,0:T(8,128)(2,1)S(1)}, u32[]{:S(2)}, u32[]{:S(2)}) collective-permute-start(bf16[8,32,1024]{2,1,0:T(8,128)(2,1)} %get-tuple-element.76), channel_id=1, source_target_pairs={{0,4},{4,0},{8,12},{12,8},{1,5},{5,1},{9,13},{13,9},{2,6},{6,2},{1... | collective-permute-start | bytes 1572872 | tf_op jit(solution)/shard_map/ppermute | solution.py:28
  104.3 20.8 %collective-permute-start.17 = (bf16[8,32,1024]{2,1,0:T(8,128)(2,1)}, bf16[8,32,1024]{2,1,0:T(8,128)(2,1)S(1)}, u32[]{:S(2)}, u32[]{:S(2)}) collective-permute-start(bf16[8,32,1024]{2,1,0:T(8,128)(2,1)} %get-tuple-element.75), channel_id=1, source_target_pairs={{0,12},{4,8},{8,4},{12,0},{1,13},{5,9},{9,5},{13,1},{2,14},{6,10},... | collective-permute-start | bytes 1572872 | tf_op jit(solution)/shard_map/ppermute | solution.py:28
  106.0 26.8 %collective-permute-start.16 = (bf16[8,32,1024]{2,1,0:T(8,128)(2,1)}, bf16[8,32,1024]{2,1,0:T(8,128)(2,1)S(1)}, u32[]{:S(2)}, u32[]{:S(2)}) collective-permute-start(bf16[8,32,1024]{2,1,0:T(8,128)(2,1)} %get-tuple-element.74), channel_id=1, source_target_pairs={{0,8},{4,12},{8,0},{12,4},{1,9},{5,13},{9,1},{13,5},{2,10},{6,14},... | collective-permute-start | bytes 1572872 | tf_op jit(solution)/shard_map/ppermute | solution.py:28
  106.1 31.1 %collective-permute-start.15 = (bf16[8,16,1024]{2,1,0:T(8,128)(2,1)}, bf16[8,16,1024]{2,1,0:T(8,128)(2,1)S(1)}, u32[]{:S(2)}, u32[]{:S(2)}) collective-permute-start(bf16[8,16,1024]{2,1,0:T(8,128)(2,1)} %get-tuple-element.72), channel_id=1, source_target_pairs={{0,12},{4,8},{8,4},{12,0},{1,13},{5,9},{9,5},{13,1},{2,14},{6,10},... | collective-permute-start | bytes 786440 | tf_op jit(solution)/shard_map/ppermute | solution.py:28
  107.6 33.4 %collective-permute-start.14 = (bf16[8,16,1024]{2,1,0:T(8,128)(2,1)}, bf16[8,16,1024]{2,1,0:T(8,128)(2,1)S(1)}, u32[]{:S(2)}, u32[]{:S(2)}) collective-permute-start(bf16[8,16,1024]{2,1,0:T(8,128)(2,1)} %get-tuple-element.70), channel_id=1, source_target_pairs={{0,12},{4,8},{8,4},{12,0},{1,13},{5,9},{9,5},{13,1},{2,14},{6,10},... | collective-permute-start | bytes 786440 | tf_op jit(solution)/shard_map/ppermute | solution.py:28
  109.0 1.2 copy-start.3
